TPU v7x, 256 devices: a whole 4x4x8 slice. The times are simulated.
256 devices in a mesh: ctx: 16 (over x, y_hi, core), chan: 16 (over z, y_lo).
Axes of the slice: x: 4, y: 4 (y_hi: 2, y_lo: 2; y = y_hi * 2 + y_lo), z: 8, core: 2. Of those that a mesh axis runs over, the one named last changes fastest.
Arguments:
- inputs: bfloat16 [256, 4096], P('ctx', 'chan'), may hold values from -6 to 6
- gain: float32 [4096], replicated, may hold values from 0.25 to 1.75
- w_in: bfloat16 [4096, 3, 4096], P(None, None, 'chan'), may hold values from -0.09375 to 0.09375
- w_out: bfloat16 [4096, 4096], P('chan'), may hold values from -0.125 to 0.125
- history: bfloat16 [4096, 2, 4096], P('ctx', None, 'chan'), may hold values from -6 to 6
- filt_far: bfloat16 [4096, 2, 4096], P('ctx', None, 'chan'), may hold values from -0.09375 to 0.09375
- filt_near: bfloat16 [256, 2, 4096], P(None, None, 'chan'), may hold values from -0.09375 to 0.09375
Outputs:
- mixed: bfloat16 [256, 4096], P('ctx', 'chan')
- gated: bfloat16 [256, 4096], P('ctx', 'chan')
All inputs are finite; a program needn't handle non-finite values.
Results may differ from a plain program's by a relative error of at most 0.0066.
Values may be sent and summed in bfloat16 or wider, within the bound.
No kernel may reach another device: no remote copies, remote signals or barrier semaphores. Data moves between devices by JAX's collectives and lax.ppermute only.
A program may use at most 64 MiB of HBM per device.

v0:
```python
import jax
import jax.numpy as jnp
from jax import lax
from jax.sharding import PartitionSpec as P


def in_order(tiles, dim):
    tiles = jnp.moveaxis(tiles, 0, dim)
    shape = tiles.shape
    return tiles.reshape(*shape[:dim], shape[dim] * shape[dim + 1], *shape[dim + 2 :])


def copy_for_each(array, axis):
    copies = jnp.broadcast_to(array, (lax.axis_size(axis), *array.shape))
    return lax.all_to_all(copies, axis, split_axis=0, concat_axis=0, tiled=True)


def gathered_copies(array, axis, dim):
    return in_order(copy_for_each(array, axis), dim)


def passed_along(block, axis, distance):
    devices = range(lax.axis_size(axis))
    route = [(i - distance, i) for i in devices if i - distance in devices]
    return lax.ppermute(block, axis, route)


def split_up(array, dim, size):
    shape = array.shape
    tiles = array.reshape(*shape[:dim], size, shape[dim] // size, *shape[dim + 1 :])
    return jnp.moveaxis(tiles, dim, 0)


def sent_and_summed(array, axis, dim):
    tiles = split_up(array, dim, lax.axis_size(axis))
    arrived = lax.all_to_all(tiles, axis, split_axis=0, concat_axis=0, tiled=True)
    return arrived.sum(axis=0)


def correlate(signal, kernel):
    result = lax.conv_general_dilated(
        signal[None],
        kernel[:, None, :],
        (1,),
        "VALID",
        dimension_numbers=("NWC", "WIO", "NWC"),
        feature_group_count=signal.shape[1],
        preferred_element_type=jnp.float32,
    )
    return result[0]


def per_device(inputs, gain, w_in, w_out, history, filt_far, filt_near):
    chan_width = inputs.shape[1]
    tok_rows = inputs.shape[0]
    fresh_count = filt_near.shape[0]
    past_len = history.shape[0]
    ctx_index = lax.axis_index("ctx")
    ctx_count = lax.axis_size("ctx")
    gathered = gathered_copies(inputs, "chan", 1)
    features = gathered.astype(jnp.float32)
    mean_sq = jnp.mean(features * features, axis=-1, keepdims=True)
    normed = (features * lax.rsqrt(mean_sq + 1e-06) * gain).astype(jnp.bfloat16)
    projected = jnp.dot(
        normed, w_in.reshape(w_in.shape[0], 3 * chan_width), preferred_element_type=jnp.float32
    )
    projected = projected.reshape(tok_rows, 3, chan_width)
    values = projected[:, 0].astype(jnp.bfloat16)
    gate_one = projected[:, 1].astype(jnp.bfloat16)
    gate_two = projected[:, 2].astype(jnp.bfloat16)
    border = passed_along(filt_far, "ctx", -1)
    border = jnp.where(ctx_index == ctx_count - 1, filt_near, border)
    window = jnp.concatenate([filt_far, border], 0).reshape(past_len + fresh_count, 2 * chan_width)
    past_part = correlate(window, history.reshape(past_len, 2 * chan_width))[:fresh_count]
    near_flat = filt_near.reshape(fresh_count, 2 * chan_width)
    padded_near = jnp.concatenate([near_flat, jnp.zeros_like(near_flat)], 0)
    own_window = lax.dynamic_slice_in_dim(
        padded_near, ctx_index * tok_rows, fresh_count + tok_rows - 1, 0
    )
    first_part = past_part[:, :chan_width] + correlate(own_window[:, :chan_width], values)
    stacked = sent_and_summed(
        jnp.concatenate([first_part, past_part[:, chan_width:]], 1)[::-1], "ctx", 0
    )
    gated = (gate_one.astype(jnp.float32) * stacked[:, :chan_width]).astype(jnp.bfloat16)
    all_gated = gathered_copies(gated, "ctx", 0)
    offset = fresh_count - (ctx_index + 1) * tok_rows
    later_window = lax.dynamic_slice_in_dim(
        padded_near[:, chan_width:], offset, tok_rows + fresh_count - 1, 0
    )
    inside = correlate(later_window, all_gated)
    second_sum = stacked[:, chan_width:] + inside[::-1]
    mixed_in = (gate_two.astype(jnp.float32) * second_sum).astype(jnp.bfloat16)
    partial_out = jnp.dot(mixed_in, w_out, preferred_element_type=jnp.float32)
    mixed = sent_and_summed(partial_out, "chan", 1).astype(jnp.bfloat16)
    return (mixed, gated)


def solution(mesh):
    placed = (
        P("ctx", "chan"),
        P(),
        P(None, None, "chan"),
        P("chan", None),
        P("ctx", None, "chan"),
        P("ctx", None, "chan"),
        P(None, None, "chan"),
    )
    return jax.shard_map(
        per_device,
        mesh=mesh,
        in_specs=placed,
        out_specs=(P("ctx", "chan"), P("ctx", "chan")),
        check_vma=False,
    )
```

profile of v0, /device:TPU:1, one launch (start us, length us, event | category | flops | bytes accessed | tf_op | source)
XLA Modules:
  0.0 104.5 jit_solution(12224894376755670321)
XLA Ops:
  0.6 0.0 copy-start
  0.6 1.5 %broadcast_in_dim.16 = bf16[16,16,256]{2,1,0:T(8,128)(2,1)} broadcast(bf16[16,256]{1,0:T(8,128)(2,1)} %param.7), dimensions={1,2} | broadcast | bytes 139264 | tf_op jit(solution)/shard_map/broadcast_in_dim | solution.py:14
  2.1 10.1 %all-to-all-start = ((bf16[16,16,256]{2,1,0:T(8,128)(2,1)}), bf16[16,16,256]{2,1,0:T(8,128)(2,1)S(1)}, u32[]{:S(2)}, u32[]{:S(2)}) async-start(bf16[16,16,256]{2,1,0:T(8,128)(2,1)} %broadcast_in_dim.16), calls=%async_computation | async-start | bytes 262144 | tf_op jit(solution)/shard_map/all_to_all | solution.py:15
  12.3 1.1 %copy.41 = bf16[256,2,256]{0,2,1:T(8,128)(2,1)S(1)} copy(bf16[256,2,256]{2,1,0:T(2,128)(2,1)} %param.12) | data formatting | bytes 524288 | tf_op args[5]
  13.4 2.9 %collective-permute-start = (bf16[256,2,256]{0,2,1:T(8,128)(2,1)S(1)}, bf16[256,2,256]{0,2,1:T(8,128)(2,1)}, u32[]{:S(2)}, u32[]{:S(2)}) collective-permute-start(bf16[256,2,256]{0,2,1:T(8,128)(2,1)S(1)} %copy.41), channel_id=1, source_target_pairs={{16,0},{32,16},{48,32},{64,48},{80,64},{96,80},{112,96},{128,112},... | collective-permute-start | bytes 786440 | tf_op jit(solution)/shard_map/ppermute | solution.py:25
  16.3 1.1 %copy.40 = bf16[256,2,256]{0,2,1:T(8,128)(2,1)S(1)} copy(bf16[256,2,256]{2,1,0:T(2,128)(2,1)} %param.13) | data formatting | bytes 524288 | tf_op args[6]
  17.4 1.0 copy.54
  18.4 0.1 fusion.19
  18.6 0.6 slice.51
  19.2 0.7 mul.42
  20.0 0.0 copy-start.1
  20.0 8.8 %copy.38 = bf16[4096,3,256]{0,2,1:T(8,128)(2,1)} copy(bf16[4096,3,256]{2,0,1:T(8,128)(2,1)} %param.9) | data formatting | bytes 12582912 | tf_op args[2]
  28.8 0.0 copy-start.3
  28.8 0.0 copy-done.1
  28.8 0.9 broadcast_in_dim_reshape.12
  29.7 0.0 all-to-all-done
  29.7 0.1 fusion.8
  29.9 0.1 fusion.20
  30.0 0.1 reshape.62
  30.1 4.5 %fusion.2 = bf16[16,3,256]{2,0,1:T(8,128)(2,1)S(1)} fusion(bf16[16,4096,1]{1,0,2:T(8,128)(2,1)S(1)} %reshape.62, bf16[4096,3,256]{0,2,1:T(8,128)(2,1)} %copy.38), kind=kOutput, calls=%fused_computation.3 | convolution fusion | flops 100675584 | bytes 6447104 | tf_op jit(solution)/shard_map/dot_general | solution.py:64
  34.6 0.0 copy-done.3
  34.6 1.2 %convolution_select_fusion = f32[8,34,256]{2,0,1:T(8,128)S(1)} fusion(bf16[1,7,15,256]{3,1,2,0:T(8,128)(2,1)} %slice.51, bf16[1,8,34,256]{3,1,2,0:T(8,128)(2,1)S(1)} %copy.45, pred[8,34]{0,1:T(8,128)(4,1)S(1)} %copy-done.3, bf16[16,1,256]{2,0,1:T(8,128)(2,1)S(1)} %slice.52), kind=kOutput, calls=%fused_computation.2 | convolution fusion | flops 2899968 | bytes 480016 | tf_op jit(solution)/shard_map/conv_general_dilated | solution.py:41
  35.8 0.1 copy.47
  36.0 0.0 collective-permute-done
  36.0 1.0 broadcast_select_fusion
  37.0 2.0 %copy.42 = bf16[1,512,512]{2,0,1:T(2,128)(2,1)} copy(bf16[1,512,512]{1,2,0:T(8,128)(2,1)S(1)} %bitcast.57) | data formatting | bytes 1048576 | tf_op jit(solution)/shard_map/broadcast_in_dim;reshape | solution.py:42
  39.0 14.6 %fusion.31 = f32[1,256,512]{2,0,1:T(1,128)S(1)} fusion(bf16[1,512,512]{2,0,1:T(2,128)(2,1)} %copy.42, bf16[256,1,512]{2,1,0:T(2,128)(2,1)} %broadcast_in_dim_reshape.12), kind=kOutput, calls=%fused_computation.46 | convolution fusion | flops 67108864 | bytes 1310720 | tf_op jit(solution)/shard_map/slice | solution.py:74
  53.6 0.1 fusion.11
  53.7 0.1 pad_maximum_fusion.1
  53.8 0.3 rev.6
  54.1 17.8 %all_to_all.20 = f32[16,16,512]{2,1,0:T(8,128)S(1)} all-to-all(f32[16,16,512]{2,1,0:T(8,128)S(1)} %bitcast.59), channel_id=1, replica_groups=mesh['ctx'=16,'chan'=16] {'ctx'}, dimensions={0} | all-to-all | bytes 1048576 | tf_op jit(solution)/shard_map/all_to_all | solution.py:36
  71.9 0.0 copy-start.2
  71.9 0.6 broadcast_in_dim.19
  72.5 4.5 %all-to-all-start.2 = ((bf16[16,16,256]{2,1,0:T(8,128)(2,1)}), bf16[16,16,256]{2,1,0:T(8,128)(2,1)S(1)}, u32[]{:S(2)}, u32[]{:S(2)}) async-start(bf16[16,16,256]{2,1,0:T(8,128)(2,1)} %broadcast_in_dim.19), calls=%async_computation.2 | async-start | bytes 262144 | tf_op jit(solution)/shard_map/all_to_all | solution.py:15
  77.1 7.6 %all-to-all-done.2 = bf16[16,16,256]{2,1,0:T(8,128)(2,1)S(1)} async-done(((bf16[16,16,256]{2,1,0:T(8,128)(2,1)}), bf16[16,16,256]{2,1,0:T(8,128)(2,1)S(1)}, u32[]{:S(2)}, u32[]{:S(2)}) %all-to-all-start.2) | async-done | bytes 131104 | tf_op jit(solution)/shard_map/all_to_all | solution.py:15
  84.8 0.7 fusion.6
  85.5 0.1 rev.7
  85.6 0.0 copy-done
  85.6 0.4 fusion.26
  86.0 17.9 %all_to_all.21 = f32[16,16,256]{2,1,0:T(8,128)S(1)} all-to-all(f32[16,16,256]{2,1,0:T(8,128)S(1)} %bitcast.62), channel_id=1, replica_groups=mesh['ctx'=16,'chan'=16] {'chan'}, dimensions={0} | all-to-all | bytes 524288 | tf_op jit(solution)/shard_map/all_to_all | solution.py:36
  103.9 0.6 reduce_sum.29
  104.5 0.0 copy-done.2
  (15 shorter events, 0.4 us)
Async XLA Ops:
  0.6 85.0 %copy-start = (bf16[256,4096]{1,0:T(8,128)(2,1)S(1)}, bf16[256,4096]{1,0:T(8,128)(2,1)}, u32[]{:S(2)}) copy-start(bf16[256,4096]{1,0:T(8,128)(2,1)} %param.10) | copy-start | bytes 6291460
  2.1 27.6 %all-to-all-start = ((bf16[16,16,256]{2,1,0:T(8,128)(2,1)}), bf16[16,16,256]{2,1,0:T(8,128)(2,1)S(1)}, u32[]{:S(2)}, u32[]{:S(2)}) async-start(bf16[16,16,256]{2,1,0:T(8,128)(2,1)} %broadcast_in_dim.16), calls=%async_computation | async-start | bytes 262144 | tf_op jit(solution)/shard_map/all_to_all | solution.py:15
  13.4 22.6 %collective-permute-start = (bf16[256,2,256]{0,2,1:T(8,128)(2,1)S(1)}, bf16[256,2,256]{0,2,1:T(8,128)(2,1)}, u32[]{:S(2)}, u32[]{:S(2)}) collective-permute-start(bf16[256,2,256]{0,2,1:T(8,128)(2,1)S(1)} %copy.41), channel_id=1, source_target_pairs={{16,0},{32,16},{48,32},{64,48},{80,64},{96,80},{112,96},{128,112},... | collective-permute-start | bytes 786440 | tf_op jit(solution)/shard_map/ppermute | solution.py:25
  20.0 8.8 %copy-start.1 = (bf16[256,2,256]{2,1,0:T(2,128)(2,1)S(1)}, bf16[256,2,256]{2,1,0:T(2,128)(2,1)}, u32[]{:S(2)}) copy-start(bf16[256,2,256]{2,1,0:T(2,128)(2,1)} %param.11) | copy-start | bytes 786436
  28.8 5.8 %copy-start.3 = (pred[8,34]{0,1:T(8,128)(4,1)S(1)}, pred[8,34]{0,1:T(8,128)(4,1)}, u32[]{:S(2)}) copy-start(pred[8,34]{0,1:T(8,128)(4,1)} %constant.40) | copy-start | bytes 820
  71.9 32.6 %copy-start.2 = (bf16[16,256]{1,0:T(8,128)(2,1)}, bf16[16,256]{1,0:T(8,128)(2,1)S(1)}, u32[]{:S(2)}) copy-start(bf16[16,256]{1,0:T(8,128)(2,1)S(1)} %fusion.22) | copy-start | bytes 24580
  72.5 12.2 %all-to-all-start.2 = ((bf16[16,16,256]{2,1,0:T(8,128)(2,1)}), bf16[16,16,256]{2,1,0:T(8,128)(2,1)S(1)}, u32[]{:S(2)}, u32[]{:S(2)}) async-start(bf16[16,16,256]{2,1,0:T(8,128)(2,1)} %broadcast_in_dim.19), calls=%async_computation.2 | async-start | bytes 262144 | tf_op jit(solution)/shard_map/all_to_all | solution.py:15
where the time goes:
time: 105 us; the launch traced here: 104 us
  blocking collectives  35.6 us (34%)
  matrix products  21.4 us (20%)
  local copies, waits for them, and re-layouts  19.4 us (18%)
  starting transfers between devices  17.5 us (17%)
  waiting for transfers between devices  7.64 us (7%)
  other arithmetic  2.05 us (2%)
    all_to_all x2, blocking collectives, sent_and_summed(): lax.all_to_all(tiles, axis, split_axis=0, concat_axis=0, tiled=True)  35.6 us
    all_to_all x2, starting transfers between devices, copy_for_each(): return lax.all_to_all(copies, axis, split_axis=0, concat_axis=0, tiled=True)  14.6 us
    slice x1, matrix products, per_device(): correlate(window, history.reshape(past_len, 2 * chan_width))[:fresh_count]  14.6 us
    unnamed x14, local copies, waits for them, and re-layouts  12.1 us
    all_to_all x2, waiting for transfers between devices, copy_for_each(): return lax.all_to_all(copies, axis, split_axis=0, concat_axis=0, tiled=True)  7.63 us
    dot_general x1, matrix products, per_device(): jnp.dot(normed, w_in.reshape(w_in.shape[0], 3 * chan_width), preferred_el...  4.51 us
    ppermute x1, starting transfers between devices, passed_along(): return lax.ppermute(block, axis, route)  2.86 us
    broadcast_in_dim x2, local copies, waits for them, and re-layouts, copy_for_each(): copies = jnp.broadcast_to(array, (lax.axis_size(axis), *array.shape))  2.15 us
  transfers between devices with their start and end apart: 3, of which 1 were waited for; matrix products, arithmetic and copies ran while one was open for 20% of the time, Pallas kernels for 0%

commit v1 on v0

v1 whole, which is shorter than its diff:
```python
import functools

import jax
import jax.numpy as jnp
import numpy as np
from jax import lax
from jax.experimental import pallas as pl
from jax.experimental.pallas import tpu as pltpu
from jax.sharding import PartitionSpec as P

BF16 = jnp.bfloat16
F32 = jnp.float32
VMEM = pl.BlockSpec(memory_space=pltpu.VMEM)
SMEM = pl.BlockSpec(memory_space=pltpu.SMEM)
ANY = pl.BlockSpec(memory_space=pl.ANY)
LIMIT = 24 << 20


def split_up(table):
    high = np.asarray(table, np.float32).astype(jnp.bfloat16)
    low = (table - high.astype(np.float64)).astype(np.float32).astype(jnp.bfloat16)
    return high, low


def dft_tables(length):
    order = np.concatenate([np.arange(0, length, 2), np.arange(1, length, 2)])
    theta = np.pi * (order + 0.5) / length
    angle = theta[:, None] * np.arange(length)[None, :]
    forward = np.concatenate([np.cos(angle), np.sin(angle)], 0)
    back = theta[None, :] * (length - 1 - np.arange(length))[:, None]
    inverse = np.concatenate([np.cos(back), -np.sin(back)], 1) / length
    return (*split_up(forward), *split_up(inverse))


def dot(a, b):
    return jnp.dot(a, b, preferred_element_type=F32)


def spectrum(high, low, rows):
    return dot(high[...], rows) + dot(low[...], rows)


def back_to_time(high, low, product):
    upper = product.astype(BF16)
    lower = (product - upper.astype(F32)).astype(BF16)
    return dot(high, upper) + dot(high, lower) + dot(low, upper)


def times_conjugate(window, signal):
    half = window.shape[0] // 2
    wc, ws = window[:half], window[half:]
    sc, ss = signal[:half], signal[half:]
    return jnp.concatenate([wc * sc + ws * ss, wc * ss - ws * sc], 0)


def past_kernel(which, last, own, border, near, history, fh, fl, ih, il, part):
    half = fh.shape[0] // 2
    quarter = half // 2
    after = jnp.where(last[0] > 0, near[:, which, :], border[:, which, :])
    first = spectrum(fh, fl, own[:, which, :])
    second = spectrum(fh, fl, after)
    bc, bs = second[:half], second[half:]
    window = first + jnp.concatenate([-bs[:quarter], bs[quarter:], bc[:quarter], -bc[quarter:]], 0)
    signal = spectrum(fh, fl, history[:, which, :])
    result = back_to_time(ih[...], il[...], times_conjugate(window, signal))
    part[...] = result.astype(BF16).reshape(part.shape)


def near_kernel(near, fh, fl, spectra):
    for which in range(2):
        spectra[which] = spectrum(fh, fl, near[:, which, :])


def project_kernel(gathered, gain, w_hbm, out, w, sems):
    pieces, rows, width = gathered.shape
    per = pieces // 4
    copies = []
    for q in range(4):
        span = pl.ds(q * per * width, per * width)
        copies.append(pltpu.make_async_copy(w_hbm.at[:, span, :], w.at[:, span, :], sems.at[q]))
        copies[-1].start()
    total = jnp.zeros((rows, width), F32)
    for s in range(pieces):
        x = gathered[s].astype(F32)
        total += x * x
    mean_sq = jnp.sum(total, axis=1, keepdims=True) / (pieces * width)
    scale = lax.rsqrt(mean_sq + 1e-06)
    sums = [jnp.zeros((rows, width), F32) for _ in range(3)]
    for s in range(pieces):
        if s % per == 0:
            copies[s // per].wait()
        g = jnp.concatenate([gain[2 * s : 2 * s + 1], gain[2 * s + 1 : 2 * s + 2]], 1)
        normed = (gathered[s].astype(F32) * scale * g).astype(BF16)
        for k in range(3):
            sums[k] += dot(normed, w[k, s * width : (s + 1) * width, :])
    for k in range(3):
        out[k] = sums[k].astype(BF16)


def payload_kernel(arrived, projected, part2, out):
    count = arrived.shape[0]
    past = jnp.sum(arrived[...].astype(F32), axis=0).astype(BF16)
    rows = jnp.concatenate([projected[0], projected[1], past], 0)
    for d in range(count):
        out[d, : rows.shape[0]] = rows
        out[d, rows.shape[0] :] = part2[d]


def mix_kernel(index, arrived, projected, spectra, fh, fl, ih, il, w_out, partial, gated_own, gated_all):
    count, packed, width = arrived.shape
    rows = packed // 4
    everything = count * rows
    values = arrived[:, :rows].reshape(everything, width)
    gate_one = arrived[:, rows : 2 * rows].reshape(everything, width).astype(F32)
    past_one = arrived[:, 2 * rows : 3 * rows].reshape(everything, width).astype(F32)
    first = back_to_time(ih[...], il[...], times_conjugate(spectra[0], spectrum(fh, fl, values)))
    gated = (gate_one * (past_one + first)).astype(BF16)
    gated_all[...] = gated
    own = pl.ds(pl.multiple_of(index[0] * rows, rows), rows)
    gated_own[...] = gated_all[own, :]
    second = back_to_time(ih[own, :], il[own, :], times_conjugate(spectra[1], spectrum(fh, fl, gated)))
    past_two = jnp.sum(arrived[:, 3 * rows :].astype(F32), axis=0)
    mixed_in = (projected[2].astype(F32) * (past_two + second)).astype(BF16)
    for d in range(partial.shape[0]):
        cols = dot(mixed_in, w_out[:, d * width : (d + 1) * width])
        partial[d] = cols.astype(BF16)


def total_kernel(arrived, out):
    out[...] = jnp.sum(arrived[...].astype(F32), axis=0).astype(BF16)


def call(kernel, out_shape, in_specs, flops, nbytes, scratch=(), name=None, limit=LIMIT):
    return pl.pallas_call(
        kernel,
        out_shape=out_shape,
        in_specs=in_specs,
        out_specs=jax.tree.map(lambda _: VMEM, out_shape),
        scratch_shapes=list(scratch),
        cost_estimate=pl.CostEstimate(flops=flops, bytes_accessed=nbytes, transcendentals=0),
        compiler_params=pltpu.CompilerParams(vmem_limit_bytes=limit),
        name=name,
    )


def exchanged(array, axis):
    return lax.all_to_all(array, axis, split_axis=0, concat_axis=0, tiled=True)


def per_device(inputs, gain, w_in, w_out, history, filt_far, filt_near):
    rows, width = inputs.shape
    fresh = filt_near.shape[0]
    ctx_count = lax.axis_size("ctx")
    chan_count = lax.axis_size("chan")
    ctx_index = lax.axis_index("ctx")
    tables = [jnp.asarray(t) for t in dft_tables(fresh)]
    index = ctx_index.reshape(1).astype(jnp.int32)
    last = (index == ctx_count - 1).astype(jnp.int32)

    border = lax.ppermute(filt_far, "ctx", [(i, i - 1) for i in range(1, ctx_count)])
    gathered = exchanged(jnp.broadcast_to(inputs, (chan_count, rows, width)), "chan")

    unit = fresh * fresh * 4 * width
    blocks = jax.ShapeDtypeStruct((ctx_count, rows, width), BF16)
    parts = [
        call(
            functools.partial(past_kernel, which),
            blocks,
            [SMEM] + [VMEM] * 8,
            unit * 9,
            4 << 20,
            name=f"past{which}",
        )(last, filt_far, border, filt_near, history, *tables)
        for which in range(2)
    ]
    spectra = call(
        near_kernel,
        jax.ShapeDtypeStruct((2, 2 * fresh, width), F32),
        [VMEM] * 3,
        unit * 4,
        2 << 20,
        name="near",
    )(filt_near, *tables[:2])
    arrived_one = exchanged(parts[0], "ctx")

    w_three = w_in.transpose(1, 0, 2)
    projected = call(
        project_kernel,
        jax.ShapeDtypeStruct((3, rows, width), BF16),
        [VMEM, VMEM, ANY],
        2 * rows * w_in.size,
        2 * w_in.size,
        scratch=[pltpu.VMEM(w_three.shape, BF16), pltpu.SemaphoreType.DMA((4,))],
        name="project",
    )(gathered, gain.reshape(-1, 128), w_three)

    packed = call(
        payload_kernel,
        jax.ShapeDtypeStruct((ctx_count, 4 * rows, width), BF16),
        [VMEM] * 3,
        1 << 20,
        1 << 20,
        name="payload",
    )(arrived_one, projected, parts[1])
    everyone = exchanged(packed, "ctx")

    partial, gated = call(
        mix_kernel,
        (
            jax.ShapeDtypeStruct((chan_count, rows, width), BF16),
            jax.ShapeDtypeStruct((rows, width), BF16),
        ),
        [SMEM] + [VMEM] * 8,
        unit * 8,
        4 << 20,
        scratch=[pltpu.VMEM((fresh, width), BF16)],
        name="mix",
    )(index, everyone, projected, spectra, *tables, w_out)
    mixed = call(
        total_kernel,
        jax.ShapeDtypeStruct((rows, width), BF16),
        [VMEM],
        1 << 16,
        1 << 17,
        name="total",
    )(exchanged(partial, "chan"))
    return (mixed, gated)


def solution(mesh):
    placed = (
        P("ctx", "chan"),
        P(),
        P(None, None, "chan"),
        P("chan", None),
        P("ctx", None, "chan"),
        P("ctx", None, "chan"),
        P(None, None, "chan"),
    )
    return jax.shard_map(
        per_device,
        mesh=mesh,
        in_specs=placed,
        out_specs=(P("ctx", "chan"), P("ctx", "chan")),
        check_vma=False,
    )
```

time: 105 us -> 82.5 us (0.79)
  matrix products: 21.4 us -> 0 us
  blocking collectives: 35.6 us -> 15.3 us
  Pallas kernels: 0 us -> 12.5 us
  starting transfers between devices: 17.5 us -> 27.8 us
  local copies, waits for them, and re-layouts: 19.4 us -> 16.3 us
  other arithmetic: 2.05 us -> 0 us
    all_to_all x2 -> x1, blocking collectives: 35.6 us -> 15.3 us  [exchanged(): return lax.all_to_all(array, axis, split_axis=0, concat_axis=0, tiled=True)]
    slice x1 -> x0, matrix products: 14.6 us -> none  [per_device(): correlate(window, history.reshape(past_len, 2 * chan_width))[:fresh_count]]
    pallas_call x0 -> x7, Pallas kernels: none -> 12.5 us  [the longest x2 4.82 us: per_device(): call(functools.partial(past_kernel, which), blocks, [SMEM] + [VMEM] * 8,...]
    all_to_all x2 -> x3, starting transfers between devices: 14.6 us -> 22.6 us  [exchanged(): return lax.all_to_all(array, axis, split_axis=0, concat_axis=0, tiled=True)]
    dot_general x2 -> x0, matrix products: 4.89 us -> none  [the longest x1 4.51 us: per_device(): jnp.dot(normed, w_in.reshape(w_in.shape[0], 3 * chan_width), preferred_el...]
    another operation x2 -> x0, local copies, waits for them, and re-layouts: 2.93 us -> none  [the longest x1 2.02 us: correlate(): signal[None]]
    unnamed x14 -> x48, local copies, waits for them, and re-layouts: 12.1 us -> 14.9 us
    ppermute x1, starting transfers between devices: 2.86 us -> 5.24 us  [per_device(): lax.ppermute(filt_far, 'ctx', [(i, i - 1) for i in range(1, ctx_count)])]
  transfers between devices with their start and end apart: 3 -> 4, of which waited for: 1 -> 1; matrix products, arithmetic and copies ran while one was open for 20% -> 2% of each run, Pallas kernels for 0% -> 10%
where the time goes in v1:
time: 82.5 us; the launch traced here: 81.3 us
  starting transfers between devices  27.8 us (34%)
  local copies, waits for them, and re-layouts  16.3 us (20%)
  blocking collectives  15.3 us (19%)
  Pallas kernels  12.5 us (15%)
  waiting for transfers between devices  8.51 us (10%)
    all_to_all x3, starting transfers between devices, exchanged(): return lax.all_to_all(array, axis, split_axis=0, concat_axis=0, tiled=True)  22.6 us
    all_to_all x1, blocking collectives, exchanged(): return lax.all_to_all(array, axis, split_axis=0, concat_axis=0, tiled=True)  15.3 us
    unnamed x48, local copies, waits for them, and re-layouts  14.9 us
    all_to_all x3, waiting for transfers between devices, exchanged(): return lax.all_to_all(array, axis, split_axis=0, concat_axis=0, tiled=True)  8.51 us
    ppermute x1, starting transfers between devices, per_device(): lax.ppermute(filt_far, 'ctx', [(i, i - 1) for i in range(1, ctx_count)])  5.24 us
    pallas_call x2, Pallas kernels, per_device(): call(functools.partial(past_kernel, which), blocks, [SMEM] + [VMEM] * 8,...  4.82 us
    pallas_call x1, Pallas kernels, per_device(): call(mix_kernel, (jax.ShapeDtypeStruct((chan_count, rows, width), BF16),...  3.09 us
    pallas_call x1, Pallas kernels, per_device(): call(project_kernel, jax.ShapeDtypeStruct((3, rows, width), BF16), [VMEM,...  2.16 us
  transfers between devices with their start and end apart: 4, of which 1 were waited for; matrix products, arithmetic and copies ran while one was open for 2% of the time, Pallas kernels for 10%

profile of v1, /device:TPU:1, one launch (start us, length us, event | category | flops | bytes accessed | tf_op | source)
XLA Modules:
  0.0 81.3 jit_solution(14114512419411140503)
XLA Ops:
  0.6 0.0 copy-start.3
  0.6 5.2 %collective-permute-start = (bf16[256,2,256]{2,1,0:T(2,128)(2,1)}, bf16[256,2,256]{2,1,0:T(2,128)(2,1)S(1)}, u32[]{:S(2)}, u32[]{:S(2)}) collective-permute-start(bf16[256,2,256]{2,1,0:T(2,128)(2,1)} %own.3), channel_id=1, source_target_pairs={{16,0},{32,16},{48,32},{64,48},{80,64},{96,80},{112,96},{128,112},... | collective-permute-start | bytes 786440 | tf_op jit(solution)/shard_map/ppermute | solution.py:160
  5.9 1.4 %broadcast_in_dim.3 = bf16[16,16,256]{2,1,0:T(8,128)(2,1)} broadcast(bf16[16,256]{1,0:T(8,128)(2,1)} %param.11), dimensions={1,2} | broadcast | bytes 139264 | tf_op jit(solution)/shard_map/broadcast_in_dim | solution.py:161
  7.3 7.6 %all-to-all-start.1 = ((bf16[16,16,256]{2,1,0:T(8,128)(2,1)}), bf16[16,16,256]{2,1,0:T(8,128)(2,1)S(1)}, u32[]{:S(2)}, u32[]{:S(2)}) async-start(bf16[16,16,256]{2,1,0:T(8,128)(2,1)} %broadcast_in_dim.3), calls=%async_computation.1 | async-start | bytes 262144 | tf_op jit(solution)/shard_map/all_to_all | solution.py:147
  14.9 0.0 collective-permute-done.border
  14.9 0.0 copy-start.2
  14.9 0.9 %copy-done.2 = bf16[512,256]{1,0:T(8,128)(2,1)S(1)} copy-done((bf16[512,256]{1,0:T(8,128)(2,1)S(1)}, bf16[512,256]{1,0:T(8,128)(2,1)}, u32[]{:S(2)}) %copy-start.2) | copy-done | bytes 262168
  15.8 0.0 copy-start.4
  15.8 0.9 %copy-done.4 = bf16[512,256]{1,0:T(8,128)(2,1)S(1)} copy-done((bf16[512,256]{1,0:T(8,128)(2,1)S(1)}, bf16[512,256]{1,0:T(8,128)(2,1)}, u32[]{:S(2)}) %copy-start.4) | copy-done | bytes 262168
  16.8 0.0 copy-start.8
  16.8 0.9 %copy-done.8 = bf16[256,2,256]{2,1,0:T(2,128)(2,1)S(1)} copy-done((bf16[256,2,256]{2,1,0:T(2,128)(2,1)S(1)}, bf16[256,2,256]{2,1,0:T(2,128)(2,1)}, u32[]{:S(2)}) %copy-start.8) | copy-done | bytes 262168
  17.7 0.0 copy-start.11
  17.7 0.9 %copy-done.11 = bf16[256,512]{1,0:T(8,128)(2,1)S(1)} copy-done((bf16[256,512]{1,0:T(8,128)(2,1)S(1)}, bf16[256,512]{1,0:T(8,128)(2,1)}, u32[]{:S(2)}) %copy-start.11) | copy-done | bytes 262168
  18.7 0.9 %copy-done.14 = bf16[256,512]{1,0:T(8,128)(2,1)S(1)} copy-done((bf16[256,512]{1,0:T(8,128)(2,1)S(1)}, bf16[256,512]{1,0:T(8,128)(2,1)}, u32[]{:S(2)}) %copy-start.14) | copy-done | bytes 262168
  19.6 0.9 %copy-done.18 = bf16[256,2,256]{2,1,0:T(2,128)(2,1)S(1)} copy-done((bf16[256,2,256]{2,1,0:T(2,128)(2,1)S(1)}, bf16[256,2,256]{2,1,0:T(2,128)(2,1)}, u32[]{:S(2)}) %copy-start.18) | copy-done | bytes 262168
  20.6 0.9 %copy-done.20 = bf16[256,2,256]{2,1,0:T(2,128)(2,1)S(1)} copy-done((bf16[256,2,256]{2,1,0:T(2,128)(2,1)S(1)}, bf16[256,2,256]{2,1,0:T(2,128)(2,1)}, u32[]{:S(2)}) %copy-start.20) | copy-done | bytes 262168
  21.5 2.7 %past0.1 = bf16[16,16,256]{2,1,0:T(8,128)(2,1)} custom-call(s32[1]{0:T(128)S(6)} %convert_element_type.3.last, bf16[256,2,256]{2,1,0:T(2,128)(2,1)S(1)} %copy-done.18, bf16[256,2,256]{2,1,0:T(2,128)(2,1)S(1)} %collective-permute-done.border, bf16[256,2,256]{2,1,0:T(2,128)(2,1)S(1)} %copy-done.8, bf16[256,2,256]{2,1,0:T(2,128)(2,1)S(1)} %copy-done.20, ...), custom_call_target="tpu_custom_call" | custom-call | flops 603979776 | bytes 4194304 | tf_op jit(solution)/shard_map/past0/pallas_call | solution.py:166
  24.3 0.0 all-to-all-done.1.gathered
  24.3 0.0 copy-done.22
  24.3 7.8 %all-to-all-start = ((bf16[16,16,256]{2,1,0:T(8,128)(2,1)}), bf16[16,16,256]{2,1,0:T(8,128)(2,1)S(1)}, u32[]{:S(2)}, u32[]{:S(2)}) async-start(bf16[16,16,256]{2,1,0:T(8,128)(2,1)} %past0.1), calls=%async_computation | async-start | bytes 262144 | tf_op jit(solution)/shard_map/all_to_all | solution.py:147
  32.1 2.8 %copy-done = bf16[4096,3,256]{2,0,1:T(8,128)(2,1)S(1)} copy-done((bf16[4096,3,256]{2,0,1:T(8,128)(2,1)S(1)}, bf16[4096,3,256]{2,0,1:T(8,128)(2,1)}, u32[]{:S(2)}) %copy-start) | copy-done | bytes 6291480
  34.9 0.7 copy-done.17
  35.6 0.0 copy-start.21
  35.6 0.0 copy-start.23
  35.6 2.2 %project.1.projected = bf16[3,16,256]{2,1,0:T(8,128)(2,1)S(1)} custom-call(bf16[16,16,256]{2,1,0:T(8,128)(2,1)S(1)} %all-to-all-done.1.gathered, f32[32,128]{1,0:T(8,128)S(1)} %bitcast.4, bf16[3,4096,256]{2,1,0:T(8,128)(2,1)S(1)} %bitcast.3), custom_call_target="tpu_custom_call" | custom-call | flops 100663296 | bytes 6291456 | tf_op jit(solution)/shard_map/project/pallas_call | solution.py:187
  37.8 0.0 copy-done.3
  37.8 0.0 copy-done.5
  37.8 0.0 copy-done.9
  37.8 0.0 copy-done.12
  37.8 0.0 copy-done.15
  37.8 0.0 copy-done.19
  37.9 0.0 copy-done.21
  37.9 0.0 copy-done.23
  37.9 2.1 %past1.1.part2 = bf16[16,16,256]{2,1,0:T(8,128)(2,1)S(1)} custom-call(s32[1]{0:T(128)S(6)} %convert_element_type.3.last, bf16[256,2,256]{2,1,0:T(2,128)(2,1)S(1)} %copy-done.19, bf16[256,2,256]{2,1,0:T(2,128)(2,1)S(1)} %copy-done.23, bf16[256,2,256]{2,1,0:T(2,128)(2,1)S(1)} %copy-done.9, bf16[256,2,256]{2,1,0:T(2,128)(2,1)S(1)} %copy-done.21, ...), custom_call_target="tpu_custom_call" | custom-call | flops 603979776 | bytes 4194304 | tf_op jit(solution)/shard_map/past1/pallas_call | solution.py:166
  40.0 0.0 all-to-all-done.arrived
  40.0 0.9 %payload.1 = bf16[16,64,256]{2,1,0:T(8,128)(2,1)} custom-call(bf16[16,16,256]{2,1,0:T(8,128)(2,1)S(1)} %all-to-all-done.arrived, bf16[3,16,256]{2,1,0:T(8,128)(2,1)S(1)} %project.1.projected, bf16[16,16,256]{2,1,0:T(8,128)(2,1)S(1)} %past1.1.part2), custom_call_target="tpu_custom_call" | custom-call | flops 1048576 | bytes 1048576 | tf_op jit(solution)/shard_map/payload/pallas_call | solution.py:197
  40.9 7.2 %all-to-all-start.2 = ((bf16[16,64,256]{2,1,0:T(8,128)(2,1)}), bf16[16,64,256]{2,1,0:T(8,128)(2,1)}, u32[]{:S(2)}, u32[]{:S(2)}) async-start(bf16[16,64,256]{2,1,0:T(8,128)(2,1)} %payload.1), calls=%async_computation.2 | async-start | bytes 1048576 | tf_op jit(solution)/shard_map/all_to_all | solution.py:147
  48.1 0.9 %copy-done.6 = bf16[512,256]{1,0:T(8,128)(2,1)S(1)} copy-done((bf16[512,256]{1,0:T(8,128)(2,1)S(1)}, bf16[512,256]{1,0:T(8,128)(2,1)}, u32[]{:S(2)}) %copy-start.6) | copy-done | bytes 262168
  49.0 0.9 %copy-done.10 = bf16[256,2,256]{2,1,0:T(2,128)(2,1)S(1)} copy-done((bf16[256,2,256]{2,1,0:T(2,128)(2,1)S(1)}, bf16[256,2,256]{2,1,0:T(2,128)(2,1)}, u32[]{:S(2)}) %copy-start.10) | copy-done | bytes 262168
  50.0 0.9 %near.6.spectra = f32[2,512,256]{2,1,0:T(8,128)S(1)} custom-call(bf16[256,2,256]{2,1,0:T(2,128)(2,1)S(1)} %copy-done.10, bf16[512,256]{1,0:T(8,128)(2,1)S(1)} %copy-done.6, bf16[512,256]{1,0:T(8,128)(2,1)S(1)} %copy-done.3), custom_call_target="tpu_custom_call" | custom-call | flops 268435456 | bytes 2097152 | tf_op jit(solution)/shard_map/near/pallas_call | solution.py:176
  50.9 8.5 %all-to-all-done.2.arrived = bf16[16,64,256]{2,1,0:T(8,128)(2,1)} async-done(((bf16[16,64,256]{2,1,0:T(8,128)(2,1)}), bf16[16,64,256]{2,1,0:T(8,128)(2,1)}, u32[]{:S(2)}, u32[]{:S(2)}) %all-to-all-start.2) | async-done | bytes 524320 | tf_op jit(solution)/shard_map/all_to_all | solution.py:147
  59.4 0.0 copy-done.1
  59.4 0.9 %copy-done.7 = bf16[512,256]{1,0:T(8,128)(2,1)S(1)} copy-done((bf16[512,256]{1,0:T(8,128)(2,1)S(1)}, bf16[512,256]{1,0:T(8,128)(2,1)}, u32[]{:S(2)}) %copy-start.7) | copy-done | bytes 262168
  60.3 0.9 %copy-done.13 = bf16[256,512]{1,0:T(8,128)(2,1)S(1)} copy-done((bf16[256,512]{1,0:T(8,128)(2,1)S(1)}, bf16[256,512]{1,0:T(8,128)(2,1)}, u32[]{:S(2)}) %copy-start.13) | copy-done | bytes 262168
  61.3 0.9 %copy-done.16 = bf16[256,512]{1,0:T(8,128)(2,1)S(1)} copy-done((bf16[256,512]{1,0:T(8,128)(2,1)S(1)}, bf16[256,512]{1,0:T(8,128)(2,1)}, u32[]{:S(2)}) %copy-start.16) | copy-done | bytes 262168
  62.2 3.1 %mix.1 = (bf16[16,16,256]{2,1,0:T(8,128)(2,1)S(1)}, bf16[16,256]{1,0:T(8,128)(2,1)}) custom-call(s32[1]{0:T(128)} %bitcast.index, bf16[16,64,256]{2,1,0:T(8,128)(2,1)} %all-to-all-done.2.arrived, bf16[3,16,256]{2,1,0:T(8,128)(2,1)S(1)} %project.1.projected, f32[2,512,256]{2,1,0:T(8,128)S(1)} %near.6.spectra, bf16[512,256]{1,0:T(8,128)(2,1)S(1)} %copy-done.7, ...), custom_call_target="tpu_custom_call" | custom-call | flops 536870912 | bytes 4194304 | tf_op jit(solution)/shard_map/mix/pallas_call | solution.py:207
  65.3 15.3 %all_to_all.20.arrived = bf16[16,16,256]{2,1,0:T(8,128)(2,1)S(1)} all-to-all(bf16[16,16,256]{2,1,0:T(8,128)(2,1)S(1)} %get-tuple-element.4), channel_id=1, replica_groups=mesh['ctx'=16,'chan'=16] {'chan'}, dimensions={0} | all-to-all | bytes 262144 | tf_op jit(solution)/shard_map/all_to_all | solution.py:147
  80.6 0.6 total.1
  (17 shorter events, 0.0 us)
Async XLA Ops:
  0.6 37.2 %copy-start.3 = (bf16[512,256]{1,0:T(8,128)(2,1)S(1)}, bf16[512,256]{1,0:T(8,128)(2,1)}, u32[]{:S(2)}) copy-start(bf16[512,256]{1,0:T(8,128)(2,1)} %constant.16.clone.fl) | copy-start | bytes 786436
  0.6 14.2 %collective-permute-start = (bf16[256,2,256]{2,1,0:T(2,128)(2,1)}, bf16[256,2,256]{2,1,0:T(2,128)(2,1)S(1)}, u32[]{:S(2)}, u32[]{:S(2)}) collective-permute-start(bf16[256,2,256]{2,1,0:T(2,128)(2,1)} %own.3), channel_id=1, source_target_pairs={{16,0},{32,16},{48,32},{64,48},{80,64},{96,80},{112,96},{128,112},... | collective-permute-start | bytes 786440 | tf_op jit(solution)/shard_map/ppermute | solution.py:160
  7.3 17.1 %all-to-all-start.1 = ((bf16[16,16,256]{2,1,0:T(8,128)(2,1)}), bf16[16,16,256]{2,1,0:T(8,128)(2,1)S(1)}, u32[]{:S(2)}, u32[]{:S(2)}) async-start(bf16[16,16,256]{2,1,0:T(8,128)(2,1)} %broadcast_in_dim.3), calls=%async_computation.1 | async-start | bytes 262144 | tf_op jit(solution)/shard_map/all_to_all | solution.py:147
  14.9 1.0 %copy-start.2 = (bf16[512,256]{1,0:T(8,128)(2,1)S(1)}, bf16[512,256]{1,0:T(8,128)(2,1)}, u32[]{:S(2)}) copy-start(bf16[512,256]{1,0:T(8,128)(2,1)} %constant.16.clone.fl) | copy-start | bytes 786436
  15.8 0.9 %copy-start.4 = (bf16[512,256]{1,0:T(8,128)(2,1)S(1)}, bf16[512,256]{1,0:T(8,128)(2,1)}, u32[]{:S(2)}) copy-start(bf16[512,256]{1,0:T(8,128)(2,1)} %constant.15.clone.fh) | copy-start | bytes 786436
  16.8 0.9 %copy-start.8 = (bf16[256,2,256]{2,1,0:T(2,128)(2,1)S(1)}, bf16[256,2,256]{2,1,0:T(2,128)(2,1)}, u32[]{:S(2)}) copy-start(bf16[256,2,256]{2,1,0:T(2,128)(2,1)} %near.7) | copy-start | bytes 786436
  17.7 0.9 %copy-start.11 = (bf16[256,512]{1,0:T(8,128)(2,1)S(1)}, bf16[256,512]{1,0:T(8,128)(2,1)}, u32[]{:S(2)}) copy-start(bf16[256,512]{1,0:T(8,128)(2,1)} %constant.18.clone.il) | copy-start | bytes 786436
  18.7 0.9 %copy-start.14 = (bf16[256,512]{1,0:T(8,128)(2,1)S(1)}, bf16[256,512]{1,0:T(8,128)(2,1)}, u32[]{:S(2)}) copy-start(bf16[256,512]{1,0:T(8,128)(2,1)} %constant.17.clone.ih) | copy-start | bytes 786436
  19.6 0.9 %copy-start.18 = (bf16[256,2,256]{2,1,0:T(2,128)(2,1)S(1)}, bf16[256,2,256]{2,1,0:T(2,128)(2,1)}, u32[]{:S(2)}) copy-start(bf16[256,2,256]{2,1,0:T(2,128)(2,1)} %own.3) | copy-start | bytes 786436
  20.6 0.9 %copy-start.20 = (bf16[256,2,256]{2,1,0:T(2,128)(2,1)S(1)}, bf16[256,2,256]{2,1,0:T(2,128)(2,1)}, u32[]{:S(2)}) copy-start(bf16[256,2,256]{2,1,0:T(2,128)(2,1)} %history.3) | copy-start | bytes 786436
  21.5 2.8 %copy-start.22 = (bf16[256,2,256]{2,1,0:T(2,128)(2,1)}, bf16[256,2,256]{2,1,0:T(2,128)(2,1)S(1)}, u32[]{:S(2)}) copy-start(bf16[256,2,256]{2,1,0:T(2,128)(2,1)S(1)} %collective-permute-done.border) | copy-start | bytes 786436
  21.5 16.3 %copy-start.5 = (bf16[512,256]{1,0:T(8,128)(2,1)S(1)}, bf16[512,256]{1,0:T(8,128)(2,1)}, u32[]{:S(2)}) copy-start(bf16[512,256]{1,0:T(8,128)(2,1)} %constant.15.clone.fh) | copy-start | bytes 786436
  21.5 37.8 %copy-start.1 = (bf16[256,4096]{1,0:T(8,128)(2,1)S(1)}, bf16[256,4096]{1,0:T(8,128)(2,1)}, u32[]{:S(2)}) copy-start(bf16[256,4096]{1,0:T(8,128)(2,1)} %w_out.1) | copy-start | bytes 6291460
  24.3 15.6 %all-to-all-start = ((bf16[16,16,256]{2,1,0:T(8,128)(2,1)}), bf16[16,16,256]{2,1,0:T(8,128)(2,1)S(1)}, u32[]{:S(2)}, u32[]{:S(2)}) async-start(bf16[16,16,256]{2,1,0:T(8,128)(2,1)} %past0.1), calls=%async_computation | async-start | bytes 262144 | tf_op jit(solution)/shard_map/all_to_all | solution.py:147
  32.1 2.8 %copy-start = (bf16[4096,3,256]{2,0,1:T(8,128)(2,1)S(1)}, bf16[4096,3,256]{2,0,1:T(8,128)(2,1)}, u32[]{:S(2)}) copy-start(bf16[4096,3,256]{2,0,1:T(8,128)(2,1)} %param.13) | copy-start | bytes 18874372
  34.9 0.7 copy-start.17
  35.6 2.2 %copy-start.9 = (bf16[256,2,256]{2,1,0:T(2,128)(2,1)S(1)}, bf16[256,2,256]{2,1,0:T(2,128)(2,1)}, u32[]{:S(2)}) copy-start(bf16[256,2,256]{2,1,0:T(2,128)(2,1)} %near.7) | copy-start | bytes 786436
  35.6 2.2 %copy-start.12 = (bf16[256,512]{1,0:T(8,128)(2,1)S(1)}, bf16[256,512]{1,0:T(8,128)(2,1)}, u32[]{:S(2)}) copy-start(bf16[256,512]{1,0:T(8,128)(2,1)} %constant.18.clone.il) | copy-start | bytes 786436
  35.6 2.2 %copy-start.15 = (bf16[256,512]{1,0:T(8,128)(2,1)S(1)}, bf16[256,512]{1,0:T(8,128)(2,1)}, u32[]{:S(2)}) copy-start(bf16[256,512]{1,0:T(8,128)(2,1)} %constant.17.clone.ih) | copy-start | bytes 786436
  35.6 2.2 %copy-start.19 = (bf16[256,2,256]{2,1,0:T(2,128)(2,1)S(1)}, bf16[256,2,256]{2,1,0:T(2,128)(2,1)}, u32[]{:S(2)}) copy-start(bf16[256,2,256]{2,1,0:T(2,128)(2,1)} %own.3) | copy-start | bytes 786436
  35.6 2.3 %copy-start.21 = (bf16[256,2,256]{2,1,0:T(2,128)(2,1)S(1)}, bf16[256,2,256]{2,1,0:T(2,128)(2,1)}, u32[]{:S(2)}) copy-start(bf16[256,2,256]{2,1,0:T(2,128)(2,1)} %history.3) | copy-start | bytes 786436
  35.6 2.2 %copy-start.23 = (bf16[256,2,256]{2,1,0:T(2,128)(2,1)S(1)}, bf16[256,2,256]{2,1,0:T(2,128)(2,1)}, u32[]{:S(2)}) copy-start(bf16[256,2,256]{2,1,0:T(2,128)(2,1)} %copy-done.22) | copy-start | bytes 786436
  40.9 18.5 %all-to-all-start.2 = ((bf16[16,64,256]{2,1,0:T(8,128)(2,1)}), bf16[16,64,256]{2,1,0:T(8,128)(2,1)}, u32[]{:S(2)}, u32[]{:S(2)}) async-start(bf16[16,64,256]{2,1,0:T(8,128)(2,1)} %payload.1), calls=%async_computation.2 | async-start | bytes 1048576 | tf_op jit(solution)/shard_map/all_to_all | solution.py:147
  48.1 0.9 %copy-start.6 = (bf16[512,256]{1,0:T(8,128)(2,1)S(1)}, bf16[512,256]{1,0:T(8,128)(2,1)}, u32[]{:S(2)}) copy-start(bf16[512,256]{1,0:T(8,128)(2,1)} %constant.15.clone.fh) | copy-start | bytes 786436
  49.0 0.9 %copy-start.10 = (bf16[256,2,256]{2,1,0:T(2,128)(2,1)S(1)}, bf16[256,2,256]{2,1,0:T(2,128)(2,1)}, u32[]{:S(2)}) copy-start(bf16[256,2,256]{2,1,0:T(2,128)(2,1)} %near.7) | copy-start | bytes 786436
  59.4 1.0 %copy-start.7 = (bf16[512,256]{1,0:T(8,128)(2,1)S(1)}, bf16[512,256]{1,0:T(8,128)(2,1)}, u32[]{:S(2)}) copy-start(bf16[512,256]{1,0:T(8,128)(2,1)} %constant.15.clone.fh) | copy-start | bytes 786436
  60.3 0.9 %copy-start.13 = (bf16[256,512]{1,0:T(8,128)(2,1)S(1)}, bf16[256,512]{1,0:T(8,128)(2,1)}, u32[]{:S(2)}) copy-start(bf16[256,512]{1,0:T(8,128)(2,1)} %constant.18.clone.il) | copy-start | bytes 786436
  61.3 0.9 %copy-start.16 = (bf16[256,512]{1,0:T(8,128)(2,1)S(1)}, bf16[256,512]{1,0:T(8,128)(2,1)}, u32[]{:S(2)}) copy-start(bf16[256,512]{1,0:T(8,128)(2,1)} %constant.17.clone.ih) | copy-start | bytes 786436

commit v2 on v1

v2 whole, which is shorter than its diff:
```python
import jax
import jax.numpy as jnp
import numpy as np
from jax import lax
from jax.experimental import pallas as pl
from jax.experimental.pallas import tpu as pltpu
from jax.sharding import PartitionSpec as P

BF16 = jnp.bfloat16
F32 = jnp.float32
VMEM = pl.BlockSpec(memory_space=pltpu.VMEM)
SMEM = pl.BlockSpec(memory_space=pltpu.SMEM)
HBM = pl.BlockSpec(memory_space=pltpu.HBM)
LIMIT = 24 << 20


def split_up(table):
    high = np.asarray(table, np.float32).astype(jnp.bfloat16)
    low = (table - high.astype(np.float64)).astype(np.float32).astype(jnp.bfloat16)
    return np.stack([high, low])


def dft_tables(length):
    order = np.concatenate([np.arange(0, length, 2), np.arange(1, length, 2)])
    theta = np.pi * (order + 0.5) / length
    angle = theta[:, None] * np.arange(length)[None, :]
    forward = np.concatenate([np.cos(angle), np.sin(angle)], 0)
    back = theta[None, :] * (length - 1 - np.arange(length))[:, None]
    inverse = np.concatenate([np.cos(back), -np.sin(back)], 1) / length
    return split_up(forward), split_up(inverse)


def dot(a, b):
    return jnp.dot(a, b, preferred_element_type=F32)


def spectrum(forward, rows):
    return dot(forward[0], rows) + dot(forward[1], rows)


def back_to_time(high, low, product):
    upper = product.astype(BF16)
    lower = (product - upper.astype(F32)).astype(BF16)
    return dot(high, upper) + dot(high, lower) + dot(low, upper)


def times_conjugate(window, signal):
    half = window.shape[0] // 2
    wc, ws = window[:half], window[half:]
    sc, ss = signal[:half], signal[half:]
    return jnp.concatenate([wc * sc + ws * ss, wc * ss - ws * sc], 0)


def past_kernel(last, border, own, near, history, f_hbm, i_hbm, gain_hbm, products, near_v, f, i, gain, own_v, history_v, sems):
    pairs = [(own, own_v), (f_hbm, f), (near, near_v), (history, history_v), (i_hbm, i), (gain_hbm, gain)]
    copies = [pltpu.make_async_copy(a, b, sems.at[n]) for n, (a, b) in enumerate(pairs)]
    for copy in copies:
        copy.start()
    half = f.shape[1] // 2
    quarter = half // 2
    for copy in copies[:4]:
        copy.wait()
    for which in range(2):
        first = spectrum(f, own_v[:, which, :])
        second = spectrum(f, jnp.where(last[0] > 0, near_v[:, which, :], border[:, which, :]))
        bc, bs = second[:half], second[half:]
        window = first + jnp.concatenate([-bs[:quarter], bs[quarter:], bc[:quarter], -bc[quarter:]], 0)
        products[which] = times_conjugate(window, spectrum(f, history_v[:, which, :]))
    for copy in copies[4:]:
        copy.wait()


def project_kernel(
    index, gathered, gain, w_hbm, f, i, near, products, out, gates, spectrum_two, padded, w, sems
):
    pieces, rows, width = gathered.shape
    steps = sems.shape[0]
    per = pieces // steps
    copies = []
    for q in range(steps):
        span = pl.ds(q * per * width, per * width)
        copies.append(pltpu.make_async_copy(w_hbm.at[:, span, :], w.at[:, span, :], sems.at[q]))
        copies[-1].start()
    part_two = back_to_time(i[0], i[1], products[1]).astype(BF16)
    out[:, rows:] = part_two.reshape(out.shape[0], rows, width)
    spectrum_two[...] = spectrum(f, near[:, 1, :])
    spectrum_one = spectrum(f, near[:, 0, :])
    total = jnp.zeros((rows, width), F32)
    for s in range(pieces):
        x = gathered[s].astype(F32)
        total += x * x
    mean_sq = jnp.sum(total, axis=1, keepdims=True) / (pieces * width)
    scale = lax.rsqrt(mean_sq + 1e-06)
    sums = [jnp.zeros((rows, width), F32) for _ in range(3)]
    for s in range(pieces):
        if s % per == 0:
            copies[s // per].wait()
        g = jnp.concatenate([gain[2 * s : 2 * s + 1], gain[2 * s + 1 : 2 * s + 2]], 1)
        normed = (gathered[s].astype(F32) * scale * g).astype(BF16)
        for k in range(3):
            sums[k] += dot(normed, w[k, s * width : (s + 1) * width, :])
    gates[0] = sums[1].astype(BF16)
    gates[1] = sums[2].astype(BF16)
    padded[...] = jnp.zeros_like(padded)
    padded[pl.ds(pl.multiple_of(index[0] * rows, rows), rows), :] = sums[0].astype(BF16)
    product = products[0] + times_conjugate(spectrum_one, spectrum(f, padded[...]))
    part_one = back_to_time(i[0], i[1], product).astype(BF16)
    out[:, :rows] = part_one.reshape(out.shape[0], rows, width)


def gate_kernel(arrived, gates, copies, gated, past_two):
    sums = jnp.sum(arrived[...].astype(F32), axis=0)
    rows = sums.shape[0] // 2
    own = (gates[0].astype(F32) * sums[:rows]).astype(BF16)
    gated[...] = own
    past_two[...] = sums[rows:]
    for d in range(copies.shape[0]):
        copies[d] = own


def mix_kernel(index, gated, gates, past_two, spectrum_two, f, i, w_hbm, partial, w_out, sem):
    load = pltpu.make_async_copy(w_hbm, w_out, sem)
    load.start()
    count, rows, width = gated.shape
    own = pl.ds(pl.multiple_of(index[0] * rows, rows), rows)
    signal = spectrum(f, gated[...].reshape(count * rows, width))
    second = back_to_time(i[0, own, :], i[1, own, :], times_conjugate(spectrum_two[...], signal))
    mixed_in = (gates[1].astype(F32) * (past_two[...] + second)).astype(BF16)
    load.wait()
    for d in range(partial.shape[0]):
        partial[d] = dot(mixed_in, w_out[:, d * width : (d + 1) * width]).astype(BF16)


def total_kernel(arrived, out):
    out[...] = jnp.sum(arrived[...].astype(F32), axis=0).astype(BF16)


def call(kernel, out_shape, in_specs, flops, nbytes, scratch=(), name=None, limit=LIMIT):
    return pl.pallas_call(
        kernel,
        out_shape=out_shape,
        in_specs=in_specs,
        out_specs=jax.tree.map(lambda _: VMEM, out_shape),
        scratch_shapes=list(scratch),
        cost_estimate=pl.CostEstimate(flops=flops, bytes_accessed=nbytes, transcendentals=0),
        compiler_params=pltpu.CompilerParams(vmem_limit_bytes=limit),
        name=name,
    )


def in_hbm(array):
    return pltpu.with_memory_space_constraint(array, pltpu.HBM)


def exchanged(array, axis):
    return lax.all_to_all(array, axis, split_axis=0, concat_axis=0, tiled=True)


def per_device(inputs, gain, w_in, w_out, history, filt_far, filt_near):
    rows, width = inputs.shape
    fresh = filt_near.shape[0]
    ctx_count = lax.axis_size("ctx")
    chan_count = lax.axis_size("chan")
    ctx_index = lax.axis_index("ctx")
    forward, inverse = [jnp.asarray(t) for t in dft_tables(fresh)]
    index = ctx_index.reshape(1).astype(jnp.int32)
    last = (index == ctx_count - 1).astype(jnp.int32)

    border = lax.ppermute(filt_far, "ctx", [(i, i - 1) for i in range(1, ctx_count)])
    gathered = exchanged(jnp.broadcast_to(inputs, (chan_count, rows, width)), "chan")

    unit = fresh * fresh * 4 * width
    w_three = w_in.transpose(1, 0, 2)
    scales = gain.reshape(-1, 128)
    whole = jax.ShapeDtypeStruct((2, 2 * fresh, width), F32)
    products, near, f, i, scales = call(
        past_kernel,
        (whole, *(jax.ShapeDtypeStruct(a.shape, a.dtype) for a in (filt_near, forward, inverse, scales))),
        [SMEM, VMEM] + [HBM] * 6,
        unit * 12,
        2 << 20,
        scratch=[pltpu.VMEM(filt_far.shape, BF16)] * 2 + [pltpu.SemaphoreType.DMA((6,))],
        name="past",
    )(last, border, *(in_hbm(a) for a in (filt_far, filt_near, history, forward, inverse, scales)))

    blocks = jax.ShapeDtypeStruct((ctx_count, rows, width), BF16)
    payload, gates, spectrum_two = call(
        project_kernel,
        (
            jax.ShapeDtypeStruct((ctx_count, 2 * rows, width), BF16),
            jax.ShapeDtypeStruct((2, rows, width), BF16),
            jax.ShapeDtypeStruct(whole.shape[1:], F32),
        ),
        [SMEM, VMEM, VMEM, HBM] + [VMEM] * 4,
        2 * rows * w_in.size + unit * 12,
        2 * w_in.size,
        scratch=[
            pltpu.VMEM((fresh, width), BF16),
            pltpu.VMEM(w_three.shape, BF16),
            pltpu.SemaphoreType.DMA((8,)),
        ],
        name="project",
    )(index, gathered, scales, in_hbm(w_three), f, i, near, products)

    copies, gated, past_two = call(
        gate_kernel,
        (blocks, jax.ShapeDtypeStruct((rows, width), BF16), jax.ShapeDtypeStruct((rows, width), F32)),
        [VMEM] * 2,
        1 << 20,
        1 << 19,
        name="gate",
    )(exchanged(payload, "ctx"), gates)

    partial = call(
        mix_kernel,
        jax.ShapeDtypeStruct((chan_count, rows, width), BF16),
        [SMEM] + [VMEM] * 6 + [HBM],
        unit * 5,
        4 << 20,
        scratch=[pltpu.VMEM(w_out.shape, BF16), pltpu.SemaphoreType.DMA],
        name="mix",
    )(index, exchanged(copies, "ctx"), gates, past_two, spectrum_two, f, i, in_hbm(w_out))
    mixed = call(
        total_kernel,
        jax.ShapeDtypeStruct((rows, width), BF16),
        [VMEM],
        1 << 16,
        1 << 17,
        name="total",
    )(exchanged(partial, "chan"))
    return (mixed, gated)


def solution(mesh):
    placed = (
        P("ctx", "chan"),
        P(),
        P(None, None, "chan"),
        P("chan", None),
        P("ctx", None, "chan"),
        P("ctx", None, "chan"),
        P(None, None, "chan"),
    )
    return jax.shard_map(
        per_device,
        mesh=mesh,
        in_specs=placed,
        out_specs=(P("ctx", "chan"), P("ctx", "chan")),
        check_vma=False,
    )
```

time: 82.5 us -> 71.6 us (0.87); the launches traced: 81.3 us -> 71.2 us
  blocking collectives: 15.3 us -> 38.3 us
  starting transfers between devices: 27.8 us -> 12.7 us
  local copies, waits for them, and re-layouts: 16.3 us -> 1.35 us
  waiting for transfers between devices: 8.51 us -> 5.55 us
    all_to_all x1 -> x3, blocking collectives: 15.3 us -> 38.3 us  [exchanged(): return lax.all_to_all(array, axis, split_axis=0, concat_axis=0, tiled=True)]
    all_to_all x3 -> x1, starting transfers between devices: 22.6 us -> 7.59 us  [exchanged(): return lax.all_to_all(array, axis, split_axis=0, concat_axis=0, tiled=True)]
    unnamed x48 -> x0, local copies, waits for them, and re-layouts: 14.9 us -> none
    all_to_all x3 -> x1, waiting for transfers between devices: 8.51 us -> 5.55 us  [exchanged(): return lax.all_to_all(array, axis, split_axis=0, concat_axis=0, tiled=True)]
    pallas_call x6 -> x4, Pallas kernels: 11.9 us -> 12 us  [the longest x1 5.05 us: per_device(): call(project_kernel, (jax.ShapeDtypeStruct((ctx_count, 2 * rows, width),...]
  transfers between devices with their start and end apart: 4 -> 2, of which waited for: 1 -> 1; matrix products, arithmetic and copies ran while one was open for 2% -> 2% of each run, Pallas kernels for 10% -> 5%
where the time goes in v2:
time: 71.6 us; the launch traced here: 71.2 us
  blocking collectives  38.3 us (53%)
  starting transfers between devices  12.7 us (18%)
  Pallas kernels  12.6 us (18%)
  waiting for transfers between devices  5.55 us (8%)
  local copies, waits for them, and re-layouts  1.35 us (2%)
    all_to_all x3, blocking collectives, exchanged(): return lax.all_to_all(array, axis, split_axis=0, concat_axis=0, tiled=True)  38.3 us
    all_to_all x1, starting transfers between devices, exchanged(): return lax.all_to_all(array, axis, split_axis=0, concat_axis=0, tiled=True)  7.59 us
    all_to_all x1, waiting for transfers between devices, exchanged(): return lax.all_to_all(array, axis, split_axis=0, concat_axis=0, tiled=True)  5.55 us
    ppermute x1, starting transfers between devices, per_device(): lax.ppermute(filt_far, 'ctx', [(i, i - 1) for i in range(1, ctx_count)])  5.11 us
    pallas_call x1, Pallas kernels, per_device(): call(project_kernel, (jax.ShapeDtypeStruct((ctx_count, 2 * rows, width),...  5.05 us
    pallas_call x1, Pallas kernels, per_device(): call(past_kernel, (whole, *(jax.ShapeDtypeStruct(a.shape, a.dtype) for a...  3.88 us
    pallas_call x1, Pallas kernels, per_device(): call(mix_kernel, jax.ShapeDtypeStruct((chan_count, rows, width), BF16), [...  2.47 us
  transfers between devices with their start and end apart: 2, of which 1 were waited for; matrix products, arithmetic and copies ran while one was open for 2% of the time, Pallas kernels for 5%

profile of v2, /device:TPU:1, one launch (start us, length us, event | category | flops | bytes accessed | tf_op | source)
XLA Modules:
  0.0 71.2 jit_solution(13210718879576671187)
XLA Ops:
  0.6 5.1 %collective-permute-start = (bf16[256,2,256]{2,1,0:T(2,128)(2,1)}, bf16[256,2,256]{2,1,0:T(2,128)(2,1)S(1)}, u32[]{:S(2)}, u32[]{:S(2)}) collective-permute-start(bf16[256,2,256]{2,1,0:T(2,128)(2,1)} %own.1), channel_id=1, source_target_pairs={{16,0},{32,16},{48,32},{64,48},{80,64},{96,80},{112,96},{128,112},... | collective-permute-start | bytes 786440 | tf_op jit(solution)/shard_map/ppermute | solution.py:169
  5.7 1.4 %broadcast_in_dim.3 = bf16[16,16,256]{2,1,0:T(8,128)(2,1)} broadcast(bf16[16,256]{1,0:T(8,128)(2,1)} %param.9), dimensions={1,2} | broadcast | bytes 139264 | tf_op jit(solution)/shard_map/broadcast_in_dim | solution.py:170
  7.1 7.6 %all-to-all-start = ((bf16[16,16,256]{2,1,0:T(8,128)(2,1)}), bf16[16,16,256]{2,1,0:T(8,128)(2,1)S(1)}, u32[]{:S(2)}, u32[]{:S(2)}) async-start(bf16[16,16,256]{2,1,0:T(8,128)(2,1)} %broadcast_in_dim.3), calls=%async_computation | async-start | bytes 262144 | tf_op jit(solution)/shard_map/all_to_all | solution.py:156
  14.7 0.0 collective-permute-done.border
  14.7 3.9 %past.1 = (f32[2,512,256]{2,1,0:T(8,128)S(1)}, bf16[256,2,256]{2,1,0:T(2,128)(2,1)S(1)}, bf16[2,512,256]{2,1,0:T(8,128)(2,1)S(1)}, bf16[2,256,512]{2,1,0:T(8,128)(2,1)S(1)}, f32[32,128]{1,0:T(8,128)S(1)}) custom-call(s32[1]{0:T(128)S(6)} %convert_element_type.3.last, bf16[256,2,256]{2,1,0:T(2,128)(2,1)S(1)} %collective-permute-done.border, ...), custom_call_target="tpu_custom_call" | custom-call | flops 805306368 | bytes 2097152 | tf_op jit(solution)/shard_map/past/pallas_call | solution.py:176
  18.6 5.5 %all-to-all-done.gathered = bf16[16,16,256]{2,1,0:T(8,128)(2,1)S(1)} async-done(((bf16[16,16,256]{2,1,0:T(8,128)(2,1)}), bf16[16,16,256]{2,1,0:T(8,128)(2,1)S(1)}, u32[]{:S(2)}, u32[]{:S(2)}) %all-to-all-start) | async-done | bytes 131104 | tf_op jit(solution)/shard_map/all_to_all | solution.py:156
  24.2 5.1 %project.1 = (bf16[16,32,256]{2,1,0:T(8,128)(2,1)S(1)}, bf16[2,16,256]{2,1,0:T(8,128)(2,1)S(1)}, f32[512,256]{1,0:T(8,128)S(1)}) custom-call(s32[1]{0:T(128)} %bitcast.index, bf16[16,16,256]{2,1,0:T(8,128)(2,1)S(1)} %all-to-all-done.gathered, f32[32,128]{1,0:T(8,128)S(1)} %get-tuple-element.13.gain, bf16[3,4096,256]{2,1,0:T(8,128)(2,1)} %bitcast.3, ...), custom_call_target="tpu_custom_call" | custom-call | flops 905969664 | bytes 6291456 | tf_op jit(solution)/shard_map/project/pallas_call | solution.py:187
  29.2 16.4 %all_to_all.20.arrived = bf16[16,32,256]{2,1,0:T(8,128)(2,1)S(1)} all-to-all(bf16[16,32,256]{2,1,0:T(8,128)(2,1)S(1)} %get-tuple-element.18), channel_id=1, replica_groups=mesh['ctx'=16,'chan'=16] {'ctx'}, dimensions={0} | all-to-all | bytes 524288 | tf_op jit(solution)/shard_map/all_to_all | solution.py:156
  45.6 0.6 gate.1
  46.3 10.6 %all_to_all.21.gated = bf16[16,16,256]{2,1,0:T(8,128)(2,1)S(1)} all-to-all(bf16[16,16,256]{2,1,0:T(8,128)(2,1)S(1)} %get-tuple-element.20), channel_id=1, replica_groups=mesh['ctx'=16,'chan'=16] {'ctx'}, dimensions={0} | all-to-all | bytes 262144 | tf_op jit(solution)/shard_map/all_to_all | solution.py:156
  56.8 2.5 %mix.1 = bf16[16,16,256]{2,1,0:T(8,128)(2,1)S(1)} custom-call(s32[1]{0:T(128)} %bitcast.index, bf16[16,16,256]{2,1,0:T(8,128)(2,1)S(1)} %all_to_all.21.gated, bf16[2,16,256]{2,1,0:T(8,128)(2,1)S(1)} %get-tuple-element.19.gates, f32[16,256]{1,0:T(8,128)S(1)} %get-tuple-element.21.past_two, f32[512,256]{1,0:T(8,128)S(1)} %get-tuple-element.22.spectrum_two, ...), custom_call_target="tpu_custom_call" | custom-call | flops 335544320 | bytes 4194304 | tf_op jit(solution)/shard_map/mix/pallas_call | solution.py:214
  59.3 11.3 %all_to_all.22.arrived = bf16[16,16,256]{2,1,0:T(8,128)(2,1)S(1)} all-to-all(bf16[16,16,256]{2,1,0:T(8,128)(2,1)S(1)} %mix.1), channel_id=1, replica_groups=mesh['ctx'=16,'chan'=16] {'chan'}, dimensions={0} | all-to-all | bytes 262144 | tf_op jit(solution)/shard_map/all_to_all | solution.py:156
  70.6 0.6 total.1
Async XLA Ops:
  0.6 14.1 %collective-permute-start = (bf16[256,2,256]{2,1,0:T(2,128)(2,1)}, bf16[256,2,256]{2,1,0:T(2,128)(2,1)S(1)}, u32[]{:S(2)}, u32[]{:S(2)}) collective-permute-start(bf16[256,2,256]{2,1,0:T(2,128)(2,1)} %own.1), channel_id=1, source_target_pairs={{16,0},{32,16},{48,32},{64,48},{80,64},{96,80},{112,96},{128,112},... | collective-permute-start | bytes 786440 | tf_op jit(solution)/shard_map/ppermute | solution.py:169
  7.1 17.1 %all-to-all-start = ((bf16[16,16,256]{2,1,0:T(8,128)(2,1)}), bf16[16,16,256]{2,1,0:T(8,128)(2,1)S(1)}, u32[]{:S(2)}, u32[]{:S(2)}) async-start(bf16[16,16,256]{2,1,0:T(8,128)(2,1)} %broadcast_in_dim.3), calls=%async_computation | async-start | bytes 262144 | tf_op jit(solution)/shard_map/all_to_all | solution.py:156

commit v3 on v2

v3 whole, which is shorter than its diff:
```python
import jax
import jax.numpy as jnp
import numpy as np
from jax import lax
from jax.experimental import pallas as pl
from jax.experimental.pallas import tpu as pltpu
from jax.sharding import PartitionSpec as P

BF16 = jnp.bfloat16
F32 = jnp.float32
VMEM = pl.BlockSpec(memory_space=pltpu.VMEM)
SMEM = pl.BlockSpec(memory_space=pltpu.SMEM)
HBM = pl.BlockSpec(memory_space=pltpu.HBM)
LIMIT = 24 << 20


def split_up(table):
    high = np.asarray(table, np.float32).astype(jnp.bfloat16)
    low = (table - high.astype(np.float64)).astype(np.float32).astype(jnp.bfloat16)
    return np.stack([high, low])


def dft_tables(length):
    order = np.concatenate([np.arange(0, length, 2), np.arange(1, length, 2)])
    theta = np.pi * (order + 0.5) / length
    angle = theta[:, None] * np.arange(length)[None, :]
    forward = np.concatenate([np.cos(angle), np.sin(angle)], 0)
    back = theta[None, :] * (length - 1 - np.arange(length))[:, None]
    inverse = np.concatenate([np.cos(back), -np.sin(back)], 1) / length
    return split_up(forward), split_up(inverse)


def dot(a, b):
    return jnp.dot(a, b, preferred_element_type=F32)


def spectrum(forward, rows):
    return dot(forward[0], rows) + dot(forward[1], rows)


def back_to_time(high, low, product):
    upper = product.astype(BF16)
    lower = (product - upper.astype(F32)).astype(BF16)
    return dot(high, upper) + dot(high, lower) + dot(low, upper)


def times_conjugate(window, signal):
    half = window.shape[0] // 2
    wc, ws = window[:half], window[half:]
    sc, ss = signal[:half], signal[half:]
    return jnp.concatenate([wc * sc + ws * ss, wc * ss - ws * sc], 0)


def past_part(which, last, own, border, near, history, f, i):
    half = f.shape[1] // 2
    quarter = half // 2
    first = spectrum(f, own[:, which, :])
    second = spectrum(f, jnp.where(last[0] > 0, near[:, which, :], border[:, which, :]))
    bc, bs = second[:half], second[half:]
    window = first + jnp.concatenate([-bs[:quarter], bs[quarter:], bc[:quarter], -bc[quarter:]], 0)
    return back_to_time(i[0], i[1], times_conjugate(window, spectrum(f, history[:, which, :]))).astype(BF16)


def past_kernel(
    last, border, own_hbm, near_hbm, history_hbm, f_hbm, i_hbm, gain_hbm,
    part_one, own, near, history, f, i, gain, sems,
):
    pairs = [(own_hbm, own), (f_hbm, f), (near_hbm, near), (history_hbm, history), (i_hbm, i), (gain_hbm, gain)]
    copies = [pltpu.make_async_copy(a, b, sems.at[n]) for n, (a, b) in enumerate(pairs)]
    for copy in copies:
        copy.start()
    for copy in copies:
        copy.wait()
    part_one[...] = past_part(0, last, own, border, near, history, f, i)


def project_kernel(last, gathered, gain, w_hbm, own, border, near, history, f, i, out, gate_two, w, sems):
    pieces, rows, width = gathered.shape
    steps = sems.shape[0]
    per = pieces // steps
    copies = []
    for q in range(steps):
        span = pl.ds(q * per * width, per * width)
        copies.append(pltpu.make_async_copy(w_hbm.at[:, span, :], w.at[:, span, :], sems.at[q]))
        copies[-1].start()
    part_two = past_part(1, last, own, border, near, history, f, i)
    out[:, 2 * rows :] = part_two.reshape(out.shape[0], rows, width)
    total = jnp.zeros((rows, width), F32)
    for s in range(pieces):
        x = gathered[s].astype(F32)
        total += x * x
    mean_sq = jnp.sum(total, axis=1, keepdims=True) / (pieces * width)
    scale = lax.rsqrt(mean_sq + 1e-06)
    sums = [jnp.zeros((rows, width), F32) for _ in range(3)]
    for s in range(pieces):
        if s % per == 0:
            copies[s // per].wait()
        g = jnp.concatenate([gain[2 * s : 2 * s + 1], gain[2 * s + 1 : 2 * s + 2]], 1)
        normed = (gathered[s].astype(F32) * scale * g).astype(BF16)
        for k in range(3):
            sums[k] += dot(normed, w[k, s * width : (s + 1) * width, :])
    gate_two[...] = sums[2].astype(BF16)
    shared = jnp.concatenate([sums[0].astype(BF16), sums[1].astype(BF16)], 0)
    for d in range(out.shape[0]):
        out[d, : 2 * rows] = shared


def near_kernel(near, f, spectra):
    for which in range(2):
        spectra[which] = spectrum(f, near[:, which, :])


def mix_kernel(
    index, arrived, gate_two, sum_here, sum_there, spectra, f, i, w_hbm, partial, gated_own, gated_all, w_out, sem
):
    load = pltpu.make_async_copy(w_hbm, w_out, sem)
    load.start()
    count, packed, width = arrived.shape
    rows = packed // 3
    fresh = count * rows
    values = arrived[:, :rows].reshape(fresh, width)
    gate_one = arrived[:, rows : 2 * rows].reshape(fresh, width).astype(F32)
    past_one = sum_here[...].astype(F32) + sum_there[...].astype(F32)
    first = back_to_time(i[0], i[1], times_conjugate(spectra[0], spectrum(f, values)))
    gated = (gate_one * (past_one + first)).astype(BF16)
    gated_all[...] = gated
    own = pl.ds(pl.multiple_of(index[0] * rows, rows), rows)
    gated_own[...] = gated_all[own, :]
    second = back_to_time(i[0, own, :], i[1, own, :], times_conjugate(spectra[1], spectrum(f, gated)))
    past_two = jnp.sum(arrived[:, 2 * rows :].astype(F32), axis=0)
    mixed_in = (gate_two[...].astype(F32) * (past_two + second)).astype(BF16)
    load.wait()
    for d in range(partial.shape[0]):
        partial[d] = dot(mixed_in, w_out[:, d * width : (d + 1) * width]).astype(BF16)


def total_kernel(arrived, out):
    out[...] = jnp.sum(arrived[...].astype(F32), axis=0).astype(BF16)


def call(kernel, out_shape, in_specs, flops, nbytes, scratch=(), limit=LIMIT):
    return pl.pallas_call(
        kernel,
        out_shape=out_shape,
        in_specs=in_specs,
        out_specs=jax.tree.map(lambda _: VMEM, out_shape),
        scratch_shapes=list(scratch),
        cost_estimate=pl.CostEstimate(flops=flops, bytes_accessed=nbytes, transcendentals=0),
        compiler_params=pltpu.CompilerParams(vmem_limit_bytes=limit),
    )


def in_hbm(array):
    return pltpu.with_memory_space_constraint(array, pltpu.HBM)


def exchanged(array, axis):
    return lax.all_to_all(array, axis, split_axis=0, concat_axis=0, tiled=True)


def swapped(array, axis, step):
    return lax.ppermute(array, axis, [(i, i ^ step) for i in range(lax.axis_size(axis))])


def added(a, b):
    return (a.astype(F32) + b.astype(F32)).astype(BF16)


def layer(inputs, gain, w_in, w_out, history, filt_far, filt_near):
    rows, width = inputs.shape
    fresh = filt_near.shape[0]
    ctx_count = lax.axis_size("ctx")
    chan_count = lax.axis_size("chan")
    ctx_index = lax.axis_index("ctx")
    forward, inverse = [jnp.asarray(t) for t in dft_tables(fresh)]
    index = ctx_index.reshape(1).astype(jnp.int32)
    last = (index == ctx_count - 1).astype(jnp.int32)

    border = lax.ppermute(filt_far, "ctx", [(i, i - 1) for i in range(1, ctx_count)])
    gathered = exchanged(jnp.broadcast_to(inputs, (chan_count, rows, width)), "chan")

    unit = fresh * fresh * 4 * width
    w_three = w_in.transpose(1, 0, 2)
    scales = gain.reshape(-1, 128)
    part_one, own, near, history, f, i, scales = call(
        past_kernel,
        (
            jax.ShapeDtypeStruct((fresh, width), BF16),
            *(
                jax.ShapeDtypeStruct(a.shape, a.dtype)
                for a in (filt_far, filt_near, history, forward, inverse, scales)
            ),
        ),
        [SMEM, VMEM] + [HBM] * 6,
        unit * 9,
        2 << 20,
        scratch=[pltpu.SemaphoreType.DMA((6,))],
    )(last, border, *(in_hbm(a) for a in (filt_far, filt_near, history, forward, inverse, scales)))

    here = part_one
    there = swapped(here, "ctx", 1)
    here = added(here, there)
    there = swapped(here, "ctx", 4)

    payload, gate_two = call(
        project_kernel,
        (
            jax.ShapeDtypeStruct((ctx_count, 3 * rows, width), BF16),
            jax.ShapeDtypeStruct((rows, width), BF16),
        ),
        [SMEM, VMEM, VMEM, HBM] + [VMEM] * 6,
        2 * rows * w_in.size + unit * 9,
        2 * w_in.size,
        scratch=[pltpu.VMEM(w_three.shape, BF16), pltpu.SemaphoreType.DMA((8,))],
    )(last, gathered, scales, in_hbm(w_three), own, border, near, history, f, i)

    here = added(here, there)
    payload, here = lax.optimization_barrier((payload, here))
    there = swapped(here, "ctx", 8)
    arrived = exchanged(payload, "ctx")
    here = added(here, there)
    there = swapped(here, "ctx", 2)
    spectra = call(
        near_kernel, jax.ShapeDtypeStruct((2, 2 * fresh, width), F32), [VMEM] * 2, unit * 4, 2 << 20
    )(near, f)

    partial, gated = call(
        mix_kernel,
        (
            jax.ShapeDtypeStruct((chan_count, rows, width), BF16),
            jax.ShapeDtypeStruct((rows, width), BF16),
        ),
        [SMEM] + [VMEM] * 7 + [HBM],
        unit * 8,
        4 << 20,
        scratch=[pltpu.VMEM((fresh, width), BF16), pltpu.VMEM(w_out.shape, BF16), pltpu.SemaphoreType.DMA],
    )(index, arrived, gate_two, here, there, spectra, f, i, in_hbm(w_out))
    mixed = call(
        total_kernel, jax.ShapeDtypeStruct((rows, width), BF16), [VMEM], 1 << 16, 1 << 17
    )(exchanged(partial, "chan"))
    return (mixed, gated)


def solution(mesh):
    placed = (
        P("ctx", "chan"),
        P(),
        P(None, None, "chan"),
        P("chan", None),
        P("ctx", None, "chan"),
        P("ctx", None, "chan"),
        P(None, None, "chan"),
    )
    return jax.shard_map(
        layer,
        mesh=mesh,
        in_specs=placed,
        out_specs=(P("ctx", "chan"), P("ctx", "chan")),
        check_vma=False,
    )
```

time: 71.6 us -> 77.5 us (1.082); the launches traced: 71.2 us -> 76.3 us
  blocking collectives: 38.3 us -> 11.2 us
  starting transfers between devices: 12.7 us -> 29.4 us
  waiting for transfers between devices: 5.55 us -> 19.3 us
  Pallas kernels: 12.6 us -> 14.2 us
    all_to_all x3 -> x1, blocking collectives: 38.3 us -> 11.2 us  [exchanged(): return lax.all_to_all(array, axis, split_axis=0, concat_axis=0, tiled=True)]
    ppermute x1 -> x5, waiting for transfers between devices: 0.01 us -> 12.2 us  [the longest x4 6.82 us: swapped(): lax.ppermute(array, axis, [(i, i ^ step) for i in range(lax.axis_size(axi...]
    all_to_all x1 -> x2, starting transfers between devices: 7.59 us -> 17.1 us  [exchanged(): return lax.all_to_all(array, axis, split_axis=0, concat_axis=0, tiled=True)]
    ppermute x1 -> x5, starting transfers between devices: 5.11 us -> 12.3 us  [the longest x4 7.16 us: swapped(): lax.ppermute(array, axis, [(i, i ^ step) for i in range(lax.axis_size(axi...]
    all_to_all x1 -> x2, waiting for transfers between devices: 5.55 us -> 7.12 us  [exchanged(): return lax.all_to_all(array, axis, split_axis=0, concat_axis=0, tiled=True)]
    pallas_call x5, Pallas kernels: 12.6 us -> 14.2 us  [the longest x1 5.49 us: layer(): call(project_kernel, (jax.ShapeDtypeStruct((ctx_count, 3 * rows, width),...]
  transfers between devices with their start and end apart: 2 -> 7, of which waited for: 1 -> 3; matrix products, arithmetic and copies ran while one was open for 2% -> 2% of each run, Pallas kernels for 5% -> 8%
where the time goes in v3:
time: 77.5 us; the launch traced here: 76.3 us
  starting transfers between devices  29.4 us (38%)
  waiting for transfers between devices  19.3 us (25%)
  Pallas kernels  14.2 us (18%)
  blocking collectives  11.2 us (14%)
  local copies, waits for them, and re-layouts  1.34 us (2%)
    all_to_all x2, starting transfers between devices, exchanged(): return lax.all_to_all(array, axis, split_axis=0, concat_axis=0, tiled=True)  17.1 us
    all_to_all x1, blocking collectives, exchanged(): return lax.all_to_all(array, axis, split_axis=0, concat_axis=0, tiled=True)  11.2 us
    ppermute x4, starting transfers between devices, swapped(): lax.ppermute(array, axis, [(i, i ^ step) for i in range(lax.axis_size(axi...  7.16 us
    all_to_all x2, waiting for transfers between devices, exchanged(): return lax.all_to_all(array, axis, split_axis=0, concat_axis=0, tiled=True)  7.12 us
    ppermute x4, waiting for transfers between devices, swapped(): lax.ppermute(array, axis, [(i, i ^ step) for i in range(lax.axis_size(axi...  6.82 us
    pallas_call x1, Pallas kernels, layer(): call(project_kernel, (jax.ShapeDtypeStruct((ctx_count, 3 * rows, width),...  5.49 us
    ppermute x1, waiting for transfers between devices, layer(): lax.ppermute(filt_far, 'ctx', [(i, i - 1) for i in range(1, ctx_count)])  5.34 us
    ppermute x1, starting transfers between devices, layer(): lax.ppermute(filt_far, 'ctx', [(i, i - 1) for i in range(1, ctx_count)])  5.11 us
  transfers between devices with their start and end apart: 7, of which 3 were waited for; matrix products, arithmetic and copies ran while one was open for 2% of the time, Pallas kernels for 8%

profile of v3, /device:TPU:1, one launch (start us, length us, event | category | flops | bytes accessed | tf_op | source)
XLA Modules:
  0.0 76.3 jit_solution(18345976928959447824)
XLA Ops:
  0.6 5.1 %collective-permute-start = (bf16[256,2,256]{2,1,0:T(2,128)(2,1)}, bf16[256,2,256]{2,1,0:T(2,128)(2,1)S(1)}, u32[]{:S(2)}, u32[]{:S(2)}) collective-permute-start(bf16[256,2,256]{2,1,0:T(2,128)(2,1)} %own_hbm.1), channel_id=1, source_target_pairs={{16,0},{32,16},{48,32},{64,48},{80,64},{96,80},{112,96},{128,112},... | collective-permute-start | bytes 786440 | tf_op jit(solution)/shard_map/ppermute | solution.py:179
  5.8 5.3 %collective-permute-done.border = bf16[256,2,256]{2,1,0:T(2,128)(2,1)S(1)} collective-permute-done((bf16[256,2,256]{2,1,0:T(2,128)(2,1)}, bf16[256,2,256]{2,1,0:T(2,128)(2,1)S(1)}, u32[]{:S(2)}, u32[]{:S(2)}) %collective-permute-start) | collective-permute-done | bytes 262176 | tf_op jit(solution)/shard_map/ppermute | solution.py:179
  11.1 3.6 %shard_map.104 = (bf16[256,256]{1,0:T(8,128)(2,1)S(1)}, bf16[256,2,256]{2,1,0:T(2,128)(2,1)S(1)}, bf16[256,2,256]{2,1,0:T(2,128)(2,1)S(1)}, bf16[256,2,256]{2,1,...) custom-call(s32[1]{0:T(128)S(6)} %convert_element_type.30.last, ...), custom_call_target="tpu_custom_call" | custom-call | flops 603979776 | bytes 2097152 | tf_op jit(solution)/shard_map/pallas_call | solution.py:185
  14.7 0.1 collective-permute-start.1
  14.8 1.3 %broadcast_in_dim.3 = bf16[16,16,256]{2,1,0:T(8,128)(2,1)} broadcast(bf16[16,256]{1,0:T(8,128)(2,1)} %param.9), dimensions={1,2} | broadcast | bytes 139264 | tf_op jit(solution)/shard_map/broadcast_in_dim | solution.py:180
  16.1 9.1 %all-to-all-start = ((bf16[16,16,256]{2,1,0:T(8,128)(2,1)}), bf16[16,16,256]{2,1,0:T(8,128)(2,1)S(1)}, u32[]{:S(2)}, u32[]{:S(2)}) async-start(bf16[16,16,256]{2,1,0:T(8,128)(2,1)} %broadcast_in_dim.3), calls=%async_computation | async-start | bytes 262144 | tf_op jit(solution)/shard_map/all_to_all | solution.py:158
  25.2 0.0 collective-permute-done.1
  25.2 1.3 %collective-permute-start.2 = (bf16[256,256]{1,0:T(8,128)(2,1)S(1)}, bf16[256,256]{1,0:T(8,128)(2,1)S(1)}, u32[]{:S(2)}, u32[]{:S(2)}) collective-permute-start(bf16[256,256]{1,0:T(8,128)(2,1)S(1)} %add_convert_fusion.2), channel_id=1, source_target_pairs={{0,64},{16,80},{32,96},{48,112},{64,0},{80,16},{96,32},{112,48},{1... | collective-permute-start | bytes 393224 | tf_op jit(solution)/shard_map/ppermute | solution.py:162
  26.5 7.1 %all-to-all-done.gathered = bf16[16,16,256]{2,1,0:T(8,128)(2,1)S(1)} async-done(((bf16[16,16,256]{2,1,0:T(8,128)(2,1)}), bf16[16,16,256]{2,1,0:T(8,128)(2,1)S(1)}, u32[]{:S(2)}, u32[]{:S(2)}) %all-to-all-start) | async-done | bytes 131104 | tf_op jit(solution)/shard_map/all_to_all | solution.py:158
  33.7 5.5 %shard_map.105 = (bf16[16,48,256]{2,1,0:T(8,128)(2,1)}, bf16[16,256]{1,0:T(8,128)(2,1)S(1)}) custom-call(s32[1]{0:T(128)S(6)} %convert_element_type.30.last, bf16[16,16,256]{2,1,0:T(8,128)(2,1)S(1)} %all-to-all-done.gathered, f32[32,128]{1,0:T(8,128)S(1)} %get-tuple-element.15.gain, bf16[3,4096,256]{2,1,0:T(8,128)(2,1)} %bitcast.3, ...), custom_call_target="tpu_custom_call" | custom-call | flops 704643072 | bytes 6291456 | tf_op jit(solution)/shard_map/pallas_call | solution.py:205
  39.2 0.0 collective-permute-done.2
  39.2 2.8 %collective-permute-start.3 = (bf16[256,256]{1,0:T(8,128)(2,1)S(1)}, bf16[256,256]{1,0:T(8,128)(2,1)S(1)}, u32[]{:S(2)}, u32[]{:S(2)}) collective-permute-start(bf16[256,256]{1,0:T(8,128)(2,1)S(1)} %add_convert_fusion.1), channel_id=1, source_target_pairs={{0,128},{16,144},{32,160},{48,176},{64,192},{80,208},{96,224},{112... | collective-permute-start | bytes 393224 | tf_op jit(solution)/shard_map/ppermute | solution.py:162
  42.0 8.0 %all-to-all-start.1 = ((bf16[16,48,256]{2,1,0:T(8,128)(2,1)}), bf16[16,48,256]{2,1,0:T(8,128)(2,1)S(1)}, u32[]{:S(2)}, u32[]{:S(2)}) async-start(bf16[16,48,256]{2,1,0:T(8,128)(2,1)} %get-tuple-element.23), calls=%async_computation.1 | async-start | bytes 786432 | tf_op jit(solution)/shard_map/all_to_all | solution.py:158
  50.1 0.0 collective-permute-done.3
  50.1 2.9 %collective-permute-start.4 = (bf16[256,256]{1,0:T(8,128)(2,1)S(1)}, bf16[256,256]{1,0:T(8,128)(2,1)S(1)}, u32[]{:S(2)}, u32[]{:S(2)}) collective-permute-start(bf16[256,256]{1,0:T(8,128)(2,1)S(1)} %add_convert_fusion.sum_here), channel_id=1, source_target_pairs={{0,32},{16,48},{32,0},{48,16},{64,96},{80,112},{96,64},{112,80},{1... | collective-permute-start | bytes 393224 | tf_op jit(solution)/shard_map/ppermute | solution.py:162
  53.1 0.9 %shard_map.106.spectra = f32[2,512,256]{2,1,0:T(8,128)S(1)} custom-call(bf16[256,2,256]{2,1,0:T(2,128)(2,1)S(1)} %get-tuple-element.17.near, bf16[2,512,256]{2,1,0:T(8,128)(2,1)S(1)} %get-tuple-element.19.f), custom_call_target="tpu_custom_call" | custom-call | flops 268435456 | bytes 2097152 | tf_op jit(solution)/shard_map/pallas_call | solution.py:223
  54.0 6.8 %collective-permute-done.4.sum_there = bf16[256,256]{1,0:T(8,128)(2,1)S(1)} collective-permute-done((bf16[256,256]{1,0:T(8,128)(2,1)S(1)}, bf16[256,256]{1,0:T(8,128)(2,1)S(1)}, u32[]{:S(2)}, u32[]{:S(2)}) %collective-permute-start.4) | collective-permute-done | bytes 131104 | tf_op jit(solution)/shard_map/ppermute | solution.py:162
  60.8 0.0 all-to-all-done.1.arrived
  60.8 3.6 %shard_map.107 = (bf16[16,16,256]{2,1,0:T(8,128)(2,1)S(1)}, bf16[16,256]{1,0:T(8,128)(2,1)}) custom-call(s32[1]{0:T(128)} %bitcast.index, bf16[16,48,256]{2,1,0:T(8,128)(2,1)S(1)} %all-to-all-done.1.arrived, bf16[16,256]{1,0:T(8,128)(2,1)S(1)} %get-tuple-element.24.gate_two, bf16[256,256]{1,0:T(8,128)(2,1)S(1)} %add_convert_fusion.sum_here, ...), custom_call_target="tpu_custom_call" | custom-call | flops 536870912 | bytes 4194304 | tf_op jit(solution)/shard_map/pallas_call | solution.py:227
  64.4 11.2 %all_to_all.15.arrived = bf16[16,16,256]{2,1,0:T(8,128)(2,1)S(1)} all-to-all(bf16[16,16,256]{2,1,0:T(8,128)(2,1)S(1)} %get-tuple-element.26), channel_id=1, replica_groups=mesh['ctx'=16,'chan'=16] {'chan'}, dimensions={0} | all-to-all | bytes 262144 | tf_op jit(solution)/shard_map/all_to_all | solution.py:158
  75.6 0.6 shard_map.108
  (3 shorter events, 0.1 us)
Async XLA Ops:
  0.6 10.5 %collective-permute-start = (bf16[256,2,256]{2,1,0:T(2,128)(2,1)}, bf16[256,2,256]{2,1,0:T(2,128)(2,1)S(1)}, u32[]{:S(2)}, u32[]{:S(2)}) collective-permute-start(bf16[256,2,256]{2,1,0:T(2,128)(2,1)} %own_hbm.1), channel_id=1, source_target_pairs={{16,0},{32,16},{48,32},{64,48},{80,64},{96,80},{112,96},{128,112},... | collective-permute-start | bytes 786440 | tf_op jit(solution)/shard_map/ppermute | solution.py:179
  14.7 10.5 %collective-permute-start.1 = (bf16[256,256]{1,0:T(8,128)(2,1)S(1)}, bf16[256,256]{1,0:T(8,128)(2,1)S(1)}, u32[]{:S(2)}, u32[]{:S(2)}) collective-permute-start(bf16[256,256]{1,0:T(8,128)(2,1)S(1)} %get-tuple-element.22), channel_id=1, source_target_pairs={{0,16},{16,0},{32,48},{48,32},{64,80},{80,64},{96,112},{112,96},{1... | collective-permute-start | bytes 393224 | tf_op jit(solution)/shard_map/ppermute | solution.py:162
  16.1 17.5 %all-to-all-start = ((bf16[16,16,256]{2,1,0:T(8,128)(2,1)}), bf16[16,16,256]{2,1,0:T(8,128)(2,1)S(1)}, u32[]{:S(2)}, u32[]{:S(2)}) async-start(bf16[16,16,256]{2,1,0:T(8,128)(2,1)} %broadcast_in_dim.3), calls=%async_computation | async-start | bytes 262144 | tf_op jit(solution)/shard_map/all_to_all | solution.py:158
  25.2 13.9 %collective-permute-start.2 = (bf16[256,256]{1,0:T(8,128)(2,1)S(1)}, bf16[256,256]{1,0:T(8,128)(2,1)S(1)}, u32[]{:S(2)}, u32[]{:S(2)}) collective-permute-start(bf16[256,256]{1,0:T(8,128)(2,1)S(1)} %add_convert_fusion.2), channel_id=1, source_target_pairs={{0,64},{16,80},{32,96},{48,112},{64,0},{80,16},{96,32},{112,48},{1... | collective-permute-start | bytes 393224 | tf_op jit(solution)/shard_map/ppermute | solution.py:162
  39.2 10.9 %collective-permute-start.3 = (bf16[256,256]{1,0:T(8,128)(2,1)S(1)}, bf16[256,256]{1,0:T(8,128)(2,1)S(1)}, u32[]{:S(2)}, u32[]{:S(2)}) collective-permute-start(bf16[256,256]{1,0:T(8,128)(2,1)S(1)} %add_convert_fusion.1), channel_id=1, source_target_pairs={{0,128},{16,144},{32,160},{48,176},{64,192},{80,208},{96,224},{112... | collective-permute-start | bytes 393224 | tf_op jit(solution)/shard_map/ppermute | solution.py:162
  42.0 18.8 %all-to-all-start.1 = ((bf16[16,48,256]{2,1,0:T(8,128)(2,1)}), bf16[16,48,256]{2,1,0:T(8,128)(2,1)S(1)}, u32[]{:S(2)}, u32[]{:S(2)}) async-start(bf16[16,48,256]{2,1,0:T(8,128)(2,1)} %get-tuple-element.23), calls=%async_computation.1 | async-start | bytes 786432 | tf_op jit(solution)/shard_map/all_to_all | solution.py:158
  50.1 10.7 %collective-permute-start.4 = (bf16[256,256]{1,0:T(8,128)(2,1)S(1)}, bf16[256,256]{1,0:T(8,128)(2,1)S(1)}, u32[]{:S(2)}, u32[]{:S(2)}) collective-permute-start(bf16[256,256]{1,0:T(8,128)(2,1)S(1)} %add_convert_fusion.sum_here), channel_id=1, source_target_pairs={{0,32},{16,48},{32,0},{48,16},{64,96},{80,112},{96,64},{112,80},{1... | collective-permute-start | bytes 393224 | tf_op jit(solution)/shard_map/ppermute | solution.py:162

commit v4 on v3

--- a/solution.py
+++ b/solution.py
@@ -51,30 +51,61 @@
     return jnp.concatenate([wc * sc + ws * ss, wc * ss - ws * sc], 0)
 
 
-def past_part(which, last, own, border, near, history, f, i):
+def spread_out(rows, spread):
+    count, kinds, width = rows.shape
+    flat = rows[...].reshape(count * kinds, width)
+    lanes = spread.shape[2]
+    for h in range(width // lanes):
+        spread[h] = flat[:, h * lanes : (h + 1) * lanes].astype(F32)
+
+
+def parted(spread, kinds, which):
+    count = spread.shape[1] // kinds
+    rows = [spread[h, pl.ds(which, count, stride=kinds), :].astype(BF16) for h in range(spread.shape[0])]
+    return jnp.concatenate(rows, 1)
+
+
+def past_part(own, after, history, f, i):
     half = f.shape[1] // 2
     quarter = half // 2
-    first = spectrum(f, own[:, which, :])
-    second = spectrum(f, jnp.where(last[0] > 0, near[:, which, :], border[:, which, :]))
+    first, second = spectrum(f, own), spectrum(f, after)
     bc, bs = second[:half], second[half:]
     window = first + jnp.concatenate([-bs[:quarter], bs[quarter:], bc[:quarter], -bc[quarter:]], 0)
-    return back_to_time(i[0], i[1], times_conjugate(window, spectrum(f, history[:, which, :]))).astype(BF16)
+    return back_to_time(i[0], i[1], times_conjugate(window, spectrum(f, history)))
 
 
 def past_kernel(
-    last, border, own_hbm, near_hbm, history_hbm, f_hbm, i_hbm, gain_hbm,
-    part_one, own, near, history, f, i, gain, sems,
+    index, last, border, own_hbm, near_hbm, history_hbm, f_hbm, i_hbm, gain_hbm,
+    keep, send, later, near, f, i, gain,
+    own, history, part, spread, sems,
 ):
-    pairs = [(own_hbm, own), (f_hbm, f), (near_hbm, near), (history_hbm, history), (i_hbm, i), (gain_hbm, gain)]
+    pairs = [(own_hbm, own), (near_hbm, near), (history_hbm, history), (f_hbm, f), (i_hbm, i), (gain_hbm, gain)]
     copies = [pltpu.make_async_copy(a, b, sems.at[n]) for n, (a, b) in enumerate(pairs)]
     for copy in copies:
         copy.start()
     for copy in copies:
         copy.wait()
-    part_one[...] = past_part(0, last, own, border, near, history, f, i)
-
-
-def project_kernel(last, gathered, gain, w_hbm, own, border, near, history, f, i, out, gate_two, w, sems):
+
+    @pl.when(last[0] > 0)
+    def _():
+        spread_out(near, spread.at[1])
+
+    @pl.when(last[0] == 0)
+    def _():
+        spread_out(border, spread.at[1])
+
+    spread_out(own, spread.at[0])
+    spread_out(history, spread.at[2])
+    for n in range(3):
+        later[n] = parted(spread.at[n], 2, 1)
+    part[...] = past_part(*(parted(spread.at[n], 2, 0) for n in range(3)), f, i)
+    half = keep.shape[0]
+    mine = index[0] % 2
+    keep[...] = part[pl.ds(pl.multiple_of(mine * half, half), half), :]
+    send[...] = part[pl.ds(pl.multiple_of((1 - mine) * half, half), half), :]
+
+
+def project_kernel(gathered, gain, w_hbm, later, f, i, out, gate_two, w, sems):
     pieces, rows, width = gathered.shape
     steps = sems.shape[0]
     per = pieces // steps
@@ -83,7 +114,7 @@
         span = pl.ds(q * per * width, per * width)
         copies.append(pltpu.make_async_copy(w_hbm.at[:, span, :], w.at[:, span, :], sems.at[q]))
         copies[-1].start()
-    part_two = past_part(1, last, own, border, near, history, f, i)
+    part_two = past_part(later[0], later[1], later[2], f, i).astype(BF16)
     out[:, 2 * rows :] = part_two.reshape(out.shape[0], rows, width)
     total = jnp.zeros((rows, width), F32)
     for s in range(pieces):
@@ -105,13 +136,15 @@
         out[d, : 2 * rows] = shared
 
 
-def near_kernel(near, f, spectra):
+def near_kernel(near, f, spectra, spread):
+    spread_out(near, spread)
     for which in range(2):
-        spectra[which] = spectrum(f, near[:, which, :])
+        spectra[which] = spectrum(f, parted(spread, 2, which))
 
 
 def mix_kernel(
-    index, arrived, gate_two, sum_here, sum_there, spectra, f, i, w_hbm, partial, gated_own, gated_all, w_out, sem
+    index, arrived, gate_two, here, there, spectra, f, i, w_hbm,
+    partial, gated_own, past_one, gated_all, w_out, sem,
 ):
     load = pltpu.make_async_copy(w_hbm, w_out, sem)
     load.start()
@@ -120,9 +153,12 @@
     fresh = count * rows
     values = arrived[:, :rows].reshape(fresh, width)
     gate_one = arrived[:, rows : 2 * rows].reshape(fresh, width).astype(F32)
-    past_one = sum_here[...].astype(F32) + sum_there[...].astype(F32)
+    half = here.shape[0]
+    mine = index[0] % 2
+    past_one[pl.ds(pl.multiple_of(mine * half, half), half), :] = here[...]
+    past_one[pl.ds(pl.multiple_of((1 - mine) * half, half), half), :] = there[...]
     first = back_to_time(i[0], i[1], times_conjugate(spectra[0], spectrum(f, values)))
-    gated = (gate_one * (past_one + first)).astype(BF16)
+    gated = (gate_one * (past_one[...].astype(F32) + first)).astype(BF16)
     gated_all[...] = gated
     own = pl.ds(pl.multiple_of(index[0] * rows, rows), rows)
     gated_own[...] = gated_all[own, :]
@@ -182,25 +218,30 @@
     unit = fresh * fresh * 4 * width
     w_three = w_in.transpose(1, 0, 2)
     scales = gain.reshape(-1, 128)
-    part_one, own, near, history, f, i, scales = call(
+    half = jax.ShapeDtypeStruct((fresh // 2, width), F32)
+    spread = (width // 128, 2 * fresh, 128)
+    keep, send, later, near, f, i, scales = call(
         past_kernel,
         (
-            jax.ShapeDtypeStruct((fresh, width), BF16),
-            *(
-                jax.ShapeDtypeStruct(a.shape, a.dtype)
-                for a in (filt_far, filt_near, history, forward, inverse, scales)
-            ),
+            half,
+            half,
+            jax.ShapeDtypeStruct((3, fresh, width), BF16),
+            *(jax.ShapeDtypeStruct(a.shape, a.dtype) for a in (filt_near, forward, inverse, scales)),
         ),
-        [SMEM, VMEM] + [HBM] * 6,
+        [SMEM, SMEM, VMEM] + [HBM] * 6,
         unit * 9,
         2 << 20,
-        scratch=[pltpu.SemaphoreType.DMA((6,))],
-    )(last, border, *(in_hbm(a) for a in (filt_far, filt_near, history, forward, inverse, scales)))
-
-    here = part_one
-    there = swapped(here, "ctx", 1)
-    here = added(here, there)
-    there = swapped(here, "ctx", 4)
+        scratch=[
+            pltpu.VMEM(filt_far.shape, BF16),
+            pltpu.VMEM(history.shape, BF16),
+            pltpu.VMEM((fresh, width), F32),
+            pltpu.VMEM((3, *spread), F32),
+            pltpu.SemaphoreType.DMA((6,)),
+        ],
+    )(index, last, border, *(in_hbm(a) for a in (filt_far, filt_near, history, forward, inverse, scales)))
+
+    here = added(keep, swapped(send, "ctx", 1))
+    there = swapped(here, "ctx", 2)
 
     payload, gate_two = call(
         project_kernel,
@@ -208,20 +249,26 @@
             jax.ShapeDtypeStruct((ctx_count, 3 * rows, width), BF16),
             jax.ShapeDtypeStruct((rows, width), BF16),
         ),
-        [SMEM, VMEM, VMEM, HBM] + [VMEM] * 6,
+        [VMEM, VMEM, HBM] + [VMEM] * 3,
         2 * rows * w_in.size + unit * 9,
         2 * w_in.size,
         scratch=[pltpu.VMEM(w_three.shape, BF16), pltpu.SemaphoreType.DMA((8,))],
-    )(last, gathered, scales, in_hbm(w_three), own, border, near, history, f, i)
+    )(gathered, scales, in_hbm(w_three), later, f, i)
 
     here = added(here, there)
     payload, here = lax.optimization_barrier((payload, here))
     there = swapped(here, "ctx", 8)
     arrived = exchanged(payload, "ctx")
     here = added(here, there)
-    there = swapped(here, "ctx", 2)
+    here = added(here, swapped(here, "ctx", 4))
+    there = swapped(here, "ctx", 1)
     spectra = call(
-        near_kernel, jax.ShapeDtypeStruct((2, 2 * fresh, width), F32), [VMEM] * 2, unit * 4, 2 << 20
+        near_kernel,
+        jax.ShapeDtypeStruct((2, 2 * fresh, width), F32),
+        [VMEM] * 2,
+        unit * 4,
+        2 << 20,
+        scratch=[pltpu.VMEM(spread, F32)],
     )(near, f)
 
     partial, gated = call(
@@ -233,7 +280,8 @@
         [SMEM] + [VMEM] * 7 + [HBM],
         unit * 8,
         4 << 20,
-        scratch=[pltpu.VMEM((fresh, width), BF16), pltpu.VMEM(w_out.shape, BF16), pltpu.SemaphoreType.DMA],
+        scratch=[pltpu.VMEM((fresh, width), BF16)] * 2
+        + [pltpu.VMEM(w_out.shape, BF16), pltpu.SemaphoreType.DMA],
     )(index, arrived, gate_two, here, there, spectra, f, i, in_hbm(w_out))
     mixed = call(
         total_kernel, jax.ShapeDtypeStruct((rows, width), BF16), [VMEM], 1 << 16, 1 << 17

time: 77.5 us -> 75.3 us (0.972); the launches traced: 76.3 us -> 74.9 us
  waiting for transfers between devices: 19.3 us -> 17.1 us
  starting transfers between devices: 29.4 us -> 31.2 us
  Pallas kernels: 14.2 us -> 13.1 us
    all_to_all x2, waiting for transfers between devices: 7.12 us -> 5.15 us  [exchanged(): return lax.all_to_all(array, axis, split_axis=0, concat_axis=0, tiled=True)]
    ppermute x4 -> x5, starting transfers between devices: 7.16 us -> 9.03 us  [swapped(): lax.ppermute(array, axis, [(i, i ^ step) for i in range(lax.axis_size(axi...]
    ppermute x4 -> x5, waiting for transfers between devices: 6.82 us -> 6.62 us  [swapped(): lax.ppermute(array, axis, [(i, i ^ step) for i in range(lax.axis_size(axi...]
  transfers between devices with their start and end apart: 7 -> 8, of which waited for: 3 -> 5; matrix products, arithmetic and copies ran while one was open for 2% -> 2% of each run, Pallas kernels for 8% -> 7%
where the time goes in v4:
time: 75.3 us; the launch traced here: 74.9 us
  starting transfers between devices  31.2 us (41%)
  waiting for transfers between devices  17.1 us (23%)
  Pallas kernels  13.1 us (17%)
  blocking collectives  11.2 us (15%)
  local copies, waits for them, and re-layouts  1.36 us (2%)
    all_to_all x2, starting transfers between devices, exchanged(): return lax.all_to_all(array, axis, split_axis=0, concat_axis=0, tiled=True)  17.1 us
    all_to_all x1, blocking collectives, exchanged(): return lax.all_to_all(array, axis, split_axis=0, concat_axis=0, tiled=True)  11.2 us
    ppermute x5, starting transfers between devices, swapped(): lax.ppermute(array, axis, [(i, i ^ step) for i in range(lax.axis_size(axi...  9.03 us
    ppermute x5, waiting for transfers between devices, swapped(): lax.ppermute(array, axis, [(i, i ^ step) for i in range(lax.axis_size(axi...  6.62 us
    ppermute x1, waiting for transfers between devices, layer(): lax.ppermute(filt_far, 'ctx', [(i, i - 1) for i in range(1, ctx_count)])  5.34 us
    all_to_all x2, waiting for transfers between devices, exchanged(): return lax.all_to_all(array, axis, split_axis=0, concat_axis=0, tiled=True)  5.15 us
    ppermute x1, starting transfers between devices, layer(): lax.ppermute(filt_far, 'ctx', [(i, i - 1) for i in range(1, ctx_count)])  5.11 us
    pallas_call x1, Pallas kernels, layer(): call(project_kernel, (jax.ShapeDtypeStruct((ctx_count, 3 * rows, width),...  4.85 us
  transfers between devices with their start and end apart: 8, of which 5 were waited for; matrix products, arithmetic and copies ran while one was open for 2% of the time, Pallas kernels for 7%

profile of v4, /device:TPU:1, one launch (start us, length us, event | category | flops | bytes accessed | tf_op | source)
XLA Modules:
  0.0 74.9 jit_solution(7852229606804522321)
XLA Ops:
  0.6 5.1 %collective-permute-start = (bf16[256,2,256]{2,1,0:T(2,128)(2,1)}, bf16[256,2,256]{2,1,0:T(2,128)(2,1)S(1)}, u32[]{:S(2)}, u32[]{:S(2)}) collective-permute-start(bf16[256,2,256]{2,1,0:T(2,128)(2,1)} %own_hbm.1), channel_id=1, source_target_pairs={{16,0},{32,16},{48,32},{64,48},{80,64},{96,80},{112,96},{128,112},... | collective-permute-start | bytes 786440 | tf_op jit(solution)/shard_map/ppermute | solution.py:215
  5.8 5.3 %collective-permute-done.border = bf16[256,2,256]{2,1,0:T(2,128)(2,1)S(1)} collective-permute-done((bf16[256,2,256]{2,1,0:T(2,128)(2,1)}, bf16[256,2,256]{2,1,0:T(2,128)(2,1)S(1)}, u32[]{:S(2)}, u32[]{:S(2)}) %collective-permute-start) | collective-permute-done | bytes 262176 | tf_op jit(solution)/shard_map/ppermute | solution.py:215
  11.1 3.4 %shard_map.104 = (f32[128,256]{1,0:T(8,128)S(1)}, f32[128,256]{1,0:T(8,128)S(1)}, bf16[3,256,256]{2,1,0:T(8,128)(2,1)S(1)}, bf16[256,2,256]{2,1,0:T(2,128)(2,1)S...) custom-call(s32[1]{0:T(128)} %bitcast.index, ...), custom_call_target="tpu_custom_call" | custom-call | flops 603979776 | bytes 2097152 | tf_op jit(solution)/shard_map/pallas_call | solution.py:223
  14.5 0.1 collective-permute-start.1
  14.6 1.4 %broadcast_in_dim.3 = bf16[16,16,256]{2,1,0:T(8,128)(2,1)} broadcast(bf16[16,256]{1,0:T(8,128)(2,1)} %param.9), dimensions={1,2} | broadcast | bytes 139264 | tf_op jit(solution)/shard_map/broadcast_in_dim | solution.py:216
  16.0 9.1 %all-to-all-start = ((bf16[16,16,256]{2,1,0:T(8,128)(2,1)}), bf16[16,16,256]{2,1,0:T(8,128)(2,1)S(1)}, u32[]{:S(2)}, u32[]{:S(2)}) async-start(bf16[16,16,256]{2,1,0:T(8,128)(2,1)} %broadcast_in_dim.3), calls=%async_computation | async-start | bytes 262144 | tf_op jit(solution)/shard_map/all_to_all | solution.py:194
  25.1 0.0 collective-permute-done.1
  25.1 3.6 %collective-permute-start.2 = (bf16[128,256]{1,0:T(8,128)(2,1)S(1)}, bf16[128,256]{1,0:T(8,128)(2,1)S(1)}, u32[]{:S(2)}, u32[]{:S(2)}) collective-permute-start(bf16[128,256]{1,0:T(8,128)(2,1)S(1)} %add_convert_fusion.3), channel_id=1, source_target_pairs={{0,32},{16,48},{32,0},{48,16},{64,96},{80,112},{96,64},{112,80},{1... | collective-permute-start | bytes 196616 | tf_op jit(solution)/shard_map/ppermute | solution.py:198
  28.7 4.8 %all-to-all-done.gathered = bf16[16,16,256]{2,1,0:T(8,128)(2,1)S(1)} async-done(((bf16[16,16,256]{2,1,0:T(8,128)(2,1)}), bf16[16,16,256]{2,1,0:T(8,128)(2,1)S(1)}, u32[]{:S(2)}, u32[]{:S(2)}) %all-to-all-start) | async-done | bytes 131104 | tf_op jit(solution)/shard_map/all_to_all | solution.py:194
  33.5 4.8 %shard_map.105 = (bf16[16,48,256]{2,1,0:T(8,128)(2,1)}, bf16[16,256]{1,0:T(8,128)(2,1)S(1)}) custom-call(bf16[16,16,256]{2,1,0:T(8,128)(2,1)S(1)} %all-to-all-done.gathered, f32[32,128]{1,0:T(8,128)S(1)} %get-tuple-element.15.gain, bf16[3,4096,256]{2,1,0:T(8,128)(2,1)} %bitcast.3, bf16[3,256,256]{2,1,0:T(8,128)(2,1)S(1)} %get-tuple-element.16.later, ...), custom_call_target="tpu_custom_call" | custom-call | flops 704643072 | bytes 6291456 | tf_op jit(solution)/shard_map/pallas_call | solution.py:246
  38.4 0.0 collective-permute-done.2
  38.4 2.8 %collective-permute-start.3 = (bf16[128,256]{1,0:T(8,128)(2,1)S(1)}, bf16[128,256]{1,0:T(8,128)(2,1)S(1)}, u32[]{:S(2)}, u32[]{:S(2)}) collective-permute-start(bf16[128,256]{1,0:T(8,128)(2,1)S(1)} %add_convert_fusion.2), channel_id=1, source_target_pairs={{0,128},{16,144},{32,160},{48,176},{64,192},{80,208},{96,224},{112... | collective-permute-start | bytes 196616 | tf_op jit(solution)/shard_map/ppermute | solution.py:198
  41.2 8.0 %all-to-all-start.1 = ((bf16[16,48,256]{2,1,0:T(8,128)(2,1)}), bf16[16,48,256]{2,1,0:T(8,128)(2,1)S(1)}, u32[]{:S(2)}, u32[]{:S(2)}) async-start(bf16[16,48,256]{2,1,0:T(8,128)(2,1)} %get-tuple-element.22), calls=%async_computation.1 | async-start | bytes 786432 | tf_op jit(solution)/shard_map/all_to_all | solution.py:194
  49.3 0.0 collective-permute-done.3
  49.3 1.4 %collective-permute-start.4 = (bf16[128,256]{1,0:T(8,128)(2,1)S(1)}, bf16[128,256]{1,0:T(8,128)(2,1)S(1)}, u32[]{:S(2)}, u32[]{:S(2)}) collective-permute-start(bf16[128,256]{1,0:T(8,128)(2,1)S(1)} %add_convert_fusion.1), channel_id=1, source_target_pairs={{0,64},{16,80},{32,96},{48,112},{64,0},{80,16},{96,32},{112,48},{1... | collective-permute-start | bytes 196616 | tf_op jit(solution)/shard_map/ppermute | solution.py:198
  50.8 6.4 %collective-permute-done.4 = bf16[128,256]{1,0:T(8,128)(2,1)S(1)} collective-permute-done((bf16[128,256]{1,0:T(8,128)(2,1)S(1)}, bf16[128,256]{1,0:T(8,128)(2,1)S(1)}, u32[]{:S(2)}, u32[]{:S(2)}) %collective-permute-start.4) | collective-permute-done | bytes 65568 | tf_op jit(solution)/shard_map/ppermute | solution.py:198
  57.1 1.1 %collective-permute-start.5 = (bf16[128,256]{1,0:T(8,128)(2,1)S(1)}, bf16[128,256]{1,0:T(8,128)(2,1)S(1)}, u32[]{:S(2)}, u32[]{:S(2)}) collective-permute-start(bf16[128,256]{1,0:T(8,128)(2,1)S(1)} %add_convert_fusion.here), channel_id=1, source_target_pairs={{0,16},{16,0},{32,48},{48,32},{64,80},{80,64},{96,112},{112,96},{1... | collective-permute-start | bytes 196616 | tf_op jit(solution)/shard_map/ppermute | solution.py:198
  58.2 0.7 shard_map.106.spectra
  58.9 0.2 collective-permute-done.5.there
  59.1 0.3 all-to-all-done.1.arrived
  59.4 3.6 %shard_map.107 = (bf16[16,16,256]{2,1,0:T(8,128)(2,1)S(1)}, bf16[16,256]{1,0:T(8,128)(2,1)}) custom-call(s32[1]{0:T(128)} %bitcast.index, bf16[16,48,256]{2,1,0:T(8,128)(2,1)S(1)} %all-to-all-done.1.arrived, bf16[16,256]{1,0:T(8,128)(2,1)S(1)} %get-tuple-element.23.gate_two, bf16[128,256]{1,0:T(8,128)(2,1)S(1)} %add_convert_fusion.here, ...), custom_call_target="tpu_custom_call" | custom-call | flops 536870912 | bytes 4194304 | tf_op jit(solution)/shard_map/pallas_call | solution.py:274
  63.0 11.2 %all_to_all.15.arrived = bf16[16,16,256]{2,1,0:T(8,128)(2,1)S(1)} all-to-all(bf16[16,16,256]{2,1,0:T(8,128)(2,1)S(1)} %get-tuple-element.26), channel_id=1, replica_groups=mesh['ctx'=16,'chan'=16] {'chan'}, dimensions={0} | all-to-all | bytes 262144 | tf_op jit(solution)/shard_map/all_to_all | solution.py:194
  74.2 0.6 shard_map.108
  (4 shorter events, 0.1 us)
Async XLA Ops:
  0.6 10.5 %collective-permute-start = (bf16[256,2,256]{2,1,0:T(2,128)(2,1)}, bf16[256,2,256]{2,1,0:T(2,128)(2,1)S(1)}, u32[]{:S(2)}, u32[]{:S(2)}) collective-permute-start(bf16[256,2,256]{2,1,0:T(2,128)(2,1)} %own_hbm.1), channel_id=1, source_target_pairs={{16,0},{32,16},{48,32},{64,48},{80,64},{96,80},{112,96},{128,112},... | collective-permute-start | bytes 786440 | tf_op jit(solution)/shard_map/ppermute | solution.py:215
  14.5 10.5 %collective-permute-start.1 = (f32[128,256]{1,0:T(8,128)S(1)}, f32[128,256]{1,0:T(8,128)S(1)}, u32[]{:S(2)}, u32[]{:S(2)}) collective-permute-start(f32[128,256]{1,0:T(8,128)S(1)} %get-tuple-element.21), channel_id=1, source_target_pairs={{0,16},{16,0},{32,48},{48,32},{64,80},{80,64},{96,112},{112,96},{1... | collective-permute-start | bytes 393224 | tf_op jit(solution)/shard_map/ppermute | solution.py:198
  16.0 17.5 %all-to-all-start = ((bf16[16,16,256]{2,1,0:T(8,128)(2,1)}), bf16[16,16,256]{2,1,0:T(8,128)(2,1)S(1)}, u32[]{:S(2)}, u32[]{:S(2)}) async-start(bf16[16,16,256]{2,1,0:T(8,128)(2,1)} %broadcast_in_dim.3), calls=%async_computation | async-start | bytes 262144 | tf_op jit(solution)/shard_map/all_to_all | solution.py:194
  25.1 13.3 %collective-permute-start.2 = (bf16[128,256]{1,0:T(8,128)(2,1)S(1)}, bf16[128,256]{1,0:T(8,128)(2,1)S(1)}, u32[]{:S(2)}, u32[]{:S(2)}) collective-permute-start(bf16[128,256]{1,0:T(8,128)(2,1)S(1)} %add_convert_fusion.3), channel_id=1, source_target_pairs={{0,32},{16,48},{32,0},{48,16},{64,96},{80,112},{96,64},{112,80},{1... | collective-permute-start | bytes 196616 | tf_op jit(solution)/shard_map/ppermute | solution.py:198
  38.4 10.9 %collective-permute-start.3 = (bf16[128,256]{1,0:T(8,128)(2,1)S(1)}, bf16[128,256]{1,0:T(8,128)(2,1)S(1)}, u32[]{:S(2)}, u32[]{:S(2)}) collective-permute-start(bf16[128,256]{1,0:T(8,128)(2,1)S(1)} %add_convert_fusion.2), channel_id=1, source_target_pairs={{0,128},{16,144},{32,160},{48,176},{64,192},{80,208},{96,224},{112... | collective-permute-start | bytes 196616 | tf_op jit(solution)/shard_map/ppermute | solution.py:198
  41.2 18.2 %all-to-all-start.1 = ((bf16[16,48,256]{2,1,0:T(8,128)(2,1)}), bf16[16,48,256]{2,1,0:T(8,128)(2,1)S(1)}, u32[]{:S(2)}, u32[]{:S(2)}) async-start(bf16[16,48,256]{2,1,0:T(8,128)(2,1)} %get-tuple-element.22), calls=%async_computation.1 | async-start | bytes 786432 | tf_op jit(solution)/shard_map/all_to_all | solution.py:194
  49.3 7.8 %collective-permute-start.4 = (bf16[128,256]{1,0:T(8,128)(2,1)S(1)}, bf16[128,256]{1,0:T(8,128)(2,1)S(1)}, u32[]{:S(2)}, u32[]{:S(2)}) collective-permute-start(bf16[128,256]{1,0:T(8,128)(2,1)S(1)} %add_convert_fusion.1), channel_id=1, source_target_pairs={{0,64},{16,80},{32,96},{48,112},{64,0},{80,16},{96,32},{112,48},{1... | collective-permute-start | bytes 196616 | tf_op jit(solution)/shard_map/ppermute | solution.py:198
  57.1 2.0 %collective-permute-start.5 = (bf16[128,256]{1,0:T(8,128)(2,1)S(1)}, bf16[128,256]{1,0:T(8,128)(2,1)S(1)}, u32[]{:S(2)}, u32[]{:S(2)}) collective-permute-start(bf16[128,256]{1,0:T(8,128)(2,1)S(1)} %add_convert_fusion.here), channel_id=1, source_target_pairs={{0,16},{16,0},{32,48},{48,32},{64,80},{80,64},{96,112},{112,96},{1... | collective-permute-start | bytes 196616 | tf_op jit(solution)/shard_map/ppermute | solution.py:198

commit v5 on v4

--- a/solution.py
+++ b/solution.py
@@ -76,8 +76,8 @@
 
 def past_kernel(
     index, last, border, own_hbm, near_hbm, history_hbm, f_hbm, i_hbm, gain_hbm,
-    keep, send, later, near, f, i, gain,
-    own, history, part, spread, sems,
+    keep, send, near, f, i, gain,
+    own, history, parts, spread, sems,
 ):
     pairs = [(own_hbm, own), (near_hbm, near), (history_hbm, history), (f_hbm, f), (i_hbm, i), (gain_hbm, gain)]
     copies = [pltpu.make_async_copy(a, b, sems.at[n]) for n, (a, b) in enumerate(pairs)]
@@ -96,16 +96,25 @@
 
     spread_out(own, spread.at[0])
     spread_out(history, spread.at[2])
-    for n in range(3):
-        later[n] = parted(spread.at[n], 2, 1)
-    part[...] = past_part(*(parted(spread.at[n], 2, 0) for n in range(3)), f, i)
-    half = keep.shape[0]
     mine = index[0] % 2
-    keep[...] = part[pl.ds(pl.multiple_of(mine * half, half), half), :]
-    send[...] = part[pl.ds(pl.multiple_of((1 - mine) * half, half), half), :]
-
-
-def project_kernel(gathered, gain, w_hbm, later, f, i, out, gate_two, w, sems):
+    fresh, lanes = keep.shape[0] // 2, keep.shape[1]
+    for which in range(2):
+        part = past_part(*(parted(spread.at[n], 2, which) for n in range(3)), f, i)
+        if which == 0:
+            low, high = part[:, :lanes], part[:, lanes:]
+            keep[:fresh] = jnp.where(mine == 0, low, high)
+            send[:fresh] = jnp.where(mine == 0, high, low)
+        else:
+            parts[...] = part.reshape(parts.shape)
+            rows = (fresh // 2, lanes)
+            for h in range(2):
+                there = pl.ds(fresh + h * rows[0], rows[0])
+                span = slice(h * lanes, (h + 1) * lanes)
+                keep[there] = parts[:, mine, :, span].reshape(rows)
+                send[there] = parts[:, 1 - mine, :, span].reshape(rows)
+
+
+def project_kernel(gathered, gain, w_hbm, keep, came, out, gate_two, w, sems):
     pieces, rows, width = gathered.shape
     steps = sems.shape[0]
     per = pieces // steps
@@ -114,8 +123,12 @@
         span = pl.ds(q * per * width, per * width)
         copies.append(pltpu.make_async_copy(w_hbm.at[:, span, :], w.at[:, span, :], sems.at[q]))
         copies[-1].start()
-    part_two = past_part(later[0], later[1], later[2], f, i).astype(BF16)
-    out[:, 2 * rows :] = part_two.reshape(out.shape[0], rows, width)
+    lanes = out.shape[2]
+    fresh = keep.shape[0] // 2
+    pair = (keep[fresh:] + came[fresh:]).astype(BF16)
+    for d in range(out.shape[0]):
+        start = (d % 2) * (fresh // 2) + (d // 2) * rows
+        out[d, 2 * rows :] = pair[start : start + rows]
     total = jnp.zeros((rows, width), F32)
     for s in range(pieces):
         x = gathered[s].astype(F32)
@@ -133,39 +146,49 @@
     gate_two[...] = sums[2].astype(BF16)
     shared = jnp.concatenate([sums[0].astype(BF16), sums[1].astype(BF16)], 0)
     for d in range(out.shape[0]):
-        out[d, : 2 * rows] = shared
-
-
-def near_kernel(near, f, spectra, spread):
-    spread_out(near, spread)
+        out[d, : 2 * rows] = shared[:, (d % 2) * lanes : (d % 2 + 1) * lanes]
+
+
+def near_kernel(index, near, f, spectra, spread):
+    lanes = spectra.shape[2]
+    half = pl.ds(pl.multiple_of((index[0] % 2) * lanes, lanes), lanes)
+    spread_out(near.at[:, :, half], spread)
     for which in range(2):
         spectra[which] = spectrum(f, parted(spread, 2, which))
 
 
-def mix_kernel(
-    index, arrived, gate_two, here, there, spectra, f, i, w_hbm,
-    partial, gated_own, past_one, gated_all, w_out, sem,
-):
+def mix_kernel(index, arrived, here, there, spectra, f, i, w_hbm, keep, send, w_out, gated_all, sums, sem):
     load = pltpu.make_async_copy(w_hbm, w_out, sem)
     load.start()
-    count, packed, width = arrived.shape
+    count, packed, lanes = arrived.shape
     rows = packed // 3
     fresh = count * rows
-    values = arrived[:, :rows].reshape(fresh, width)
-    gate_one = arrived[:, rows : 2 * rows].reshape(fresh, width).astype(F32)
-    half = here.shape[0]
+    values = arrived[:, :rows].reshape(fresh, lanes)
+    gate_one = arrived[:, rows : 2 * rows].reshape(fresh, lanes).astype(F32)
+    past_one = here[...].astype(F32) + there[...].astype(F32)
+    first = back_to_time(i[0], i[1], times_conjugate(spectra[0], spectrum(f, values)))
+    gated = (gate_one * (past_one + first)).astype(BF16)
+    gated_all[...] = gated
     mine = index[0] % 2
-    past_one[pl.ds(pl.multiple_of(mine * half, half), half), :] = here[...]
-    past_one[pl.ds(pl.multiple_of((1 - mine) * half, half), half), :] = there[...]
-    first = back_to_time(i[0], i[1], times_conjugate(spectra[0], spectrum(f, values)))
-    gated = (gate_one * (past_one[...].astype(F32) + first)).astype(BF16)
-    gated_all[...] = gated
-    own = pl.ds(pl.multiple_of(index[0] * rows, rows), rows)
-    gated_own[...] = gated_all[own, :]
-    second = back_to_time(i[0, own, :], i[1, own, :], times_conjugate(spectra[1], spectrum(f, gated)))
-    past_two = jnp.sum(arrived[:, 2 * rows :].astype(F32), axis=0)
-    mixed_in = (gate_two[...].astype(F32) * (past_two + second)).astype(BF16)
+    chip = pl.ds(pl.multiple_of((index[0] - mine) * rows, 2 * rows), 2 * rows)
+    second = back_to_time(i[0, chip, :], i[1, chip, :], times_conjugate(spectra[1], spectrum(f, gated)))
+    past_two = [arrived[p, 2 * rows :].astype(F32) for p in range(2)]
+    for s in range(2, count):
+        past_two[s % 2] += arrived[s, 2 * rows :].astype(F32)
+    sums[0] = (second + jnp.concatenate(past_two, 0)).reshape(sums.shape[1:])
+    sums[1] = gated_all[chip, :].astype(F32).reshape(sums.shape[1:])
+    keep[...] = sums[:, mine]
+    send[...] = sums[:, 1 - mine]
     load.wait()
+
+
+def finish_kernel(index, keep, came, gate_two, w_out, partial, gated):
+    first = index[0] % 2 == 0
+    low, high = jnp.where(first, keep[...], came[...]), jnp.where(first, came[...], keep[...])
+    both = jnp.concatenate([low, high], 2)
+    gated[...] = both[1].astype(BF16)
+    mixed_in = (gate_two[...].astype(F32) * both[0]).astype(BF16)
+    width = partial.shape[2]
     for d in range(partial.shape[0]):
         partial[d] = dot(mixed_in, w_out[:, d * width : (d + 1) * width]).astype(BF16)
 
@@ -218,71 +241,83 @@
     unit = fresh * fresh * 4 * width
     w_three = w_in.transpose(1, 0, 2)
     scales = gain.reshape(-1, 128)
-    half = jax.ShapeDtypeStruct((fresh // 2, width), F32)
-    spread = (width // 128, 2 * fresh, 128)
-    keep, send, later, near, f, i, scales = call(
+    lanes = width // 2
+    half = jax.ShapeDtypeStruct((2 * fresh, lanes), F32)
+    spread = (2 * fresh, lanes)
+    keep, send, near, f, i, scales = call(
         past_kernel,
         (
             half,
             half,
-            jax.ShapeDtypeStruct((3, fresh, width), BF16),
             *(jax.ShapeDtypeStruct(a.shape, a.dtype) for a in (filt_near, forward, inverse, scales)),
         ),
         [SMEM, SMEM, VMEM] + [HBM] * 6,
-        unit * 9,
+        unit * 18,
         2 << 20,
         scratch=[
             pltpu.VMEM(filt_far.shape, BF16),
             pltpu.VMEM(history.shape, BF16),
-            pltpu.VMEM((fresh, width), F32),
-            pltpu.VMEM((3, *spread), F32),
+            pltpu.VMEM((ctx_count // 2, 2, rows, width), F32),
+            pltpu.VMEM((3, 2, *spread), F32),
             pltpu.SemaphoreType.DMA((6,)),
         ],
     )(index, last, border, *(in_hbm(a) for a in (filt_far, filt_near, history, forward, inverse, scales)))
 
-    here = added(keep, swapped(send, "ctx", 1))
+    came = swapped(send, "ctx", 1)
+    here = added(keep[:fresh], came[:fresh])
     there = swapped(here, "ctx", 2)
 
     payload, gate_two = call(
         project_kernel,
         (
-            jax.ShapeDtypeStruct((ctx_count, 3 * rows, width), BF16),
+            jax.ShapeDtypeStruct((ctx_count, 3 * rows, lanes), BF16),
             jax.ShapeDtypeStruct((rows, width), BF16),
         ),
-        [VMEM, VMEM, HBM] + [VMEM] * 3,
-        2 * rows * w_in.size + unit * 9,
+        [VMEM, VMEM, HBM, VMEM, VMEM],
+        2 * rows * w_in.size,
         2 * w_in.size,
         scratch=[pltpu.VMEM(w_three.shape, BF16), pltpu.SemaphoreType.DMA((8,))],
-    )(gathered, scales, in_hbm(w_three), later, f, i)
+    )(gathered, scales, in_hbm(w_three), keep, came)
 
     here = added(here, there)
     payload, here = lax.optimization_barrier((payload, here))
     there = swapped(here, "ctx", 8)
     arrived = exchanged(payload, "ctx")
     here = added(here, there)
-    here = added(here, swapped(here, "ctx", 4))
-    there = swapped(here, "ctx", 1)
+    there = swapped(here, "ctx", 4)
     spectra = call(
         near_kernel,
-        jax.ShapeDtypeStruct((2, 2 * fresh, width), F32),
-        [VMEM] * 2,
+        jax.ShapeDtypeStruct((2, 2 * fresh, lanes), F32),
+        [SMEM, VMEM, VMEM],
+        unit * 2,
+        2 << 20,
+        scratch=[pltpu.VMEM((1, *spread), F32)],
+    )(index, near, f)
+
+    block = jax.ShapeDtypeStruct((2, rows, lanes), F32)
+    keep, send, w_out = call(
+        mix_kernel,
+        (block, block, jax.ShapeDtypeStruct(w_out.shape, BF16)),
+        [SMEM] + [VMEM] * 6 + [HBM],
         unit * 4,
-        2 << 20,
-        scratch=[pltpu.VMEM(spread, F32)],
-    )(near, f)
-
+        4 << 20,
+        scratch=[
+            pltpu.VMEM((fresh, lanes), BF16),
+            pltpu.VMEM((2, 2, rows, lanes), F32),
+            pltpu.SemaphoreType.DMA,
+        ],
+    )(index, arrived, here, there, spectra, f, i, in_hbm(w_out))
+    came = swapped(send, "ctx", 1)
     partial, gated = call(
-        mix_kernel,
+        finish_kernel,
         (
             jax.ShapeDtypeStruct((chan_count, rows, width), BF16),
             jax.ShapeDtypeStruct((rows, width), BF16),
         ),
-        [SMEM] + [VMEM] * 7 + [HBM],
-        unit * 8,
-        4 << 20,
-        scratch=[pltpu.VMEM((fresh, width), BF16)] * 2
-        + [pltpu.VMEM(w_out.shape, BF16), pltpu.SemaphoreType.DMA],
-    )(index, arrived, gate_two, here, there, spectra, f, i, in_hbm(w_out))
+        [SMEM] + [VMEM] * 4,
+        unit,
+        1 << 20,
+    )(index, keep, came, gate_two, w_out)
     mixed = call(
         total_kernel, jax.ShapeDtypeStruct((rows, width), BF16), [VMEM], 1 << 16, 1 << 17
     )(exchanged(partial, "chan"))

time: 75.3 us -> 74.1 us (0.984)
  starting transfers between devices: 31.2 us -> 30.4 us
    all_to_all x2, waiting for transfers between devices: 5.15 us -> 7.66 us  [exchanged(): return lax.all_to_all(array, axis, split_axis=0, concat_axis=0, tiled=True)]
    ppermute x5, waiting for transfers between devices: 6.62 us -> 4.85 us  [swapped(): lax.ppermute(array, axis, [(i, i ^ step) for i in range(lax.axis_size(axi...]
    ppermute x5, starting transfers between devices: 9.03 us -> 8.14 us  [swapped(): lax.ppermute(array, axis, [(i, i ^ step) for i in range(lax.axis_size(axi...]
    pallas_call x4 -> x5, Pallas kernels: 12.5 us -> 11.9 us  [the longest x1 4.25 us: layer(): call(past_kernel, (half, half, *(jax.ShapeDtypeStruct(a.shape, a.dtype) f...]
  transfers between devices with their start and end apart: 8 -> 8, of which waited for: 5 -> 5; matrix products, arithmetic and copies ran while one was open for 2% -> 1% of each run, Pallas kernels for 7% -> 6%
where the time goes in v5:
time: 74.1 us; the launch traced here: 73.7 us
  starting transfers between devices  30.4 us (41%)
  waiting for transfers between devices  17.8 us (24%)
  Pallas kernels  12.5 us (17%)
  blocking collectives  11.5 us (16%)
  between operations  0.75 us (1%)
    all_to_all x2, starting transfers between devices, exchanged(): return lax.all_to_all(array, axis, split_axis=0, concat_axis=0, tiled=True)  17.1 us
    all_to_all x1, blocking collectives, exchanged(): return lax.all_to_all(array, axis, split_axis=0, concat_axis=0, tiled=True)  11.5 us
    ppermute x5, starting transfers between devices, swapped(): lax.ppermute(array, axis, [(i, i ^ step) for i in range(lax.axis_size(axi...  8.14 us
    all_to_all x2, waiting for transfers between devices, exchanged(): return lax.all_to_all(array, axis, split_axis=0, concat_axis=0, tiled=True)  7.66 us
    ppermute x1, waiting for transfers between devices, layer(): lax.ppermute(filt_far, 'ctx', [(i, i - 1) for i in range(1, ctx_count)])  5.34 us
    ppermute x1, starting transfers between devices, layer(): lax.ppermute(filt_far, 'ctx', [(i, i - 1) for i in range(1, ctx_count)])  5.11 us
    ppermute x5, waiting for transfers between devices, swapped(): lax.ppermute(array, axis, [(i, i ^ step) for i in range(lax.axis_size(axi...  4.85 us
    pallas_call x1, Pallas kernels, layer(): call(past_kernel, (half, half, *(jax.ShapeDtypeStruct(a.shape, a.dtype) f...  4.25 us
  transfers between devices with their start and end apart: 8, of which 5 were waited for; matrix products, arithmetic and copies ran while one was open for 1% of the time, Pallas kernels for 6%

profile of v5, /device:TPU:1, one launch (start us, length us, event | category | flops | bytes accessed | tf_op | source)
XLA Modules:
  0.0 73.7 jit_solution(911623026618450805)
XLA Ops:
  0.6 5.1 %collective-permute-start = (bf16[256,2,256]{2,1,0:T(2,128)(2,1)}, bf16[256,2,256]{2,1,0:T(2,128)(2,1)S(1)}, u32[]{:S(2)}, u32[]{:S(2)}) collective-permute-start(bf16[256,2,256]{2,1,0:T(2,128)(2,1)} %own_hbm.1), channel_id=1, source_target_pairs={{16,0},{32,16},{48,32},{64,48},{80,64},{96,80},{112,96},{128,112},... | collective-permute-start | bytes 786440 | tf_op jit(solution)/shard_map/ppermute | solution.py:238
  5.8 5.3 %collective-permute-done.border = bf16[256,2,256]{2,1,0:T(2,128)(2,1)S(1)} collective-permute-done((bf16[256,2,256]{2,1,0:T(2,128)(2,1)}, bf16[256,2,256]{2,1,0:T(2,128)(2,1)S(1)}, u32[]{:S(2)}, u32[]{:S(2)}) %collective-permute-start) | collective-permute-done | bytes 262176 | tf_op jit(solution)/shard_map/ppermute | solution.py:238
  11.1 0.0 copy-start
  11.1 4.3 %shard_map.104 = (f32[512,128]{1,0:T(8,128)S(1)}, f32[512,128]{1,0:T(8,128)S(1)}, bf16[256,2,256]{2,1,0:T(2,128)(2,1)S(1)}, bf16[2,512,256]{2,1,0:T(8,128)(2,1)S...) custom-call(s32[1]{0:T(128)} %bitcast.index, s32[1]{0:T(128)S(6)} %convert_element_type.24.last, ...), custom_call_target="tpu_custom_call" | custom-call | flops 1207959552 | bytes 2097152 | tf_op jit(solution)/shard_map/pallas_call | solution.py:247
  15.4 0.1 collective-permute-start.1
  15.5 0.0 copy-done
  15.5 0.7 broadcast_in_dim.3
  16.1 9.1 %all-to-all-start = ((bf16[16,16,256]{2,1,0:T(8,128)(2,1)}), bf16[16,16,256]{2,1,0:T(8,128)(2,1)S(1)}, u32[]{:S(2)}, u32[]{:S(2)}) async-start(bf16[16,16,256]{2,1,0:T(8,128)(2,1)} %broadcast_in_dim.3), calls=%async_computation | async-start | bytes 262144 | tf_op jit(solution)/shard_map/all_to_all | solution.py:217
  25.2 0.0 collective-permute-done.1.came
  25.2 3.6 %collective-permute-start.2 = (bf16[256,128]{1,0:T(8,128)(2,1)S(1)}, bf16[256,128]{1,0:T(8,128)(2,1)S(1)}, u32[]{:S(2)}, u32[]{:S(2)}) collective-permute-start(bf16[256,128]{1,0:T(8,128)(2,1)S(1)} %fusion), channel_id=1, source_target_pairs={{0,32},{16,48},{32,0},{48,16},{64,96},{80,112},{96,64},{112,80},{1... | collective-permute-start | bytes 196616 | tf_op jit(solution)/shard_map/ppermute | solution.py:221
  28.8 4.8 %all-to-all-done.gathered = bf16[16,16,256]{2,1,0:T(8,128)(2,1)S(1)} async-done(((bf16[16,16,256]{2,1,0:T(8,128)(2,1)}), bf16[16,16,256]{2,1,0:T(8,128)(2,1)S(1)}, u32[]{:S(2)}, u32[]{:S(2)}) %all-to-all-start) | async-done | bytes 131104 | tf_op jit(solution)/shard_map/all_to_all | solution.py:217
  33.7 3.8 %shard_map.105 = (bf16[16,48,128]{2,1,0:T(8,128)(2,1)}, bf16[16,256]{1,0:T(8,128)(2,1)S(1)}) custom-call(bf16[16,16,256]{2,1,0:T(8,128)(2,1)S(1)} %all-to-all-done.gathered, f32[32,128]{1,0:T(8,128)S(1)} %get-tuple-element.17.gain, bf16[3,4096,256]{2,1,0:T(8,128)(2,1)} %bitcast.3, f32[512,128]{1,0:T(8,128)S(1)} %get-tuple-element.18.keep, ...), custom_call_target="tpu_custom_call" | custom-call | flops 100663296 | bytes 6291456 | tf_op jit(solution)/shard_map/pallas_call | solution.py:270
  37.5 0.0 collective-permute-done.2
  37.5 2.8 %collective-permute-start.3 = (bf16[256,128]{1,0:T(8,128)(2,1)S(1)}, bf16[256,128]{1,0:T(8,128)(2,1)S(1)}, u32[]{:S(2)}, u32[]{:S(2)}) collective-permute-start(bf16[256,128]{1,0:T(8,128)(2,1)S(1)} %add_convert_fusion.1), channel_id=1, source_target_pairs={{0,128},{16,144},{32,160},{48,176},{64,192},{80,208},{96,224},{112... | collective-permute-start | bytes 196616 | tf_op jit(solution)/shard_map/ppermute | solution.py:221
  40.3 8.0 %all-to-all-start.1 = ((bf16[16,48,128]{2,1,0:T(8,128)(2,1)}), bf16[16,48,128]{2,1,0:T(8,128)(2,1)S(1)}, u32[]{:S(2)}, u32[]{:S(2)}) async-start(bf16[16,48,128]{2,1,0:T(8,128)(2,1)} %get-tuple-element.21), calls=%async_computation.1 | async-start | bytes 393216 | tf_op jit(solution)/shard_map/all_to_all | solution.py:217
  48.4 0.0 collective-permute-done.3
  48.4 1.4 %collective-permute-start.4 = (bf16[256,128]{1,0:T(8,128)(2,1)S(1)}, bf16[256,128]{1,0:T(8,128)(2,1)S(1)}, u32[]{:S(2)}, u32[]{:S(2)}) collective-permute-start(bf16[256,128]{1,0:T(8,128)(2,1)S(1)} %add_convert_fusion.here), channel_id=1, source_target_pairs={{0,64},{16,80},{32,96},{48,112},{64,0},{80,16},{96,32},{112,48},{1... | collective-permute-start | bytes 196616 | tf_op jit(solution)/shard_map/ppermute | solution.py:221
  49.8 0.5 shard_map.106.spectra
  50.4 3.7 %collective-permute-done.4.there = bf16[256,128]{1,0:T(8,128)(2,1)S(1)} collective-permute-done((bf16[256,128]{1,0:T(8,128)(2,1)S(1)}, bf16[256,128]{1,0:T(8,128)(2,1)S(1)}, u32[]{:S(2)}, u32[]{:S(2)}) %collective-permute-start.4) | collective-permute-done | bytes 65568 | tf_op jit(solution)/shard_map/ppermute | solution.py:221
  54.1 2.8 %all-to-all-done.1.arrived = bf16[16,48,128]{2,1,0:T(8,128)(2,1)S(1)} async-done(((bf16[16,48,128]{2,1,0:T(8,128)(2,1)}), bf16[16,48,128]{2,1,0:T(8,128)(2,1)S(1)}, u32[]{:S(2)}, u32[]{:S(2)}) %all-to-all-start.1) | async-done | bytes 196640 | tf_op jit(solution)/shard_map/all_to_all | solution.py:217
  56.9 2.5 %shard_map.107 = (f32[2,16,128]{2,1,0:T(8,128)S(1)}, f32[2,16,128]{2,1,0:T(8,128)S(1)}, bf16[256,4096]{1,0:T(8,128)(2,1)S(1)}) custom-call(s32[1]{0:T(128)} %bitcast.index, bf16[16,48,128]{2,1,0:T(8,128)(2,1)S(1)} %all-to-all-done.1.arrived, bf16[256,128]{1,0:T(8,128)(2,1)S(1)} %add_convert_fusion.here, bf16[256,128]{1,0:T(8,128)(2,1)S(1)} %collective-permute-done.4.there, ...), custom_call_target="tpu_custom_call" | custom-call | flops 268435456 | bytes 4194304 | tf_op jit(solution)/shard_map/pallas_call | solution.py:298
  59.4 0.2 collective-permute-start.5
  59.6 1.1 %collective-permute-done.5.came = f32[2,16,128]{2,1,0:T(8,128)S(1)} collective-permute-done((f32[2,16,128]{2,1,0:T(8,128)S(1)}, f32[2,16,128]{2,1,0:T(8,128)S(1)}, u32[]{:S(2)}, u32[]{:S(2)}) %collective-permute-start.5) | collective-permute-done | bytes 16416 | tf_op jit(solution)/shard_map/ppermute | solution.py:221
  60.7 0.9 %shard_map.108 = (bf16[16,16,256]{2,1,0:T(8,128)(2,1)S(1)}, bf16[16,256]{1,0:T(8,128)(2,1)}) custom-call(s32[1]{0:T(128)} %bitcast.index, f32[2,16,128]{2,1,0:T(8,128)S(1)} %get-tuple-element.26.keep, f32[2,16,128]{2,1,0:T(8,128)S(1)} %collective-permute-done.5.came, bf16[16,256]{1,0:T(8,128)(2,1)S(1)} %get-tuple-element.28.gate_two, ...), custom_call_target="tpu_custom_call" | custom-call | flops 67108864 | bytes 1048576 | tf_op jit(solution)/shard_map/pallas_call | solution.py:311
  61.6 11.5 %all_to_all.15.arrived = bf16[16,16,256]{2,1,0:T(8,128)(2,1)S(1)} all-to-all(bf16[16,16,256]{2,1,0:T(8,128)(2,1)S(1)} %get-tuple-element.30), channel_id=1, replica_groups=mesh['ctx'=16,'chan'=16] {'chan'}, dimensions={0} | all-to-all | bytes 262144 | tf_op jit(solution)/shard_map/all_to_all | solution.py:217
  73.1 0.6 shard_map.109
  (3 shorter events, 0.1 us)
Async XLA Ops:
  0.6 10.5 %collective-permute-start = (bf16[256,2,256]{2,1,0:T(2,128)(2,1)}, bf16[256,2,256]{2,1,0:T(2,128)(2,1)S(1)}, u32[]{:S(2)}, u32[]{:S(2)}) collective-permute-start(bf16[256,2,256]{2,1,0:T(2,128)(2,1)} %own_hbm.1), channel_id=1, source_target_pairs={{16,0},{32,16},{48,32},{64,48},{80,64},{96,80},{112,96},{128,112},... | collective-permute-start | bytes 786440 | tf_op jit(solution)/shard_map/ppermute | solution.py:238
  11.1 4.4 %copy-start = (bf16[16,256]{1,0:T(8,128)(2,1)S(1)}, bf16[16,256]{1,0:T(8,128)(2,1)}, u32[]{:S(2)}) copy-start(bf16[16,256]{1,0:T(8,128)(2,1)} %param.9) | copy-start | bytes 24580
  15.4 9.8 %collective-permute-start.1 = (f32[512,128]{1,0:T(8,128)S(1)}, f32[512,128]{1,0:T(8,128)S(1)}, u32[]{:S(2)}, u32[]{:S(2)}) collective-permute-start(f32[512,128]{1,0:T(8,128)S(1)} %get-tuple-element.19), channel_id=1, source_target_pairs={{0,16},{16,0},{32,48},{48,32},{64,80},{80,64},{96,112},{112,96},{1... | collective-permute-start | bytes 786440 | tf_op jit(solution)/shard_map/ppermute | solution.py:221
  16.1 17.5 %all-to-all-start = ((bf16[16,16,256]{2,1,0:T(8,128)(2,1)}), bf16[16,16,256]{2,1,0:T(8,128)(2,1)S(1)}, u32[]{:S(2)}, u32[]{:S(2)}) async-start(bf16[16,16,256]{2,1,0:T(8,128)(2,1)} %broadcast_in_dim.3), calls=%async_computation | async-start | bytes 262144 | tf_op jit(solution)/shard_map/all_to_all | solution.py:217
  25.2 12.2 %collective-permute-start.2 = (bf16[256,128]{1,0:T(8,128)(2,1)S(1)}, bf16[256,128]{1,0:T(8,128)(2,1)S(1)}, u32[]{:S(2)}, u32[]{:S(2)}) collective-permute-start(bf16[256,128]{1,0:T(8,128)(2,1)S(1)} %fusion), channel_id=1, source_target_pairs={{0,32},{16,48},{32,0},{48,16},{64,96},{80,112},{96,64},{112,80},{1... | collective-permute-start | bytes 196616 | tf_op jit(solution)/shard_map/ppermute | solution.py:221
  37.5 10.9 %collective-permute-start.3 = (bf16[256,128]{1,0:T(8,128)(2,1)S(1)}, bf16[256,128]{1,0:T(8,128)(2,1)S(1)}, u32[]{:S(2)}, u32[]{:S(2)}) collective-permute-start(bf16[256,128]{1,0:T(8,128)(2,1)S(1)} %add_convert_fusion.1), channel_id=1, source_target_pairs={{0,128},{16,144},{32,160},{48,176},{64,192},{80,208},{96,224},{112... | collective-permute-start | bytes 196616 | tf_op jit(solution)/shard_map/ppermute | solution.py:221
  40.3 16.6 %all-to-all-start.1 = ((bf16[16,48,128]{2,1,0:T(8,128)(2,1)}), bf16[16,48,128]{2,1,0:T(8,128)(2,1)S(1)}, u32[]{:S(2)}, u32[]{:S(2)}) async-start(bf16[16,48,128]{2,1,0:T(8,128)(2,1)} %get-tuple-element.21), calls=%async_computation.1 | async-start | bytes 393216 | tf_op jit(solution)/shard_map/all_to_all | solution.py:217
  48.4 5.7 %collective-permute-start.4 = (bf16[256,128]{1,0:T(8,128)(2,1)S(1)}, bf16[256,128]{1,0:T(8,128)(2,1)S(1)}, u32[]{:S(2)}, u32[]{:S(2)}) collective-permute-start(bf16[256,128]{1,0:T(8,128)(2,1)S(1)} %add_convert_fusion.here), channel_id=1, source_target_pairs={{0,64},{16,80},{32,96},{48,112},{64,0},{80,16},{96,32},{112,48},{1... | collective-permute-start | bytes 196616 | tf_op jit(solution)/shard_map/ppermute | solution.py:221
  59.4 1.3 %collective-permute-start.5 = (f32[2,16,128]{2,1,0:T(8,128)S(1)}, f32[2,16,128]{2,1,0:T(8,128)S(1)}, u32[]{:S(2)}, u32[]{:S(2)}) collective-permute-start(f32[2,16,128]{2,1,0:T(8,128)S(1)} %get-tuple-element.27), channel_id=1, source_target_pairs={{0,16},{16,0},{32,48},{48,32},{64,80},{80,64},{96,112},{112,96},{1... | collective-permute-start | bytes 49160 | tf_op jit(solution)/shard_map/ppermute | solution.py:221

commit v6 on v5

--- a/solution.py
+++ b/solution.py
@@ -74,18 +74,21 @@
     return back_to_time(i[0], i[1], times_conjugate(window, spectrum(f, history)))
 
 
-def past_kernel(
-    index, last, border, own_hbm, near_hbm, history_hbm, f_hbm, i_hbm, gain_hbm,
-    keep, send, near, f, i, gain,
-    own, history, parts, spread, sems,
-):
-    pairs = [(own_hbm, own), (near_hbm, near), (history_hbm, history), (f_hbm, f), (i_hbm, i), (gain_hbm, gain)]
-    copies = [pltpu.make_async_copy(a, b, sems.at[n]) for n, (a, b) in enumerate(pairs)]
-    for copy in copies:
-        copy.start()
-    for copy in copies:
-        copy.wait()
-
+def open_kernel(*refs):
+    (inputs, *loads), (copies, *kept), (held, sems) = refs[:7], refs[7:14], refs[14:]
+    moves = [pltpu.make_async_copy(a, b, sems.at[n]) for n, (a, b) in enumerate(zip([inputs, *loads], [held, *kept]))]
+    for move in moves:
+        move.start()
+    moves[0].wait()
+    count = copies.shape[0]
+    sent = [pltpu.make_async_copy(held, copies.at[d], sems.at[len(moves) + d]) for d in range(count)]
+    for move in sent:
+        move.start()
+    for move in moves[1:] + sent:
+        move.wait()
+
+
+def second_past_kernel(index, last, border, own, near, history, f, i, keep, send, later, parts, spread):
     @pl.when(last[0] > 0)
     def _():
         spread_out(near, spread.at[1])
@@ -97,21 +100,25 @@
     spread_out(own, spread.at[0])
     spread_out(history, spread.at[2])
     mine = index[0] % 2
-    fresh, lanes = keep.shape[0] // 2, keep.shape[1]
-    for which in range(2):
-        part = past_part(*(parted(spread.at[n], 2, which) for n in range(3)), f, i)
-        if which == 0:
-            low, high = part[:, :lanes], part[:, lanes:]
-            keep[:fresh] = jnp.where(mine == 0, low, high)
-            send[:fresh] = jnp.where(mine == 0, high, low)
-        else:
-            parts[...] = part.reshape(parts.shape)
-            rows = (fresh // 2, lanes)
-            for h in range(2):
-                there = pl.ds(fresh + h * rows[0], rows[0])
-                span = slice(h * lanes, (h + 1) * lanes)
-                keep[there] = parts[:, mine, :, span].reshape(rows)
-                send[there] = parts[:, 1 - mine, :, span].reshape(rows)
+    part = past_part(*(parted(spread.at[n], 2, 1) for n in range(3)), f, i)
+    parts[...] = part.reshape(parts.shape)
+    half, lanes = keep.shape[0] // 2, keep.shape[1]
+    for h in range(2):
+        there = pl.ds(h * half, half)
+        span = slice(h * lanes, (h + 1) * lanes)
+        keep[there] = parts[:, mine, :, span].reshape(half, lanes)
+        send[there] = parts[:, 1 - mine, :, span].reshape(half, lanes)
+    for n in range(3):
+        later[n] = parted(spread.at[n], 2, 0)
+
+
+def first_past_kernel(index, rows, f, i, keep, send):
+    part = past_part(rows[0], rows[1], rows[2], f, i)
+    lanes = keep.shape[1]
+    low, high = part[:, :lanes], part[:, lanes:]
+    mine = index[0] % 2
+    keep[...] = jnp.where(mine == 0, low, high)
+    send[...] = jnp.where(mine == 0, high, low)
 
 
 def project_kernel(gathered, gain, w_hbm, keep, came, out, gate_two, w, sems):
@@ -124,8 +131,8 @@
         copies.append(pltpu.make_async_copy(w_hbm.at[:, span, :], w.at[:, span, :], sems.at[q]))
         copies[-1].start()
     lanes = out.shape[2]
-    fresh = keep.shape[0] // 2
-    pair = (keep[fresh:] + came[fresh:]).astype(BF16)
+    fresh = keep.shape[0]
+    pair = (keep[...] + came[...]).astype(BF16)
     for d in range(out.shape[0]):
         start = (d % 2) * (fresh // 2) + (d // 2) * rows
         out[d, 2 * rows :] = pair[start : start + rows]
@@ -157,7 +164,7 @@
         spectra[which] = spectrum(f, parted(spread, 2, which))
 
 
-def mix_kernel(index, arrived, here, there, spectra, f, i, w_hbm, keep, send, w_out, gated_all, sums, sem):
+def mix_kernel(index, arrived, here, one, two, three, spectra, f, i, w_hbm, keep, send, w_out, gated_all, sums, sem):
     load = pltpu.make_async_copy(w_hbm, w_out, sem)
     load.start()
     count, packed, lanes = arrived.shape
@@ -165,7 +172,7 @@
     fresh = count * rows
     values = arrived[:, :rows].reshape(fresh, lanes)
     gate_one = arrived[:, rows : 2 * rows].reshape(fresh, lanes).astype(F32)
-    past_one = here[...].astype(F32) + there[...].astype(F32)
+    past_one = here[...].astype(F32) + one[...].astype(F32) + two[...].astype(F32) + three[...].astype(F32)
     first = back_to_time(i[0], i[1], times_conjugate(spectra[0], spectrum(f, values)))
     gated = (gate_one * (past_one + first)).astype(BF16)
     gated_all[...] = gated
@@ -197,12 +204,12 @@
     out[...] = jnp.sum(arrived[...].astype(F32), axis=0).astype(BF16)
 
 
-def call(kernel, out_shape, in_specs, flops, nbytes, scratch=(), limit=LIMIT):
+def call(kernel, out_shape, in_specs, flops, nbytes, scratch=(), limit=LIMIT, out_specs=None):
     return pl.pallas_call(
         kernel,
         out_shape=out_shape,
         in_specs=in_specs,
-        out_specs=jax.tree.map(lambda _: VMEM, out_shape),
+        out_specs=out_specs or jax.tree.map(lambda _: VMEM, out_shape),
         scratch_shapes=list(scratch),
         cost_estimate=pl.CostEstimate(flops=flops, bytes_accessed=nbytes, transcendentals=0),
         compiler_params=pltpu.CompilerParams(vmem_limit_bytes=limit),
@@ -235,37 +242,40 @@
     index = ctx_index.reshape(1).astype(jnp.int32)
     last = (index == ctx_count - 1).astype(jnp.int32)
 
-    border = lax.ppermute(filt_far, "ctx", [(i, i - 1) for i in range(1, ctx_count)])
-    gathered = exchanged(jnp.broadcast_to(inputs, (chan_count, rows, width)), "chan")
-
     unit = fresh * fresh * 4 * width
     w_three = w_in.transpose(1, 0, 2)
-    scales = gain.reshape(-1, 128)
+    border = lax.ppermute(filt_far, "ctx", [(i, i - 1) for i in range(1, ctx_count)])
+    loads = (filt_far, filt_near, history, forward, inverse, gain.reshape(-1, 128))
+    copies, own, near, past, f, i, scales = call(
+        open_kernel,
+        (
+            jax.ShapeDtypeStruct((chan_count, rows, width), BF16),
+            *(jax.ShapeDtypeStruct(a.shape, a.dtype) for a in loads),
+        ),
+        [HBM] * 7,
+        1 << 10,
+        1 << 21,
+        scratch=[pltpu.VMEM((rows, width), BF16), pltpu.SemaphoreType.DMA((7 + chan_count,))],
+        out_specs=(pl.BlockSpec(memory_space=pl.ANY), *[VMEM] * 6),
+    )(*(in_hbm(a) for a in (inputs, *loads)))
+    gathered = exchanged(copies, "chan")
+
     lanes = width // 2
-    half = jax.ShapeDtypeStruct((2 * fresh, lanes), F32)
+    half = jax.ShapeDtypeStruct((fresh, lanes), F32)
     spread = (2 * fresh, lanes)
-    keep, send, near, f, i, scales = call(
-        past_kernel,
-        (
-            half,
-            half,
-            *(jax.ShapeDtypeStruct(a.shape, a.dtype) for a in (filt_near, forward, inverse, scales)),
-        ),
-        [SMEM, SMEM, VMEM] + [HBM] * 6,
-        unit * 18,
+    keep_two, send_two, later = call(
+        second_past_kernel,
+        (half, half, jax.ShapeDtypeStruct((3, fresh, width), BF16)),
+        [SMEM, SMEM] + [VMEM] * 6,
+        unit * 9,
         2 << 20,
-        scratch=[
-            pltpu.VMEM(filt_far.shape, BF16),
-            pltpu.VMEM(history.shape, BF16),
-            pltpu.VMEM((ctx_count // 2, 2, rows, width), F32),
-            pltpu.VMEM((3, 2, *spread), F32),
-            pltpu.SemaphoreType.DMA((6,)),
-        ],
-    )(index, last, border, *(in_hbm(a) for a in (filt_far, filt_near, history, forward, inverse, scales)))
-
-    came = swapped(send, "ctx", 1)
-    here = added(keep[:fresh], came[:fresh])
-    there = swapped(here, "ctx", 2)
+        scratch=[pltpu.VMEM((ctx_count // 2, 2, rows, width), F32), pltpu.VMEM((3, 2, *spread), F32)],
+    )(index, last, border, own, near, past, f, i)
+    came_two = swapped(send_two, "ctx", 1)
+    keep_one, send_one = call(
+        first_past_kernel, (half, half), [SMEM] + [VMEM] * 3, unit * 9, 1 << 20
+    )(index, later, f, i)
+    came_one = swapped(send_one, "ctx", 1)
 
     payload, gate_two = call(
         project_kernel,
@@ -277,14 +287,14 @@
         2 * rows * w_in.size,
         2 * w_in.size,
         scratch=[pltpu.VMEM(w_three.shape, BF16), pltpu.SemaphoreType.DMA((8,))],
-    )(gathered, scales, in_hbm(w_three), keep, came)
-
-    here = added(here, there)
+    )(gathered, scales, in_hbm(w_three), keep_two, came_two)
+
+    here = added(keep_one, came_one)
     payload, here = lax.optimization_barrier((payload, here))
-    there = swapped(here, "ctx", 8)
+    there = swapped(here, "ctx", 2)
     arrived = exchanged(payload, "ctx")
     here = added(here, there)
-    there = swapped(here, "ctx", 4)
+    others = [swapped(here, "ctx", step) for step in (12, 8, 4)]
     spectra = call(
         near_kernel,
         jax.ShapeDtypeStruct((2, 2 * fresh, lanes), F32),
@@ -298,7 +308,7 @@
     keep, send, w_out = call(
         mix_kernel,
         (block, block, jax.ShapeDtypeStruct(w_out.shape, BF16)),
-        [SMEM] + [VMEM] * 6 + [HBM],
+        [SMEM] + [VMEM] * 8 + [HBM],
         unit * 4,
         4 << 20,
         scratch=[
@@ -306,7 +316,7 @@
             pltpu.VMEM((2, 2, rows, lanes), F32),
             pltpu.SemaphoreType.DMA,
         ],
-    )(index, arrived, here, there, spectra, f, i, in_hbm(w_out))
+    )(index, arrived, here, *others, spectra, f, i, in_hbm(w_out))
     came = swapped(send, "ctx", 1)
     partial, gated = call(
         finish_kernel,

time: 74.1 us -> 73.7 us (level)
    ppermute x1, waiting for transfers between devices: 5.34 us -> 3.64 us  [layer(): lax.ppermute(filt_far, 'ctx', [(i, i - 1) for i in range(1, ctx_count)])]
    ppermute x5 -> x7, waiting for transfers between devices: 4.85 us -> 6.38 us  [swapped(): lax.ppermute(array, axis, [(i, i ^ step) for i in range(lax.axis_size(axi...]
    all_to_all x2, starting transfers between devices: 17.1 us -> 15.7 us  [exchanged(): return lax.all_to_all(array, axis, split_axis=0, concat_axis=0, tiled=True)]
    ppermute x5 -> x7, starting transfers between devices: 8.14 us -> 9.29 us  [swapped(): lax.ppermute(array, axis, [(i, i ^ step) for i in range(lax.axis_size(axi...]
    pallas_call x1 -> x3, Pallas kernels: 4.25 us -> 4.89 us  [the longest x1 1.9 us: layer(): call(second_past_kernel, (half, half, jax.ShapeDtypeStruct((3, fresh, wid...]
  transfers between devices with their start and end apart: 8 -> 10, of which waited for: 5 -> 6; matrix products, arithmetic and copies ran while one was open for 1% -> 0% of each run, Pallas kernels for 6% -> 3%
where the time goes in v6:
time: 73.7 us; the launch traced here: 73 us
  starting transfers between devices  30.1 us (41%)
  waiting for transfers between devices  17.6 us (24%)
  Pallas kernels  13.1 us (18%)
  blocking collectives  11.4 us (15%)
    all_to_all x2, starting transfers between devices, exchanged(): return lax.all_to_all(array, axis, split_axis=0, concat_axis=0, tiled=True)  15.7 us
    all_to_all x1, blocking collectives, exchanged(): return lax.all_to_all(array, axis, split_axis=0, concat_axis=0, tiled=True)  11.4 us
    ppermute x7, starting transfers between devices, swapped(): lax.ppermute(array, axis, [(i, i ^ step) for i in range(lax.axis_size(axi...  9.29 us
    all_to_all x2, waiting for transfers between devices, exchanged(): return lax.all_to_all(array, axis, split_axis=0, concat_axis=0, tiled=True)  7.6 us
    ppermute x7, waiting for transfers between devices, swapped(): lax.ppermute(array, axis, [(i, i ^ step) for i in range(lax.axis_size(axi...  6.38 us
    ppermute x1, starting transfers between devices, layer(): lax.ppermute(filt_far, 'ctx', [(i, i - 1) for i in range(1, ctx_count)])  5.11 us
    pallas_call x1, Pallas kernels, layer(): call(project_kernel, (jax.ShapeDtypeStruct((ctx_count, 3 * rows, lanes),...  3.77 us
    ppermute x1, waiting for transfers between devices, layer(): lax.ppermute(filt_far, 'ctx', [(i, i - 1) for i in range(1, ctx_count)])  3.64 us
  transfers between devices with their start and end apart: 10, of which 6 were waited for; matrix products, arithmetic and copies ran while one was open for 0% of the time, Pallas kernels for 3%

profile of v6, /device:TPU:1, one launch (start us, length us, event | category | flops | bytes accessed | tf_op | source)
XLA Modules:
  0.0 73.0 jit_solution(9846711509230537271)
XLA Ops:
  0.6 5.1 %collective-permute-start = (bf16[256,2,256]{2,1,0:T(2,128)(2,1)}, bf16[256,2,256]{2,1,0:T(2,128)(2,1)S(1)}, u32[]{:S(2)}, u32[]{:S(2)}) collective-permute-start(bf16[256,2,256]{2,1,0:T(2,128)(2,1)} %refs_1_.1), channel_id=1, source_target_pairs={{16,0},{32,16},{48,32},{64,48},{80,64},{96,80},{112,96},{128,112},... | collective-permute-start | bytes 786440 | tf_op jit(solution)/shard_map/ppermute | solution.py:247
  5.7 1.7 %shard_map.104 = (bf16[16,16,256]{2,1,0:T(8,128)(2,1)}, bf16[256,2,256]{2,1,0:T(2,128)(2,1)S(1)}, bf16[256,2,256]{2,1,0:T(2,128)(2,1)S(1)}, bf16[256,2,256]{2,1,...) custom-call(bf16[16,256]{1,0:T(8,128)(2,1)} %refs_0_.1, ...), custom_call_target="tpu_custom_call" | custom-call | flops 1024 | bytes 2097152 | tf_op jit(solution)/shard_map/pallas_call | solution.py:249
  7.4 3.6 %collective-permute-done.border = bf16[256,2,256]{2,1,0:T(2,128)(2,1)S(1)} collective-permute-done((bf16[256,2,256]{2,1,0:T(2,128)(2,1)}, bf16[256,2,256]{2,1,0:T(2,128)(2,1)S(1)}, u32[]{:S(2)}, u32[]{:S(2)}) %collective-permute-start) | collective-permute-done | bytes 262176 | tf_op jit(solution)/shard_map/ppermute | solution.py:247
  11.1 1.9 %shard_map.105 = (f32[256,128]{1,0:T(8,128)S(1)}, f32[256,128]{1,0:T(8,128)S(1)}, bf16[3,256,256]{2,1,0:T(8,128)(2,1)S(1)}) custom-call(s32[1]{0:T(128)} %bitcast.index, s32[1]{0:T(128)S(6)} %convert_element_type.15.last, bf16[256,2,256]{2,1,0:T(2,128)(2,1)S(1)} %collective-permute-done.border, bf16[256,2,256]{2,1,0:T(2,128)(2,1)S(1)} %get-tuple-element.25.own, ...), custom_call_target="tpu_custom_call" | custom-call | flops 603979776 | bytes 2097152 | tf_op jit(solution)/shard_map/pallas_call | solution.py:266
  13.0 1.3 %shard_map.107 = (f32[256,128]{1,0:T(8,128)S(1)}, f32[256,128]{1,0:T(8,128)S(1)}) custom-call(s32[1]{0:T(128)} %bitcast.index, bf16[3,256,256]{2,1,0:T(8,128)(2,1)S(1)} %get-tuple-element.33.rows, bf16[2,512,256]{2,1,0:T(8,128)(2,1)S(1)} %get-tuple-element.28.f, bf16[2,256,512]{2,1,0:T(8,128)(2,1)S(1)} %get-tuple-element.29.i), custom_call_target="tpu_custom_call" | custom-call | flops 603979776 | bytes 1048576 | tf_op jit(solution)/shard_map/pallas_call | solution.py:275
  14.3 0.1 collective-permute-start.2
  14.4 9.1 %all-to-all-start = ((bf16[16,16,256]{2,1,0:T(8,128)(2,1)}), bf16[16,16,256]{2,1,0:T(8,128)(2,1)S(1)}, u32[]{:S(2)}, u32[]{:S(2)}) async-start(bf16[16,16,256]{2,1,0:T(8,128)(2,1)} %get-tuple-element.23), calls=%async_computation | async-start | bytes 262144 | tf_op jit(solution)/shard_map/all_to_all | solution.py:224
  23.5 0.9 %collective-permute-start.1 = (f32[256,128]{1,0:T(8,128)S(1)}, f32[256,128]{1,0:T(8,128)S(1)}, u32[]{:S(2)}, u32[]{:S(2)}) collective-permute-start(f32[256,128]{1,0:T(8,128)S(1)} %get-tuple-element.31), channel_id=1, source_target_pairs={{0,16},{16,0},{32,48},{48,32},{64,80},{80,64},{96,112},{112,96},{1... | collective-permute-start | bytes 393224 | tf_op jit(solution)/shard_map/ppermute | solution.py:228
  24.3 0.0 collective-permute-done.2
  24.4 7.6 %all-to-all-done.gathered = bf16[16,16,256]{2,1,0:T(8,128)(2,1)S(1)} async-done(((bf16[16,16,256]{2,1,0:T(8,128)(2,1)}), bf16[16,16,256]{2,1,0:T(8,128)(2,1)S(1)}, u32[]{:S(2)}, u32[]{:S(2)}) %all-to-all-start) | async-done | bytes 131104 | tf_op jit(solution)/shard_map/all_to_all | solution.py:224
  32.0 0.0 collective-permute-done.1.came
  32.0 3.8 %shard_map.106 = (bf16[16,48,128]{2,1,0:T(8,128)(2,1)}, bf16[16,256]{1,0:T(8,128)(2,1)S(1)}) custom-call(bf16[16,16,256]{2,1,0:T(8,128)(2,1)S(1)} %all-to-all-done.gathered, f32[32,128]{1,0:T(8,128)S(1)} %get-tuple-element.24.gain, bf16[3,4096,256]{2,1,0:T(8,128)(2,1)} %bitcast.3, f32[256,128]{1,0:T(8,128)S(1)} %get-tuple-element.30.keep, ...), custom_call_target="tpu_custom_call" | custom-call | flops 100663296 | bytes 6291456 | tf_op jit(solution)/shard_map/pallas_call | solution.py:280
  35.7 3.6 %collective-permute-start.3 = (bf16[256,128]{1,0:T(8,128)(2,1)S(1)}, bf16[256,128]{1,0:T(8,128)(2,1)S(1)}, u32[]{:S(2)}, u32[]{:S(2)}) collective-permute-start(bf16[256,128]{1,0:T(8,128)(2,1)S(1)} %add_convert_fusion.1), channel_id=1, source_target_pairs={{0,32},{16,48},{32,0},{48,16},{64,96},{80,112},{96,64},{112,80},{1... | collective-permute-start | bytes 196616 | tf_op jit(solution)/shard_map/ppermute | solution.py:228
  39.4 6.7 %all-to-all-start.1 = ((bf16[16,48,128]{2,1,0:T(8,128)(2,1)}), bf16[16,48,128]{2,1,0:T(8,128)(2,1)S(1)}, u32[]{:S(2)}, u32[]{:S(2)}) async-start(bf16[16,48,128]{2,1,0:T(8,128)(2,1)} %get-tuple-element.36), calls=%async_computation.1 | async-start | bytes 393216 | tf_op jit(solution)/shard_map/all_to_all | solution.py:224
  46.0 0.0 collective-permute-done.3
  46.1 1.4 %collective-permute-start.6 = (bf16[256,128]{1,0:T(8,128)(2,1)S(1)}, bf16[256,128]{1,0:T(8,128)(2,1)S(1)}, u32[]{:S(2)}, u32[]{:S(2)}) collective-permute-start(bf16[256,128]{1,0:T(8,128)(2,1)S(1)} %add_convert_fusion.here), channel_id=1, source_target_pairs={{0,64},{16,80},{32,96},{48,112},{64,0},{80,16},{96,32},{112,48},{1... | collective-permute-start | bytes 196616 | tf_op jit(solution)/shard_map/ppermute | solution.py:228
  47.5 2.4 %collective-permute-start.5 = (bf16[256,128]{1,0:T(8,128)(2,1)S(1)}, bf16[256,128]{1,0:T(8,128)(2,1)S(1)}, u32[]{:S(2)}, u32[]{:S(2)}) collective-permute-start(bf16[256,128]{1,0:T(8,128)(2,1)S(1)} %add_convert_fusion.here), channel_id=1, source_target_pairs={{0,128},{16,144},{32,160},{48,176},{64,192},{80,208},{96,224},{112... | collective-permute-start | bytes 196616 | tf_op jit(solution)/shard_map/ppermute | solution.py:228
  49.9 0.1 collective-permute-start.4
  50.0 0.5 shard_map.108.spectra
  50.5 1.2 %collective-permute-done.6.three = bf16[256,128]{1,0:T(8,128)(2,1)S(1)} collective-permute-done((bf16[256,128]{1,0:T(8,128)(2,1)S(1)}, bf16[256,128]{1,0:T(8,128)(2,1)S(1)}, u32[]{:S(2)}, u32[]{:S(2)}) %collective-permute-start.6) | collective-permute-done | bytes 65568 | tf_op jit(solution)/shard_map/ppermute | solution.py:228
  51.8 2.9 %collective-permute-done.5.two = bf16[256,128]{1,0:T(8,128)(2,1)S(1)} collective-permute-done((bf16[256,128]{1,0:T(8,128)(2,1)S(1)}, bf16[256,128]{1,0:T(8,128)(2,1)S(1)}, u32[]{:S(2)}, u32[]{:S(2)}) %collective-permute-start.5) | collective-permute-done | bytes 65568 | tf_op jit(solution)/shard_map/ppermute | solution.py:228
  54.7 1.4 %collective-permute-done.4.one = bf16[256,128]{1,0:T(8,128)(2,1)S(1)} collective-permute-done((bf16[256,128]{1,0:T(8,128)(2,1)S(1)}, bf16[256,128]{1,0:T(8,128)(2,1)S(1)}, u32[]{:S(2)}, u32[]{:S(2)}) %collective-permute-start.4) | collective-permute-done | bytes 65568 | tf_op jit(solution)/shard_map/ppermute | solution.py:228
  56.1 0.0 all-to-all-done.1.arrived
  56.1 2.5 %shard_map.109 = (f32[2,16,128]{2,1,0:T(8,128)S(1)}, f32[2,16,128]{2,1,0:T(8,128)S(1)}, bf16[256,4096]{1,0:T(8,128)(2,1)S(1)}) custom-call(s32[1]{0:T(128)} %bitcast.index, bf16[16,48,128]{2,1,0:T(8,128)(2,1)S(1)} %all-to-all-done.1.arrived, bf16[256,128]{1,0:T(8,128)(2,1)S(1)} %add_convert_fusion.here, bf16[256,128]{1,0:T(8,128)(2,1)S(1)} %collective-permute-done.4.one, ...), custom_call_target="tpu_custom_call" | custom-call | flops 268435456 | bytes 4194304 | tf_op jit(solution)/shard_map/pallas_call | solution.py:308
  58.6 0.8 %collective-permute-start.7 = (f32[2,16,128]{2,1,0:T(8,128)S(1)}, f32[2,16,128]{2,1,0:T(8,128)S(1)}, u32[]{:S(2)}, u32[]{:S(2)}) collective-permute-start(f32[2,16,128]{2,1,0:T(8,128)S(1)} %get-tuple-element.39), channel_id=1, source_target_pairs={{0,16},{16,0},{32,48},{48,32},{64,80},{80,64},{96,112},{112,96},{1... | collective-permute-start | bytes 49160 | tf_op jit(solution)/shard_map/ppermute | solution.py:228
  59.3 0.8 %collective-permute-done.7.came = f32[2,16,128]{2,1,0:T(8,128)S(1)} collective-permute-done((f32[2,16,128]{2,1,0:T(8,128)S(1)}, f32[2,16,128]{2,1,0:T(8,128)S(1)}, u32[]{:S(2)}, u32[]{:S(2)}) %collective-permute-start.7) | collective-permute-done | bytes 16416 | tf_op jit(solution)/shard_map/ppermute | solution.py:228
  60.2 0.9 %shard_map.110 = (bf16[16,16,256]{2,1,0:T(8,128)(2,1)S(1)}, bf16[16,256]{1,0:T(8,128)(2,1)}) custom-call(s32[1]{0:T(128)} %bitcast.index, f32[2,16,128]{2,1,0:T(8,128)S(1)} %get-tuple-element.38.keep, f32[2,16,128]{2,1,0:T(8,128)S(1)} %collective-permute-done.7.came, bf16[16,256]{1,0:T(8,128)(2,1)S(1)} %get-tuple-element.40.gate_two, ...), custom_call_target="tpu_custom_call" | custom-call | flops 67108864 | bytes 1048576 | tf_op jit(solution)/shard_map/pallas_call | solution.py:321
  61.1 11.4 %all_to_all.15.arrived = bf16[16,16,256]{2,1,0:T(8,128)(2,1)S(1)} all-to-all(bf16[16,16,256]{2,1,0:T(8,128)(2,1)S(1)} %get-tuple-element.42), channel_id=1, replica_groups=mesh['ctx'=16,'chan'=16] {'chan'}, dimensions={0} | all-to-all | bytes 262144 | tf_op jit(solution)/shard_map/all_to_all | solution.py:224
  72.4 0.6 shard_map.111
  (2 shorter events, 0.0 us)
Async XLA Ops:
  0.6 10.5 %collective-permute-start = (bf16[256,2,256]{2,1,0:T(2,128)(2,1)}, bf16[256,2,256]{2,1,0:T(2,128)(2,1)S(1)}, u32[]{:S(2)}, u32[]{:S(2)}) collective-permute-start(bf16[256,2,256]{2,1,0:T(2,128)(2,1)} %refs_1_.1), channel_id=1, source_target_pairs={{16,0},{32,16},{48,32},{64,48},{80,64},{96,80},{112,96},{128,112},... | collective-permute-start | bytes 786440 | tf_op jit(solution)/shard_map/ppermute | solution.py:247
  14.3 10.0 %collective-permute-start.2 = (f32[256,128]{1,0:T(8,128)S(1)}, f32[256,128]{1,0:T(8,128)S(1)}, u32[]{:S(2)}, u32[]{:S(2)}) collective-permute-start(f32[256,128]{1,0:T(8,128)S(1)} %get-tuple-element.35), channel_id=1, source_target_pairs={{0,16},{16,0},{32,48},{48,32},{64,80},{80,64},{96,112},{112,96},{1... | collective-permute-start | bytes 393224 | tf_op jit(solution)/shard_map/ppermute | solution.py:228
  14.4 17.6 %all-to-all-start = ((bf16[16,16,256]{2,1,0:T(8,128)(2,1)}), bf16[16,16,256]{2,1,0:T(8,128)(2,1)S(1)}, u32[]{:S(2)}, u32[]{:S(2)}) async-start(bf16[16,16,256]{2,1,0:T(8,128)(2,1)} %get-tuple-element.23), calls=%async_computation | async-start | bytes 262144 | tf_op jit(solution)/shard_map/all_to_all | solution.py:224
  23.5 8.5 %collective-permute-start.1 = (f32[256,128]{1,0:T(8,128)S(1)}, f32[256,128]{1,0:T(8,128)S(1)}, u32[]{:S(2)}, u32[]{:S(2)}) collective-permute-start(f32[256,128]{1,0:T(8,128)S(1)} %get-tuple-element.31), channel_id=1, source_target_pairs={{0,16},{16,0},{32,48},{48,32},{64,80},{80,64},{96,112},{112,96},{1... | collective-permute-start | bytes 393224 | tf_op jit(solution)/shard_map/ppermute | solution.py:228
  35.7 10.3 %collective-permute-start.3 = (bf16[256,128]{1,0:T(8,128)(2,1)S(1)}, bf16[256,128]{1,0:T(8,128)(2,1)S(1)}, u32[]{:S(2)}, u32[]{:S(2)}) collective-permute-start(bf16[256,128]{1,0:T(8,128)(2,1)S(1)} %add_convert_fusion.1), channel_id=1, source_target_pairs={{0,32},{16,48},{32,0},{48,16},{64,96},{80,112},{96,64},{112,80},{1... | collective-permute-start | bytes 196616 | tf_op jit(solution)/shard_map/ppermute | solution.py:228
  39.4 16.7 %all-to-all-start.1 = ((bf16[16,48,128]{2,1,0:T(8,128)(2,1)}), bf16[16,48,128]{2,1,0:T(8,128)(2,1)S(1)}, u32[]{:S(2)}, u32[]{:S(2)}) async-start(bf16[16,48,128]{2,1,0:T(8,128)(2,1)} %get-tuple-element.36), calls=%async_computation.1 | async-start | bytes 393216 | tf_op jit(solution)/shard_map/all_to_all | solution.py:224
  46.1 5.7 %collective-permute-start.6 = (bf16[256,128]{1,0:T(8,128)(2,1)S(1)}, bf16[256,128]{1,0:T(8,128)(2,1)S(1)}, u32[]{:S(2)}, u32[]{:S(2)}) collective-permute-start(bf16[256,128]{1,0:T(8,128)(2,1)S(1)} %add_convert_fusion.here), channel_id=1, source_target_pairs={{0,64},{16,80},{32,96},{48,112},{64,0},{80,16},{96,32},{112,48},{1... | collective-permute-start | bytes 196616 | tf_op jit(solution)/shard_map/ppermute | solution.py:228
  47.5 7.2 %collective-permute-start.5 = (bf16[256,128]{1,0:T(8,128)(2,1)S(1)}, bf16[256,128]{1,0:T(8,128)(2,1)S(1)}, u32[]{:S(2)}, u32[]{:S(2)}) collective-permute-start(bf16[256,128]{1,0:T(8,128)(2,1)S(1)} %add_convert_fusion.here), channel_id=1, source_target_pairs={{0,128},{16,144},{32,160},{48,176},{64,192},{80,208},{96,224},{112... | collective-permute-start | bytes 196616 | tf_op jit(solution)/shard_map/ppermute | solution.py:228
  49.9 6.2 %collective-permute-start.4 = (bf16[256,128]{1,0:T(8,128)(2,1)S(1)}, bf16[256,128]{1,0:T(8,128)(2,1)S(1)}, u32[]{:S(2)}, u32[]{:S(2)}) collective-permute-start(bf16[256,128]{1,0:T(8,128)(2,1)S(1)} %add_convert_fusion.here), channel_id=1, source_target_pairs={{0,192},{16,208},{32,224},{48,240},{64,128},{80,144},{96,160},{112... | collective-permute-start | bytes 196616 | tf_op jit(solution)/shard_map/ppermute | solution.py:228
  58.6 1.6 %collective-permute-start.7 = (f32[2,16,128]{2,1,0:T(8,128)S(1)}, f32[2,16,128]{2,1,0:T(8,128)S(1)}, u32[]{:S(2)}, u32[]{:S(2)}) collective-permute-start(f32[2,16,128]{2,1,0:T(8,128)S(1)} %get-tuple-element.39), channel_id=1, source_target_pairs={{0,16},{16,0},{32,48},{48,32},{64,80},{80,64},{96,112},{112,96},{1... | collective-permute-start | bytes 49160 | tf_op jit(solution)/shard_map/ppermute | solution.py:228

commit v7 on v6

--- a/solution.py
+++ b/solution.py
@@ -88,7 +88,7 @@
         move.wait()
 
 
-def second_past_kernel(index, last, border, own, near, history, f, i, keep, send, later, parts, spread):
+def first_past_kernel(index, last, border, own, near, history, f, i, keep, send, later, spread):
     @pl.when(last[0] > 0)
     def _():
         spread_out(near, spread.at[1])
@@ -99,26 +99,25 @@
 
     spread_out(own, spread.at[0])
     spread_out(history, spread.at[2])
+    part = past_part(*(parted(spread.at[n], 2, 0) for n in range(3)), f, i)
+    lanes = keep.shape[1]
+    low, high = part[:, :lanes], part[:, lanes:]
     mine = index[0] % 2
-    part = past_part(*(parted(spread.at[n], 2, 1) for n in range(3)), f, i)
-    parts[...] = part.reshape(parts.shape)
+    keep[...] = jnp.where(mine == 0, low, high)
+    send[...] = jnp.where(mine == 0, high, low)
+    for n in range(3):
+        later[n] = parted(spread.at[n], 2, 1)
+
+
+def second_past_kernel(index, rows, f, i, keep, send, parts):
+    mine = index[0] % 2
+    parts[...] = past_part(rows[0], rows[1], rows[2], f, i).reshape(parts.shape)
     half, lanes = keep.shape[0] // 2, keep.shape[1]
     for h in range(2):
         there = pl.ds(h * half, half)
         span = slice(h * lanes, (h + 1) * lanes)
         keep[there] = parts[:, mine, :, span].reshape(half, lanes)
         send[there] = parts[:, 1 - mine, :, span].reshape(half, lanes)
-    for n in range(3):
-        later[n] = parted(spread.at[n], 2, 0)
-
-
-def first_past_kernel(index, rows, f, i, keep, send):
-    part = past_part(rows[0], rows[1], rows[2], f, i)
-    lanes = keep.shape[1]
-    low, high = part[:, :lanes], part[:, lanes:]
-    mine = index[0] % 2
-    keep[...] = jnp.where(mine == 0, low, high)
-    send[...] = jnp.where(mine == 0, high, low)
 
 
 def project_kernel(gathered, gain, w_hbm, keep, came, out, gate_two, w, sems):
@@ -164,7 +163,7 @@
         spectra[which] = spectrum(f, parted(spread, 2, which))
 
 
-def mix_kernel(index, arrived, here, one, two, three, spectra, f, i, w_hbm, keep, send, w_out, gated_all, sums, sem):
+def mix_kernel(index, arrived, here, there, spectra, f, i, w_hbm, keep, send, w_out, gated_all, sums, sem):
     load = pltpu.make_async_copy(w_hbm, w_out, sem)
     load.start()
     count, packed, lanes = arrived.shape
@@ -172,7 +171,7 @@
     fresh = count * rows
     values = arrived[:, :rows].reshape(fresh, lanes)
     gate_one = arrived[:, rows : 2 * rows].reshape(fresh, lanes).astype(F32)
-    past_one = here[...].astype(F32) + one[...].astype(F32) + two[...].astype(F32) + three[...].astype(F32)
+    past_one = here[...].astype(F32) + there[...].astype(F32)
     first = back_to_time(i[0], i[1], times_conjugate(spectra[0], spectrum(f, values)))
     gated = (gate_one * (past_one + first)).astype(BF16)
     gated_all[...] = gated
@@ -263,19 +262,26 @@
     lanes = width // 2
     half = jax.ShapeDtypeStruct((fresh, lanes), F32)
     spread = (2 * fresh, lanes)
-    keep_two, send_two, later = call(
-        second_past_kernel,
+    keep_one, send_one, later = call(
+        first_past_kernel,
         (half, half, jax.ShapeDtypeStruct((3, fresh, width), BF16)),
         [SMEM, SMEM] + [VMEM] * 6,
         unit * 9,
         2 << 20,
-        scratch=[pltpu.VMEM((ctx_count // 2, 2, rows, width), F32), pltpu.VMEM((3, 2, *spread), F32)],
+        scratch=[pltpu.VMEM((3, 2, *spread), F32)],
     )(index, last, border, own, near, past, f, i)
+    came_one = swapped(send_one, "ctx", 1)
+    keep_two, send_two = call(
+        second_past_kernel,
+        (half, half),
+        [SMEM] + [VMEM] * 3,
+        unit * 9,
+        1 << 20,
+        scratch=[pltpu.VMEM((ctx_count // 2, 2, rows, width), F32)],
+    )(index, later, f, i)
     came_two = swapped(send_two, "ctx", 1)
-    keep_one, send_one = call(
-        first_past_kernel, (half, half), [SMEM] + [VMEM] * 3, unit * 9, 1 << 20
-    )(index, later, f, i)
-    came_one = swapped(send_one, "ctx", 1)
+    here = added(keep_one, came_one)
+    there = swapped(here, "ctx", 2)
 
     payload, gate_two = call(
         project_kernel,
@@ -289,12 +295,12 @@
         scratch=[pltpu.VMEM(w_three.shape, BF16), pltpu.SemaphoreType.DMA((8,))],
     )(gathered, scales, in_hbm(w_three), keep_two, came_two)
 
-    here = added(keep_one, came_one)
+    here = added(here, there)
     payload, here = lax.optimization_barrier((payload, here))
-    there = swapped(here, "ctx", 2)
+    there = swapped(here, "ctx", 8)
     arrived = exchanged(payload, "ctx")
     here = added(here, there)
-    others = [swapped(here, "ctx", step) for step in (12, 8, 4)]
+    there = swapped(here, "ctx", 4)
     spectra = call(
         near_kernel,
         jax.ShapeDtypeStruct((2, 2 * fresh, lanes), F32),
@@ -308,7 +314,7 @@
     keep, send, w_out = call(
         mix_kernel,
         (block, block, jax.ShapeDtypeStruct(w_out.shape, BF16)),
-        [SMEM] + [VMEM] * 8 + [HBM],
+        [SMEM] + [VMEM] * 6 + [HBM],
         unit * 4,
         4 << 20,
         scratch=[
@@ -316,7 +322,7 @@
             pltpu.VMEM((2, 2, rows, lanes), F32),
             pltpu.SemaphoreType.DMA,
         ],
-    )(index, arrived, here, *others, spectra, f, i, in_hbm(w_out))
+    )(index, arrived, here, there, spectra, f, i, in_hbm(w_out))
     came = swapped(send, "ctx", 1)
     partial, gated = call(
         finish_kernel,

time: 73.7 us -> 71.1 us (0.965)
  waiting for transfers between devices: 17.6 us -> 14.1 us
  starting transfers between devices: 30.1 us -> 31.1 us
    all_to_all x2, waiting for transfers between devices: 7.6 us -> 5.57 us  [exchanged(): return lax.all_to_all(array, axis, split_axis=0, concat_axis=0, tiled=True)]
    ppermute x7 -> x6, waiting for transfers between devices: 6.38 us -> 4.85 us  [swapped(): lax.ppermute(array, axis, [(i, i ^ step) for i in range(lax.axis_size(axi...]
    all_to_all x2, starting transfers between devices: 15.7 us -> 17 us  [exchanged(): return lax.all_to_all(array, axis, split_axis=0, concat_axis=0, tiled=True)]
    ppermute x7 -> x6, starting transfers between devices: 9.29 us -> 9.01 us  [swapped(): lax.ppermute(array, axis, [(i, i ^ step) for i in range(lax.axis_size(axi...]
  transfers between devices with their start and end apart: 10 -> 9, of which waited for: 6 -> 5; matrix products, arithmetic and copies ran while one was open for 0% -> 0% of each run, Pallas kernels for 3% -> 10%
where the time goes in v7:
time: 71.1 us; the launch traced here: 70.7 us
  starting transfers between devices  31.1 us (44%)
  waiting for transfers between devices  14.1 us (20%)
  Pallas kernels  13.1 us (18%)
  blocking collectives  11.5 us (16%)
  between operations  0.74 us (1%)
    all_to_all x2, starting transfers between devices, exchanged(): return lax.all_to_all(array, axis, split_axis=0, concat_axis=0, tiled=True)  17 us
    all_to_all x1, blocking collectives, exchanged(): return lax.all_to_all(array, axis, split_axis=0, concat_axis=0, tiled=True)  11.5 us
    ppermute x6, starting transfers between devices, swapped(): lax.ppermute(array, axis, [(i, i ^ step) for i in range(lax.axis_size(axi...  9.01 us
    all_to_all x2, waiting for transfers between devices, exchanged(): return lax.all_to_all(array, axis, split_axis=0, concat_axis=0, tiled=True)  5.57 us
    ppermute x1, starting transfers between devices, layer(): lax.ppermute(filt_far, 'ctx', [(i, i - 1) for i in range(1, ctx_count)])  5.11 us
    ppermute x6, waiting for transfers between devices, swapped(): lax.ppermute(array, axis, [(i, i ^ step) for i in range(lax.axis_size(axi...  4.85 us
    pallas_call x1, Pallas kernels, layer(): call(project_kernel, (jax.ShapeDtypeStruct((ctx_count, 3 * rows, lanes),...  3.77 us
    ppermute x1, waiting for transfers between devices, layer(): lax.ppermute(filt_far, 'ctx', [(i, i - 1) for i in range(1, ctx_count)])  3.64 us
  transfers between devices with their start and end apart: 9, of which 5 were waited for; matrix products, arithmetic and copies ran while one was open for 0% of the time, Pallas kernels for 10%

profile of v7, /device:TPU:1, one launch (start us, length us, event | category | flops | bytes accessed | tf_op | source)
XLA Modules:
  0.0 70.7 jit_solution(14685068240006927046)
XLA Ops:
  0.6 5.1 %collective-permute-start = (bf16[256,2,256]{2,1,0:T(2,128)(2,1)}, bf16[256,2,256]{2,1,0:T(2,128)(2,1)S(1)}, u32[]{:S(2)}, u32[]{:S(2)}) collective-permute-start(bf16[256,2,256]{2,1,0:T(2,128)(2,1)} %refs_1_.1), channel_id=1, source_target_pairs={{16,0},{32,16},{48,32},{64,48},{80,64},{96,80},{112,96},{128,112},... | collective-permute-start | bytes 786440 | tf_op jit(solution)/shard_map/ppermute | solution.py:246
  5.7 1.7 %shard_map.104 = (bf16[16,16,256]{2,1,0:T(8,128)(2,1)}, bf16[256,2,256]{2,1,0:T(2,128)(2,1)S(1)}, bf16[256,2,256]{2,1,0:T(2,128)(2,1)S(1)}, bf16[256,2,256]{2,1,...) custom-call(bf16[16,256]{1,0:T(8,128)(2,1)} %refs_0_.1, ...), custom_call_target="tpu_custom_call" | custom-call | flops 1024 | bytes 2097152 | tf_op jit(solution)/shard_map/pallas_call | solution.py:248
  7.4 3.6 %collective-permute-done.border = bf16[256,2,256]{2,1,0:T(2,128)(2,1)S(1)} collective-permute-done((bf16[256,2,256]{2,1,0:T(2,128)(2,1)}, bf16[256,2,256]{2,1,0:T(2,128)(2,1)S(1)}, u32[]{:S(2)}, u32[]{:S(2)}) %collective-permute-start) | collective-permute-done | bytes 262176 | tf_op jit(solution)/shard_map/ppermute | solution.py:246
  11.1 1.9 %shard_map.105 = (f32[256,128]{1,0:T(8,128)S(1)}, f32[256,128]{1,0:T(8,128)S(1)}, bf16[3,256,256]{2,1,0:T(8,128)(2,1)S(1)}) custom-call(s32[1]{0:T(128)} %bitcast.index, s32[1]{0:T(128)S(6)} %convert_element_type.24.last, bf16[256,2,256]{2,1,0:T(2,128)(2,1)S(1)} %collective-permute-done.border, bf16[256,2,256]{2,1,0:T(2,128)(2,1)S(1)} %get-tuple-element.25.own, ...), custom_call_target="tpu_custom_call" | custom-call | flops 603979776 | bytes 2097152 | tf_op jit(solution)/shard_map/pallas_call | solution.py:265
  13.0 0.1 collective-permute-start.2
  13.1 9.1 %all-to-all-start = ((bf16[16,16,256]{2,1,0:T(8,128)(2,1)}), bf16[16,16,256]{2,1,0:T(8,128)(2,1)S(1)}, u32[]{:S(2)}, u32[]{:S(2)}) async-start(bf16[16,16,256]{2,1,0:T(8,128)(2,1)} %get-tuple-element.23), calls=%async_computation | async-start | bytes 262144 | tf_op jit(solution)/shard_map/all_to_all | solution.py:223
  22.1 1.3 %shard_map.106 = (f32[256,128]{1,0:T(8,128)S(1)}, f32[256,128]{1,0:T(8,128)S(1)}) custom-call(s32[1]{0:T(128)} %bitcast.index, bf16[3,256,256]{2,1,0:T(8,128)(2,1)S(1)} %get-tuple-element.30.rows, bf16[2,512,256]{2,1,0:T(8,128)(2,1)S(1)} %get-tuple-element.28.f, bf16[2,256,512]{2,1,0:T(8,128)(2,1)S(1)} %get-tuple-element.29.i), custom_call_target="tpu_custom_call" | custom-call | flops 603979776 | bytes 1048576 | tf_op jit(solution)/shard_map/pallas_call | solution.py:274
  23.5 0.9 %collective-permute-start.1 = (f32[256,128]{1,0:T(8,128)S(1)}, f32[256,128]{1,0:T(8,128)S(1)}, u32[]{:S(2)}, u32[]{:S(2)}) collective-permute-start(f32[256,128]{1,0:T(8,128)S(1)} %get-tuple-element.32), channel_id=1, source_target_pairs={{0,16},{16,0},{32,48},{48,32},{64,80},{80,64},{96,112},{112,96},{1... | collective-permute-start | bytes 393224 | tf_op jit(solution)/shard_map/ppermute | solution.py:227
  24.3 0.0 collective-permute-done.2
  24.4 3.6 %collective-permute-start.3 = (bf16[256,128]{1,0:T(8,128)(2,1)S(1)}, bf16[256,128]{1,0:T(8,128)(2,1)S(1)}, u32[]{:S(2)}, u32[]{:S(2)}) collective-permute-start(bf16[256,128]{1,0:T(8,128)(2,1)S(1)} %add_convert_fusion.2), channel_id=1, source_target_pairs={{0,32},{16,48},{32,0},{48,16},{64,96},{80,112},{96,64},{112,80},{1... | collective-permute-start | bytes 196616 | tf_op jit(solution)/shard_map/ppermute | solution.py:227
  28.0 2.7 %all-to-all-done.gathered = bf16[16,16,256]{2,1,0:T(8,128)(2,1)S(1)} async-done(((bf16[16,16,256]{2,1,0:T(8,128)(2,1)}), bf16[16,16,256]{2,1,0:T(8,128)(2,1)S(1)}, u32[]{:S(2)}, u32[]{:S(2)}) %all-to-all-start) | async-done | bytes 131104 | tf_op jit(solution)/shard_map/all_to_all | solution.py:223
  30.7 0.0 collective-permute-done.1.came
  30.7 3.8 %shard_map.107 = (bf16[16,48,128]{2,1,0:T(8,128)(2,1)}, bf16[16,256]{1,0:T(8,128)(2,1)S(1)}) custom-call(bf16[16,16,256]{2,1,0:T(8,128)(2,1)S(1)} %all-to-all-done.gathered, f32[32,128]{1,0:T(8,128)S(1)} %get-tuple-element.24.gain, bf16[3,4096,256]{2,1,0:T(8,128)(2,1)} %bitcast.3, f32[256,128]{1,0:T(8,128)S(1)} %get-tuple-element.31.keep, ...), custom_call_target="tpu_custom_call" | custom-call | flops 100663296 | bytes 6291456 | tf_op jit(solution)/shard_map/pallas_call | solution.py:286
  34.5 0.0 collective-permute-done.3
  34.5 2.8 %collective-permute-start.4 = (bf16[256,128]{1,0:T(8,128)(2,1)S(1)}, bf16[256,128]{1,0:T(8,128)(2,1)S(1)}, u32[]{:S(2)}, u32[]{:S(2)}) collective-permute-start(bf16[256,128]{1,0:T(8,128)(2,1)S(1)} %add_convert_fusion.1), channel_id=1, source_target_pairs={{0,128},{16,144},{32,160},{48,176},{64,192},{80,208},{96,224},{112... | collective-permute-start | bytes 196616 | tf_op jit(solution)/shard_map/ppermute | solution.py:227
  37.4 7.9 %all-to-all-start.1 = ((bf16[16,48,128]{2,1,0:T(8,128)(2,1)}), bf16[16,48,128]{2,1,0:T(8,128)(2,1)S(1)}, u32[]{:S(2)}, u32[]{:S(2)}) async-start(bf16[16,48,128]{2,1,0:T(8,128)(2,1)} %get-tuple-element.36), calls=%async_computation.1 | async-start | bytes 393216 | tf_op jit(solution)/shard_map/all_to_all | solution.py:223
  45.3 0.0 collective-permute-done.4
  45.3 1.4 %collective-permute-start.5 = (bf16[256,128]{1,0:T(8,128)(2,1)S(1)}, bf16[256,128]{1,0:T(8,128)(2,1)S(1)}, u32[]{:S(2)}, u32[]{:S(2)}) collective-permute-start(bf16[256,128]{1,0:T(8,128)(2,1)S(1)} %add_convert_fusion.here), channel_id=1, source_target_pairs={{0,64},{16,80},{32,96},{48,112},{64,0},{80,16},{96,32},{112,48},{1... | collective-permute-start | bytes 196616 | tf_op jit(solution)/shard_map/ppermute | solution.py:227
  46.8 0.5 shard_map.108.spectra
  47.3 3.7 %collective-permute-done.5.there = bf16[256,128]{1,0:T(8,128)(2,1)S(1)} collective-permute-done((bf16[256,128]{1,0:T(8,128)(2,1)S(1)}, bf16[256,128]{1,0:T(8,128)(2,1)S(1)}, u32[]{:S(2)}, u32[]{:S(2)}) %collective-permute-start.5) | collective-permute-done | bytes 65568 | tf_op jit(solution)/shard_map/ppermute | solution.py:227
  51.0 2.8 %all-to-all-done.1.arrived = bf16[16,48,128]{2,1,0:T(8,128)(2,1)S(1)} async-done(((bf16[16,48,128]{2,1,0:T(8,128)(2,1)}), bf16[16,48,128]{2,1,0:T(8,128)(2,1)S(1)}, u32[]{:S(2)}, u32[]{:S(2)}) %all-to-all-start.1) | async-done | bytes 196640 | tf_op jit(solution)/shard_map/all_to_all | solution.py:223
  53.9 2.5 %shard_map.109 = (f32[2,16,128]{2,1,0:T(8,128)S(1)}, f32[2,16,128]{2,1,0:T(8,128)S(1)}, bf16[256,4096]{1,0:T(8,128)(2,1)S(1)}) custom-call(s32[1]{0:T(128)} %bitcast.index, bf16[16,48,128]{2,1,0:T(8,128)(2,1)S(1)} %all-to-all-done.1.arrived, bf16[256,128]{1,0:T(8,128)(2,1)S(1)} %add_convert_fusion.here, bf16[256,128]{1,0:T(8,128)(2,1)S(1)} %collective-permute-done.5.there, ...), custom_call_target="tpu_custom_call" | custom-call | flops 268435456 | bytes 4194304 | tf_op jit(solution)/shard_map/pallas_call | solution.py:314
  56.4 0.2 collective-permute-start.6
  56.6 1.1 %collective-permute-done.6.came = f32[2,16,128]{2,1,0:T(8,128)S(1)} collective-permute-done((f32[2,16,128]{2,1,0:T(8,128)S(1)}, f32[2,16,128]{2,1,0:T(8,128)S(1)}, u32[]{:S(2)}, u32[]{:S(2)}) %collective-permute-start.6) | collective-permute-done | bytes 16416 | tf_op jit(solution)/shard_map/ppermute | solution.py:227
  57.6 0.9 %shard_map.110 = (bf16[16,16,256]{2,1,0:T(8,128)(2,1)S(1)}, bf16[16,256]{1,0:T(8,128)(2,1)}) custom-call(s32[1]{0:T(128)} %bitcast.index, f32[2,16,128]{2,1,0:T(8,128)S(1)} %get-tuple-element.38.keep, f32[2,16,128]{2,1,0:T(8,128)S(1)} %collective-permute-done.6.came, bf16[16,256]{1,0:T(8,128)(2,1)S(1)} %get-tuple-element.40.gate_two, ...), custom_call_target="tpu_custom_call" | custom-call | flops 67108864 | bytes 1048576 | tf_op jit(solution)/shard_map/pallas_call | solution.py:327
  58.5 11.5 %all_to_all.15.arrived = bf16[16,16,256]{2,1,0:T(8,128)(2,1)S(1)} all-to-all(bf16[16,16,256]{2,1,0:T(8,128)(2,1)S(1)} %get-tuple-element.42), channel_id=1, replica_groups=mesh['ctx'=16,'chan'=16] {'chan'}, dimensions={0} | all-to-all | bytes 262144 | tf_op jit(solution)/shard_map/all_to_all | solution.py:223
  70.0 0.6 shard_map.111
  (3 shorter events, 0.1 us)
Async XLA Ops:
  0.6 10.5 %collective-permute-start = (bf16[256,2,256]{2,1,0:T(2,128)(2,1)}, bf16[256,2,256]{2,1,0:T(2,128)(2,1)S(1)}, u32[]{:S(2)}, u32[]{:S(2)}) collective-permute-start(bf16[256,2,256]{2,1,0:T(2,128)(2,1)} %refs_1_.1), channel_id=1, source_target_pairs={{16,0},{32,16},{48,32},{64,48},{80,64},{96,80},{112,96},{128,112},... | collective-permute-start | bytes 786440 | tf_op jit(solution)/shard_map/ppermute | solution.py:246
  13.0 11.4 %collective-permute-start.2 = (f32[256,128]{1,0:T(8,128)S(1)}, f32[256,128]{1,0:T(8,128)S(1)}, u32[]{:S(2)}, u32[]{:S(2)}) collective-permute-start(f32[256,128]{1,0:T(8,128)S(1)} %get-tuple-element.35), channel_id=1, source_target_pairs={{0,16},{16,0},{32,48},{48,32},{64,80},{80,64},{96,112},{112,96},{1... | collective-permute-start | bytes 393224 | tf_op jit(solution)/shard_map/ppermute | solution.py:227
  13.1 17.7 %all-to-all-start = ((bf16[16,16,256]{2,1,0:T(8,128)(2,1)}), bf16[16,16,256]{2,1,0:T(8,128)(2,1)S(1)}, u32[]{:S(2)}, u32[]{:S(2)}) async-start(bf16[16,16,256]{2,1,0:T(8,128)(2,1)} %get-tuple-element.23), calls=%async_computation | async-start | bytes 262144 | tf_op jit(solution)/shard_map/all_to_all | solution.py:223
  23.5 7.2 %collective-permute-start.1 = (f32[256,128]{1,0:T(8,128)S(1)}, f32[256,128]{1,0:T(8,128)S(1)}, u32[]{:S(2)}, u32[]{:S(2)}) collective-permute-start(f32[256,128]{1,0:T(8,128)S(1)} %get-tuple-element.32), channel_id=1, source_target_pairs={{0,16},{16,0},{32,48},{48,32},{64,80},{80,64},{96,112},{112,96},{1... | collective-permute-start | bytes 393224 | tf_op jit(solution)/shard_map/ppermute | solution.py:227
  24.4 10.1 %collective-permute-start.3 = (bf16[256,128]{1,0:T(8,128)(2,1)S(1)}, bf16[256,128]{1,0:T(8,128)(2,1)S(1)}, u32[]{:S(2)}, u32[]{:S(2)}) collective-permute-start(bf16[256,128]{1,0:T(8,128)(2,1)S(1)} %add_convert_fusion.2), channel_id=1, source_target_pairs={{0,32},{16,48},{32,0},{48,16},{64,96},{80,112},{96,64},{112,80},{1... | collective-permute-start | bytes 196616 | tf_op jit(solution)/shard_map/ppermute | solution.py:227
  34.5 10.8 %collective-permute-start.4 = (bf16[256,128]{1,0:T(8,128)(2,1)S(1)}, bf16[256,128]{1,0:T(8,128)(2,1)S(1)}, u32[]{:S(2)}, u32[]{:S(2)}) collective-permute-start(bf16[256,128]{1,0:T(8,128)(2,1)S(1)} %add_convert_fusion.1), channel_id=1, source_target_pairs={{0,128},{16,144},{32,160},{48,176},{64,192},{80,208},{96,224},{112... | collective-permute-start | bytes 196616 | tf_op jit(solution)/shard_map/ppermute | solution.py:227
  37.4 16.5 %all-to-all-start.1 = ((bf16[16,48,128]{2,1,0:T(8,128)(2,1)}), bf16[16,48,128]{2,1,0:T(8,128)(2,1)S(1)}, u32[]{:S(2)}, u32[]{:S(2)}) async-start(bf16[16,48,128]{2,1,0:T(8,128)(2,1)} %get-tuple-element.36), calls=%async_computation.1 | async-start | bytes 393216 | tf_op jit(solution)/shard_map/all_to_all | solution.py:223
  45.3 5.7 %collective-permute-start.5 = (bf16[256,128]{1,0:T(8,128)(2,1)S(1)}, bf16[256,128]{1,0:T(8,128)(2,1)S(1)}, u32[]{:S(2)}, u32[]{:S(2)}) collective-permute-start(bf16[256,128]{1,0:T(8,128)(2,1)S(1)} %add_convert_fusion.here), channel_id=1, source_target_pairs={{0,64},{16,80},{32,96},{48,112},{64,0},{80,16},{96,32},{112,48},{1... | collective-permute-start | bytes 196616 | tf_op jit(solution)/shard_map/ppermute | solution.py:227
  56.4 1.3 %collective-permute-start.6 = (f32[2,16,128]{2,1,0:T(8,128)S(1)}, f32[2,16,128]{2,1,0:T(8,128)S(1)}, u32[]{:S(2)}, u32[]{:S(2)}) collective-permute-start(f32[2,16,128]{2,1,0:T(8,128)S(1)} %get-tuple-element.39), channel_id=1, source_target_pairs={{0,16},{16,0},{32,48},{48,32},{64,80},{80,64},{96,112},{112,96},{1... | collective-permute-start | bytes 49160 | tf_op jit(solution)/shard_map/ppermute | solution.py:227

commit v8 on v7

--- a/solution.py
+++ b/solution.py
@@ -88,7 +88,12 @@
         move.wait()
 
 
-def first_past_kernel(index, last, border, own, near, history, f, i, keep, send, later, spread):
+def first_past_kernel(
+    index, last, border, own, near, history, f, i, w_hbm, keep, send, later, w_head, spread, sem
+):
+    load = pltpu.make_async_copy(w_hbm.at[:, pl.ds(0, w_head.shape[1]), :], w_head, sem)
+    load.start()
+
     @pl.when(last[0] > 0)
     def _():
         spread_out(near, spread.at[1])
@@ -107,6 +112,7 @@
     send[...] = jnp.where(mine == 0, high, low)
     for n in range(3):
         later[n] = parted(spread.at[n], 2, 1)
+    load.wait()
 
 
 def second_past_kernel(index, rows, f, i, keep, send, parts):
@@ -120,14 +126,16 @@
         send[there] = parts[:, 1 - mine, :, span].reshape(half, lanes)
 
 
-def project_kernel(gathered, gain, w_hbm, keep, came, out, gate_two, w, sems):
+def project_kernel(gathered, gain, w_head, w_hbm, keep, came, out, gate_two, w, sems):
     pieces, rows, width = gathered.shape
+    ready = w_head.shape[1] // width
     steps = sems.shape[0]
-    per = pieces // steps
+    per = (pieces - ready) // steps
     copies = []
     for q in range(steps):
-        span = pl.ds(q * per * width, per * width)
-        copies.append(pltpu.make_async_copy(w_hbm.at[:, span, :], w.at[:, span, :], sems.at[q]))
+        there = pl.ds(q * per * width, per * width)
+        here = pl.ds((ready + q * per) * width, per * width)
+        copies.append(pltpu.make_async_copy(w_hbm.at[:, here, :], w.at[:, there, :], sems.at[q]))
         copies[-1].start()
     lanes = out.shape[2]
     fresh = keep.shape[0]
@@ -143,28 +151,33 @@
     scale = lax.rsqrt(mean_sq + 1e-06)
     sums = [jnp.zeros((rows, width), F32) for _ in range(3)]
     for s in range(pieces):
-        if s % per == 0:
-            copies[s // per].wait()
+        if s >= ready and (s - ready) % per == 0:
+            copies[(s - ready) // per].wait()
+        block, n = (w_head, s) if s < ready else (w, s - ready)
         g = jnp.concatenate([gain[2 * s : 2 * s + 1], gain[2 * s + 1 : 2 * s + 2]], 1)
         normed = (gathered[s].astype(F32) * scale * g).astype(BF16)
         for k in range(3):
-            sums[k] += dot(normed, w[k, s * width : (s + 1) * width, :])
+            sums[k] += dot(normed, block[k, n * width : (n + 1) * width, :])
     gate_two[...] = sums[2].astype(BF16)
     shared = jnp.concatenate([sums[0].astype(BF16), sums[1].astype(BF16)], 0)
     for d in range(out.shape[0]):
         out[d, : 2 * rows] = shared[:, (d % 2) * lanes : (d % 2 + 1) * lanes]
 
 
-def near_kernel(index, near, f, spectra, spread):
+def near_kernel(index, near, f, w_hbm, spectra, w_out, spread, sem):
+    load = pltpu.make_async_copy(w_hbm.at[:, pl.ds(0, w_out.shape[1])], w_out, sem)
+    load.start()
     lanes = spectra.shape[2]
     half = pl.ds(pl.multiple_of((index[0] % 2) * lanes, lanes), lanes)
     spread_out(near.at[:, :, half], spread)
     for which in range(2):
         spectra[which] = spectrum(f, parted(spread, 2, which))
-
-
-def mix_kernel(index, arrived, here, there, spectra, f, i, w_hbm, keep, send, w_out, gated_all, sums, sem):
-    load = pltpu.make_async_copy(w_hbm, w_out, sem)
+    load.wait()
+
+
+def mix_kernel(index, arrived, here, there, spectra, f, i, w_hbm, keep, send, w_tail, gated_all, sums, sem):
+    start = w_hbm.shape[1] - w_tail.shape[1]
+    load = pltpu.make_async_copy(w_hbm.at[:, pl.ds(start, w_tail.shape[1])], w_tail, sem)
     load.start()
     count, packed, lanes = arrived.shape
     rows = packed // 3
@@ -188,7 +201,7 @@
     load.wait()
 
 
-def finish_kernel(index, keep, came, gate_two, w_out, partial, gated):
+def finish_kernel(index, keep, came, gate_two, w_head, w_tail, partial, gated):
     first = index[0] % 2 == 0
     low, high = jnp.where(first, keep[...], came[...]), jnp.where(first, came[...], keep[...])
     both = jnp.concatenate([low, high], 2)
@@ -196,7 +209,11 @@
     mixed_in = (gate_two[...].astype(F32) * both[0]).astype(BF16)
     width = partial.shape[2]
     for d in range(partial.shape[0]):
-        partial[d] = dot(mixed_in, w_out[:, d * width : (d + 1) * width]).astype(BF16)
+        start = d * width
+        block = w_head
+        if start >= w_head.shape[1]:
+            start, block = start - w_head.shape[1], w_tail
+        partial[d] = dot(mixed_in, block[:, start : start + width]).astype(BF16)
 
 
 def total_kernel(arrived, out):
@@ -262,14 +279,15 @@
     lanes = width // 2
     half = jax.ShapeDtypeStruct((fresh, lanes), F32)
     spread = (2 * fresh, lanes)
-    keep_one, send_one, later = call(
+    head = jax.ShapeDtypeStruct((3, 3 * width, width), BF16)
+    keep_one, send_one, later, w_head = call(
         first_past_kernel,
-        (half, half, jax.ShapeDtypeStruct((3, fresh, width), BF16)),
-        [SMEM, SMEM] + [VMEM] * 6,
+        (half, half, jax.ShapeDtypeStruct((3, fresh, width), BF16), head),
+        [SMEM, SMEM] + [VMEM] * 6 + [HBM],
         unit * 9,
         2 << 20,
-        scratch=[pltpu.VMEM((3, 2, *spread), F32)],
-    )(index, last, border, own, near, past, f, i)
+        scratch=[pltpu.VMEM((3, 2, *spread), F32), pltpu.SemaphoreType.DMA],
+    )(index, last, border, own, near, past, f, i, in_hbm(w_three))
     came_one = swapped(send_one, "ctx", 1)
     keep_two, send_two = call(
         second_past_kernel,
@@ -289,11 +307,14 @@
             jax.ShapeDtypeStruct((ctx_count, 3 * rows, lanes), BF16),
             jax.ShapeDtypeStruct((rows, width), BF16),
         ),
-        [VMEM, VMEM, HBM, VMEM, VMEM],
+        [VMEM, VMEM, VMEM, HBM, VMEM, VMEM],
         2 * rows * w_in.size,
         2 * w_in.size,
-        scratch=[pltpu.VMEM(w_three.shape, BF16), pltpu.SemaphoreType.DMA((8,))],
-    )(gathered, scales, in_hbm(w_three), keep_two, came_two)
+        scratch=[
+            pltpu.VMEM((3, w_three.shape[1] - head.shape[1], width), BF16),
+            pltpu.SemaphoreType.DMA((chan_count - 3,)),
+        ],
+    )(gathered, scales, w_head, in_hbm(w_three), keep_two, came_two)
 
     here = added(here, there)
     payload, here = lax.optimization_barrier((payload, here))
@@ -301,19 +322,20 @@
     arrived = exchanged(payload, "ctx")
     here = added(here, there)
     there = swapped(here, "ctx", 4)
-    spectra = call(
+    side = jax.ShapeDtypeStruct((width, w_out.shape[1] // 2), BF16)
+    spectra, w_head = call(
         near_kernel,
-        jax.ShapeDtypeStruct((2, 2 * fresh, lanes), F32),
-        [SMEM, VMEM, VMEM],
+        (jax.ShapeDtypeStruct((2, 2 * fresh, lanes), F32), side),
+        [SMEM, VMEM, VMEM, HBM],
         unit * 2,
         2 << 20,
-        scratch=[pltpu.VMEM((1, *spread), F32)],
-    )(index, near, f)
+        scratch=[pltpu.VMEM((1, *spread), F32), pltpu.SemaphoreType.DMA],
+    )(index, near, f, in_hbm(w_out))
 
     block = jax.ShapeDtypeStruct((2, rows, lanes), F32)
-    keep, send, w_out = call(
+    keep, send, w_tail = call(
         mix_kernel,
-        (block, block, jax.ShapeDtypeStruct(w_out.shape, BF16)),
+        (block, block, side),
         [SMEM] + [VMEM] * 6 + [HBM],
         unit * 4,
         4 << 20,
@@ -330,10 +352,10 @@
             jax.ShapeDtypeStruct((chan_count, rows, width), BF16),
             jax.ShapeDtypeStruct((rows, width), BF16),
         ),
-        [SMEM] + [VMEM] * 4,
+        [SMEM] + [VMEM] * 5,
         unit,
         1 << 20,
-    )(index, keep, came, gate_two, w_out)
+    )(index, keep, came, gate_two, w_head, w_tail)
     mixed = call(
         total_kernel, jax.ShapeDtypeStruct((rows, width), BF16), [VMEM], 1 << 16, 1 << 17
     )(exchanged(partial, "chan"))

time: 71.1 us -> 70.9 us (level)
  waiting for transfers between devices: 14.1 us -> 12.2 us
  local copies, waits for them, and re-layouts: 0 us -> 1.73 us
    unnamed x0 -> x4, local copies, waits for them, and re-layouts: none -> 1.73 us
    all_to_all x2, waiting for transfers between devices: 5.57 us -> 4.46 us  [exchanged(): return lax.all_to_all(array, axis, split_axis=0, concat_axis=0, tiled=True)]
    ppermute x6, waiting for transfers between devices: 4.85 us -> 4.1 us  [swapped(): lax.ppermute(array, axis, [(i, i ^ step) for i in range(lax.axis_size(axi...]
  transfers between devices with their start and end apart: 9 -> 9, of which waited for: 5 -> 5; matrix products, arithmetic and copies ran while one was open for 0% -> 0% of each run, Pallas kernels for 10% -> 11%
where the time goes in v8:
time: 70.9 us; the launch traced here: 70.5 us
  starting transfers between devices  31.1 us (44%)
  Pallas kernels  13.2 us (19%)
  waiting for transfers between devices  12.2 us (17%)
  blocking collectives  11.4 us (16%)
  local copies, waits for them, and re-layouts  1.73 us (2%)
  between operations  0.75 us (1%)
    all_to_all x2, starting transfers between devices, exchanged(): return lax.all_to_all(array, axis, split_axis=0, concat_axis=0, tiled=True)  17.1 us
    all_to_all x1, blocking collectives, exchanged(): return lax.all_to_all(array, axis, split_axis=0, concat_axis=0, tiled=True)  11.4 us
    ppermute x6, starting transfers between devices, swapped(): lax.ppermute(array, axis, [(i, i ^ step) for i in range(lax.axis_size(axi...  8.94 us
    ppermute x1, starting transfers between devices, layer(): lax.ppermute(filt_far, 'ctx', [(i, i - 1) for i in range(1, ctx_count)])  5.11 us
    all_to_all x2, waiting for transfers between devices, exchanged(): return lax.all_to_all(array, axis, split_axis=0, concat_axis=0, tiled=True)  4.46 us
    ppermute x6, waiting for transfers between devices, swapped(): lax.ppermute(array, axis, [(i, i ^ step) for i in range(lax.axis_size(axi...  4.1 us
    ppermute x1, waiting for transfers between devices, layer(): lax.ppermute(filt_far, 'ctx', [(i, i - 1) for i in range(1, ctx_count)])  3.64 us
    pallas_call x1, Pallas kernels, layer(): call(project_kernel, (jax.ShapeDtypeStruct((ctx_count, 3 * rows, lanes),...  3.41 us
  transfers between devices with their start and end apart: 9, of which 5 were waited for; matrix products, arithmetic and copies ran while one was open for 0% of the time, Pallas kernels for 11%

profile of v8, /device:TPU:1, one launch (start us, length us, event | category | flops | bytes accessed | tf_op | source)
XLA Modules:
  0.0 70.5 jit_solution(3739876766743978746)
XLA Ops:
  0.6 5.1 %collective-permute-start = (bf16[256,2,256]{2,1,0:T(2,128)(2,1)}, bf16[256,2,256]{2,1,0:T(2,128)(2,1)S(1)}, u32[]{:S(2)}, u32[]{:S(2)}) collective-permute-start(bf16[256,2,256]{2,1,0:T(2,128)(2,1)} %refs_1_.1), channel_id=1, source_target_pairs={{16,0},{32,16},{48,32},{64,48},{80,64},{96,80},{112,96},{128,112},... | collective-permute-start | bytes 786440 | tf_op jit(solution)/shard_map/ppermute | solution.py:263
  5.7 1.7 %shard_map.104 = (bf16[16,16,256]{2,1,0:T(8,128)(2,1)}, bf16[256,2,256]{2,1,0:T(2,128)(2,1)S(1)}, bf16[256,2,256]{2,1,0:T(2,128)(2,1)S(1)}, bf16[256,2,256]{2,1,...) custom-call(bf16[16,256]{1,0:T(8,128)(2,1)} %refs_0_.1, ...), custom_call_target="tpu_custom_call" | custom-call | flops 1024 | bytes 2097152 | tf_op jit(solution)/shard_map/pallas_call | solution.py:265
  7.4 3.6 %collective-permute-done.border = bf16[256,2,256]{2,1,0:T(2,128)(2,1)S(1)} collective-permute-done((bf16[256,2,256]{2,1,0:T(2,128)(2,1)}, bf16[256,2,256]{2,1,0:T(2,128)(2,1)S(1)}, u32[]{:S(2)}, u32[]{:S(2)}) %collective-permute-start) | collective-permute-done | bytes 262176 | tf_op jit(solution)/shard_map/ppermute | solution.py:263
  11.1 1.9 %shard_map.105 = (f32[256,128]{1,0:T(8,128)S(1)}, f32[256,128]{1,0:T(8,128)S(1)}, bf16[3,256,256]{2,1,0:T(8,128)(2,1)S(1)}, bf16[3,768,256]{2,1,0:T(8,128)(2,1)S(1)}) custom-call(s32[1]{0:T(128)} %bitcast.index, s32[1]{0:T(128)S(6)} %convert_element_type.24.last, bf16[256,2,256]{2,1,0:T(2,128)(2,1)S(1)} %collective-permute-done.border, ...), custom_call_target="tpu_custom_call" | custom-call | flops 603979776 | bytes 2097152 | tf_op jit(solution)/shard_map/pallas_call | solution.py:283
  13.0 0.0 copy-start
  13.0 0.7 %copy-done = bf16[3,256,256]{2,1,0:T(8,128)(2,1)} copy-done((bf16[3,256,256]{2,1,0:T(8,128)(2,1)}, bf16[3,256,256]{2,1,0:T(8,128)(2,1)S(1)}, u32[]{:S(2)}) %copy-start) | copy-done | bytes 393240
  13.7 0.0 collective-permute-start.2
  13.7 9.1 %all-to-all-start = ((bf16[16,16,256]{2,1,0:T(8,128)(2,1)}), bf16[16,16,256]{2,1,0:T(8,128)(2,1)S(1)}, u32[]{:S(2)}, u32[]{:S(2)}) async-start(bf16[16,16,256]{2,1,0:T(8,128)(2,1)} %get-tuple-element.26), calls=%async_computation | async-start | bytes 262144 | tf_op jit(solution)/shard_map/all_to_all | solution.py:240
  22.8 0.0 copy-start.1
  22.8 1.0 %copy-done.1 = bf16[3,256,256]{2,1,0:T(8,128)(2,1)S(1)} copy-done((bf16[3,256,256]{2,1,0:T(8,128)(2,1)S(1)}, bf16[3,256,256]{2,1,0:T(8,128)(2,1)}, u32[]{:S(2)}) %copy-start.1) | copy-done | bytes 393240
  23.8 1.3 %shard_map.106 = (f32[256,128]{1,0:T(8,128)S(1)}, f32[256,128]{1,0:T(8,128)S(1)}) custom-call(s32[1]{0:T(128)} %bitcast.index, bf16[3,256,256]{2,1,0:T(8,128)(2,1)S(1)} %copy-done.1, bf16[2,512,256]{2,1,0:T(8,128)(2,1)S(1)} %get-tuple-element.31.f, bf16[2,256,512]{2,1,0:T(8,128)(2,1)S(1)} %get-tuple-element.32.i), custom_call_target="tpu_custom_call" | custom-call | flops 603979776 | bytes 1048576 | tf_op jit(solution)/shard_map/pallas_call | solution.py:292
  25.1 0.9 %collective-permute-start.1 = (f32[256,128]{1,0:T(8,128)S(1)}, f32[256,128]{1,0:T(8,128)S(1)}, u32[]{:S(2)}, u32[]{:S(2)}) collective-permute-start(f32[256,128]{1,0:T(8,128)S(1)} %get-tuple-element.36), channel_id=1, source_target_pairs={{0,16},{16,0},{32,48},{48,32},{64,80},{80,64},{96,112},{112,96},{1... | collective-permute-start | bytes 393224 | tf_op jit(solution)/shard_map/ppermute | solution.py:244
  26.0 0.0 collective-permute-done.2
  26.0 3.6 %collective-permute-start.3 = (bf16[256,128]{1,0:T(8,128)(2,1)S(1)}, bf16[256,128]{1,0:T(8,128)(2,1)S(1)}, u32[]{:S(2)}, u32[]{:S(2)}) collective-permute-start(bf16[256,128]{1,0:T(8,128)(2,1)S(1)} %add_convert_fusion.2), channel_id=1, source_target_pairs={{0,32},{16,48},{32,0},{48,16},{64,96},{80,112},{96,64},{112,80},{1... | collective-permute-start | bytes 196616 | tf_op jit(solution)/shard_map/ppermute | solution.py:244
  29.6 1.6 %all-to-all-done.gathered = bf16[16,16,256]{2,1,0:T(8,128)(2,1)S(1)} async-done(((bf16[16,16,256]{2,1,0:T(8,128)(2,1)}), bf16[16,16,256]{2,1,0:T(8,128)(2,1)S(1)}, u32[]{:S(2)}, u32[]{:S(2)}) %all-to-all-start) | async-done | bytes 131104 | tf_op jit(solution)/shard_map/all_to_all | solution.py:240
  31.3 0.0 collective-permute-done.1.came
  31.3 3.4 %shard_map.107 = (bf16[16,48,128]{2,1,0:T(8,128)(2,1)}, bf16[16,256]{1,0:T(8,128)(2,1)S(1)}) custom-call(bf16[16,16,256]{2,1,0:T(8,128)(2,1)S(1)} %all-to-all-done.gathered, f32[32,128]{1,0:T(8,128)S(1)} %get-tuple-element.27.gain, bf16[3,768,256]{2,1,0:T(8,128)(2,1)S(1)} %get-tuple-element.33.w_head, bf16[3,4096,256]{2,1,0:T(8,128)(2,1)} %bitcast.4, ...), custom_call_target="tpu_custom_call" | custom-call | flops 100663296 | bytes 6291456 | tf_op jit(solution)/shard_map/pallas_call | solution.py:304
  34.7 0.0 collective-permute-done.3
  34.7 2.8 %collective-permute-start.4 = (bf16[256,128]{1,0:T(8,128)(2,1)S(1)}, bf16[256,128]{1,0:T(8,128)(2,1)S(1)}, u32[]{:S(2)}, u32[]{:S(2)}) collective-permute-start(bf16[256,128]{1,0:T(8,128)(2,1)S(1)} %add_convert_fusion.1), channel_id=1, source_target_pairs={{0,128},{16,144},{32,160},{48,176},{64,192},{80,208},{96,224},{112... | collective-permute-start | bytes 196616 | tf_op jit(solution)/shard_map/ppermute | solution.py:244
  37.6 8.0 %all-to-all-start.1 = ((bf16[16,48,128]{2,1,0:T(8,128)(2,1)}), bf16[16,48,128]{2,1,0:T(8,128)(2,1)S(1)}, u32[]{:S(2)}, u32[]{:S(2)}) async-start(bf16[16,48,128]{2,1,0:T(8,128)(2,1)} %get-tuple-element.40), calls=%async_computation.1 | async-start | bytes 393216 | tf_op jit(solution)/shard_map/all_to_all | solution.py:240
  45.6 0.0 collective-permute-done.4
  45.6 1.4 %collective-permute-start.5 = (bf16[256,128]{1,0:T(8,128)(2,1)S(1)}, bf16[256,128]{1,0:T(8,128)(2,1)S(1)}, u32[]{:S(2)}, u32[]{:S(2)}) collective-permute-start(bf16[256,128]{1,0:T(8,128)(2,1)S(1)} %add_convert_fusion.here), channel_id=1, source_target_pairs={{0,64},{16,80},{32,96},{48,112},{64,0},{80,16},{96,32},{112,48},{1... | collective-permute-start | bytes 196616 | tf_op jit(solution)/shard_map/ppermute | solution.py:244
  47.1 1.3 %shard_map.108 = (f32[2,512,128]{2,1,0:T(8,128)S(1)}, bf16[256,2048]{1,0:T(8,128)(2,1)S(1)}) custom-call(s32[1]{0:T(128)} %bitcast.index, bf16[256,2,256]{2,1,0:T(2,128)(2,1)S(1)} %get-tuple-element.29.near, bf16[2,512,256]{2,1,0:T(8,128)(2,1)S(1)} %get-tuple-element.31.f, bf16[256,4096]{1,0:T(8,128)(2,1)} %w_hbm.3), custom_call_target="tpu_custom_call" | custom-call | flops 134217728 | bytes 2097152 | tf_op jit(solution)/shard_map/pallas_call | solution.py:326
  48.3 3.0 %collective-permute-done.5.there = bf16[256,128]{1,0:T(8,128)(2,1)S(1)} collective-permute-done((bf16[256,128]{1,0:T(8,128)(2,1)S(1)}, bf16[256,128]{1,0:T(8,128)(2,1)S(1)}, u32[]{:S(2)}, u32[]{:S(2)}) %collective-permute-start.5) | collective-permute-done | bytes 65568 | tf_op jit(solution)/shard_map/ppermute | solution.py:244
  51.3 2.8 %all-to-all-done.1.arrived = bf16[16,48,128]{2,1,0:T(8,128)(2,1)S(1)} async-done(((bf16[16,48,128]{2,1,0:T(8,128)(2,1)}), bf16[16,48,128]{2,1,0:T(8,128)(2,1)S(1)}, u32[]{:S(2)}, u32[]{:S(2)}) %all-to-all-start.1) | async-done | bytes 196640 | tf_op jit(solution)/shard_map/all_to_all | solution.py:240
  54.2 2.1 %shard_map.109 = (f32[2,16,128]{2,1,0:T(8,128)S(1)}, f32[2,16,128]{2,1,0:T(8,128)S(1)}, bf16[256,2048]{1,0:T(8,128)(2,1)S(1)}) custom-call(s32[1]{0:T(128)} %bitcast.index, bf16[16,48,128]{2,1,0:T(8,128)(2,1)S(1)} %all-to-all-done.1.arrived, bf16[256,128]{1,0:T(8,128)(2,1)S(1)} %add_convert_fusion.here, bf16[256,128]{1,0:T(8,128)(2,1)S(1)} %collective-permute-done.5.there, ...), custom_call_target="tpu_custom_call" | custom-call | flops 268435456 | bytes 4194304 | tf_op jit(solution)/shard_map/pallas_call | solution.py:336
  56.3 0.2 collective-permute-start.6
  56.5 1.1 %collective-permute-done.6.came = f32[2,16,128]{2,1,0:T(8,128)S(1)} collective-permute-done((f32[2,16,128]{2,1,0:T(8,128)S(1)}, f32[2,16,128]{2,1,0:T(8,128)S(1)}, u32[]{:S(2)}, u32[]{:S(2)}) %collective-permute-start.6) | collective-permute-done | bytes 16416 | tf_op jit(solution)/shard_map/ppermute | solution.py:244
  57.6 0.9 %shard_map.110 = (bf16[16,16,256]{2,1,0:T(8,128)(2,1)S(1)}, bf16[16,256]{1,0:T(8,128)(2,1)}) custom-call(s32[1]{0:T(128)} %bitcast.index, f32[2,16,128]{2,1,0:T(8,128)S(1)} %get-tuple-element.43.keep, f32[2,16,128]{2,1,0:T(8,128)S(1)} %collective-permute-done.6.came, bf16[16,256]{1,0:T(8,128)(2,1)S(1)} %get-tuple-element.45.gate_two, ...), custom_call_target="tpu_custom_call" | custom-call | flops 67108864 | bytes 1048576 | tf_op jit(solution)/shard_map/pallas_call | solution.py:349
  58.4 11.4 %all_to_all.15.arrived = bf16[16,16,256]{2,1,0:T(8,128)(2,1)S(1)} all-to-all(bf16[16,16,256]{2,1,0:T(8,128)(2,1)S(1)} %get-tuple-element.48), channel_id=1, replica_groups=mesh['ctx'=16,'chan'=16] {'chan'}, dimensions={0} | all-to-all | bytes 262144 | tf_op jit(solution)/shard_map/all_to_all | solution.py:240
  69.8 0.6 shard_map.111
  (3 shorter events, 0.1 us)
Async XLA Ops:
  0.6 10.5 %collective-permute-start = (bf16[256,2,256]{2,1,0:T(2,128)(2,1)}, bf16[256,2,256]{2,1,0:T(2,128)(2,1)S(1)}, u32[]{:S(2)}, u32[]{:S(2)}) collective-permute-start(bf16[256,2,256]{2,1,0:T(2,128)(2,1)} %refs_1_.1), channel_id=1, source_target_pairs={{16,0},{32,16},{48,32},{64,48},{80,64},{96,80},{112,96},{128,112},... | collective-permute-start | bytes 786440 | tf_op jit(solution)/shard_map/ppermute | solution.py:263
  13.0 0.7 %copy-start = (bf16[3,256,256]{2,1,0:T(8,128)(2,1)}, bf16[3,256,256]{2,1,0:T(8,128)(2,1)S(1)}, u32[]{:S(2)}) copy-start(bf16[3,256,256]{2,1,0:T(8,128)(2,1)S(1)} %get-tuple-element.34.rows) | copy-start | bytes 1179652
  13.7 12.3 %collective-permute-start.2 = (f32[256,128]{1,0:T(8,128)S(1)}, f32[256,128]{1,0:T(8,128)S(1)}, u32[]{:S(2)}, u32[]{:S(2)}) collective-permute-start(f32[256,128]{1,0:T(8,128)S(1)} %get-tuple-element.39), channel_id=1, source_target_pairs={{0,16},{16,0},{32,48},{48,32},{64,80},{80,64},{96,112},{112,96},{1... | collective-permute-start | bytes 393224 | tf_op jit(solution)/shard_map/ppermute | solution.py:244
  13.7 17.5 %all-to-all-start = ((bf16[16,16,256]{2,1,0:T(8,128)(2,1)}), bf16[16,16,256]{2,1,0:T(8,128)(2,1)S(1)}, u32[]{:S(2)}, u32[]{:S(2)}) async-start(bf16[16,16,256]{2,1,0:T(8,128)(2,1)} %get-tuple-element.26), calls=%async_computation | async-start | bytes 262144 | tf_op jit(solution)/shard_map/all_to_all | solution.py:240
  22.8 1.0 %copy-start.1 = (bf16[3,256,256]{2,1,0:T(8,128)(2,1)S(1)}, bf16[3,256,256]{2,1,0:T(8,128)(2,1)}, u32[]{:S(2)}) copy-start(bf16[3,256,256]{2,1,0:T(8,128)(2,1)} %copy-done) | copy-start | bytes 1179652
  25.1 6.1 %collective-permute-start.1 = (f32[256,128]{1,0:T(8,128)S(1)}, f32[256,128]{1,0:T(8,128)S(1)}, u32[]{:S(2)}, u32[]{:S(2)}) collective-permute-start(f32[256,128]{1,0:T(8,128)S(1)} %get-tuple-element.36), channel_id=1, source_target_pairs={{0,16},{16,0},{32,48},{48,32},{64,80},{80,64},{96,112},{112,96},{1... | collective-permute-start | bytes 393224 | tf_op jit(solution)/shard_map/ppermute | solution.py:244
  26.0 8.7 %collective-permute-start.3 = (bf16[256,128]{1,0:T(8,128)(2,1)S(1)}, bf16[256,128]{1,0:T(8,128)(2,1)S(1)}, u32[]{:S(2)}, u32[]{:S(2)}) collective-permute-start(bf16[256,128]{1,0:T(8,128)(2,1)S(1)} %add_convert_fusion.2), channel_id=1, source_target_pairs={{0,32},{16,48},{32,0},{48,16},{64,96},{80,112},{96,64},{112,80},{1... | collective-permute-start | bytes 196616 | tf_op jit(solution)/shard_map/ppermute | solution.py:244
  34.7 10.9 %collective-permute-start.4 = (bf16[256,128]{1,0:T(8,128)(2,1)S(1)}, bf16[256,128]{1,0:T(8,128)(2,1)S(1)}, u32[]{:S(2)}, u32[]{:S(2)}) collective-permute-start(bf16[256,128]{1,0:T(8,128)(2,1)S(1)} %add_convert_fusion.1), channel_id=1, source_target_pairs={{0,128},{16,144},{32,160},{48,176},{64,192},{80,208},{96,224},{112... | collective-permute-start | bytes 196616 | tf_op jit(solution)/shard_map/ppermute | solution.py:244
  37.6 16.6 %all-to-all-start.1 = ((bf16[16,48,128]{2,1,0:T(8,128)(2,1)}), bf16[16,48,128]{2,1,0:T(8,128)(2,1)S(1)}, u32[]{:S(2)}, u32[]{:S(2)}) async-start(bf16[16,48,128]{2,1,0:T(8,128)(2,1)} %get-tuple-element.40), calls=%async_computation.1 | async-start | bytes 393216 | tf_op jit(solution)/shard_map/all_to_all | solution.py:240
  45.6 5.7 %collective-permute-start.5 = (bf16[256,128]{1,0:T(8,128)(2,1)S(1)}, bf16[256,128]{1,0:T(8,128)(2,1)S(1)}, u32[]{:S(2)}, u32[]{:S(2)}) collective-permute-start(bf16[256,128]{1,0:T(8,128)(2,1)S(1)} %add_convert_fusion.here), channel_id=1, source_target_pairs={{0,64},{16,80},{32,96},{48,112},{64,0},{80,16},{96,32},{112,48},{1... | collective-permute-start | bytes 196616 | tf_op jit(solution)/shard_map/ppermute | solution.py:244
  56.3 1.3 %collective-permute-start.6 = (f32[2,16,128]{2,1,0:T(8,128)S(1)}, f32[2,16,128]{2,1,0:T(8,128)S(1)}, u32[]{:S(2)}, u32[]{:S(2)}) collective-permute-start(f32[2,16,128]{2,1,0:T(8,128)S(1)} %get-tuple-element.44), channel_id=1, source_target_pairs={{0,16},{16,0},{32,48},{48,32},{64,80},{80,64},{96,112},{112,96},{1... | collective-permute-start | bytes 49160 | tf_op jit(solution)/shard_map/ppermute | solution.py:244

commit v9 on v8

--- a/solution.py
+++ b/solution.py
@@ -74,17 +74,13 @@
     return back_to_time(i[0], i[1], times_conjugate(window, spectrum(f, history)))
 
 
-def open_kernel(*refs):
-    (inputs, *loads), (copies, *kept), (held, sems) = refs[:7], refs[7:14], refs[14:]
-    moves = [pltpu.make_async_copy(a, b, sems.at[n]) for n, (a, b) in enumerate(zip([inputs, *loads], [held, *kept]))]
+def open_kernel(inputs, *refs):
+    loads, copies, kept, sems = refs[:6], refs[6], refs[7:13], refs[13]
+    pairs = [(inputs, copies.at[d]) for d in range(copies.shape[0])] + list(zip(loads, kept))
+    moves = [pltpu.make_async_copy(a, b, sems.at[n]) for n, (a, b) in enumerate(pairs)]
     for move in moves:
         move.start()
-    moves[0].wait()
-    count = copies.shape[0]
-    sent = [pltpu.make_async_copy(held, copies.at[d], sems.at[len(moves) + d]) for d in range(count)]
-    for move in sent:
-        move.start()
-    for move in moves[1:] + sent:
+    for move in moves:
         move.wait()
 
 
@@ -271,7 +267,7 @@
         [HBM] * 7,
         1 << 10,
         1 << 21,
-        scratch=[pltpu.VMEM((rows, width), BF16), pltpu.SemaphoreType.DMA((7 + chan_count,))],
+        scratch=[pltpu.SemaphoreType.DMA((6 + chan_count,))],
         out_specs=(pl.BlockSpec(memory_space=pl.ANY), *[VMEM] * 6),
     )(*(in_hbm(a) for a in (inputs, *loads)))
     gathered = exchanged(copies, "chan")
@@ -299,7 +295,7 @@
     )(index, later, f, i)
     came_two = swapped(send_two, "ctx", 1)
     here = added(keep_one, came_one)
-    there = swapped(here, "ctx", 2)
+    there = swapped(here, "ctx", 4)
 
     payload, gate_two = call(
         project_kernel,
@@ -318,10 +314,10 @@
 
     here = added(here, there)
     payload, here = lax.optimization_barrier((payload, here))
-    there = swapped(here, "ctx", 8)
+    there = swapped(here, "ctx", 2)
     arrived = exchanged(payload, "ctx")
     here = added(here, there)
-    there = swapped(here, "ctx", 4)
+    there = swapped(here, "ctx", 8)
     side = jax.ShapeDtypeStruct((width, w_out.shape[1] // 2), BF16)
     spectra, w_head = call(
         near_kernel,

time: 70.9 us -> 70.4 us (level)
  Pallas kernels: 13.2 us -> 16.8 us
  waiting for transfers between devices: 12.2 us -> 9.38 us
  starting transfers between devices: 31.1 us -> 29.8 us
    ppermute x1, waiting for transfers between devices: 3.64 us -> 0.04 us  [layer(): lax.ppermute(filt_far, 'ctx', [(i, i - 1) for i in range(1, ctx_count)])]
    pallas_call x1, Pallas kernels: 1.69 us -> 5.29 us  [layer(): call(open_kernel, (jax.ShapeDtypeStruct((chan_count, rows, width), BF16),...]
    all_to_all x2, starting transfers between devices: 17.1 us -> 15.8 us  [exchanged(): return lax.all_to_all(array, axis, split_axis=0, concat_axis=0, tiled=True)]
    all_to_all x2, waiting for transfers between devices: 4.46 us -> 5.25 us  [exchanged(): return lax.all_to_all(array, axis, split_axis=0, concat_axis=0, tiled=True)]
  transfers between devices with their start and end apart: 9 -> 9, of which waited for: 5 -> 4; matrix products, arithmetic and copies ran while one was open for 0% -> 0% of each run, Pallas kernels for 11% -> 16%
where the time goes in v9:
time: 70.4 us; the launch traced here: 70 us
  starting transfers between devices  29.8 us (42%)
  Pallas kernels  16.8 us (24%)
  blocking collectives  11.5 us (16%)
  waiting for transfers between devices  9.38 us (13%)
  local copies, waits for them, and re-layouts  1.73 us (2%)
  between operations  0.75 us (1%)
    all_to_all x2, starting transfers between devices, exchanged(): return lax.all_to_all(array, axis, split_axis=0, concat_axis=0, tiled=True)  15.8 us
    all_to_all x1, blocking collectives, exchanged(): return lax.all_to_all(array, axis, split_axis=0, concat_axis=0, tiled=True)  11.5 us
    ppermute x6, starting transfers between devices, swapped(): lax.ppermute(array, axis, [(i, i ^ step) for i in range(lax.axis_size(axi...  8.93 us
    pallas_call x1, Pallas kernels, layer(): call(open_kernel, (jax.ShapeDtypeStruct((chan_count, rows, width), BF16),...  5.29 us
    all_to_all x2, waiting for transfers between devices, exchanged(): return lax.all_to_all(array, axis, split_axis=0, concat_axis=0, tiled=True)  5.25 us
    ppermute x1, starting transfers between devices, layer(): lax.ppermute(filt_far, 'ctx', [(i, i - 1) for i in range(1, ctx_count)])  5.11 us
    ppermute x6, waiting for transfers between devices, swapped(): lax.ppermute(array, axis, [(i, i ^ step) for i in range(lax.axis_size(axi...  4.09 us
    pallas_call x1, Pallas kernels, layer(): call(project_kernel, (jax.ShapeDtypeStruct((ctx_count, 3 * rows, lanes),...  3.41 us
  transfers between devices with their start and end apart: 9, of which 4 were waited for; matrix products, arithmetic and copies ran while one was open for 0% of the time, Pallas kernels for 16%

profile of v9, /device:TPU:1, one launch (start us, length us, event | category | flops | bytes accessed | tf_op | source)
XLA Modules:
  0.0 70.0 jit_solution(14211820575619988378)
XLA Ops:
  0.6 5.1 %collective-permute-start = (bf16[256,2,256]{2,1,0:T(2,128)(2,1)}, bf16[256,2,256]{2,1,0:T(2,128)(2,1)S(1)}, u32[]{:S(2)}, u32[]{:S(2)}) collective-permute-start(bf16[256,2,256]{2,1,0:T(2,128)(2,1)} %refs_0_.1), channel_id=1, source_target_pairs={{16,0},{32,16},{48,32},{64,48},{80,64},{96,80},{112,96},{128,112},... | collective-permute-start | bytes 786440 | tf_op jit(solution)/shard_map/ppermute | solution.py:259
  5.7 5.3 %shard_map.104 = (bf16[16,16,256]{2,1,0:T(8,128)(2,1)}, bf16[256,2,256]{2,1,0:T(2,128)(2,1)S(1)}, bf16[256,2,256]{2,1,0:T(2,128)(2,1)S(1)}, bf16[256,2,256]{2,1,...) custom-call(bf16[16,256]{1,0:T(8,128)(2,1)} %inputs.1, ...), custom_call_target="tpu_custom_call" | custom-call | flops 1024 | bytes 2097152 | tf_op jit(solution)/shard_map/pallas_call | solution.py:261
  11.0 0.0 collective-permute-done.border
  11.1 1.9 %shard_map.105 = (f32[256,128]{1,0:T(8,128)S(1)}, f32[256,128]{1,0:T(8,128)S(1)}, bf16[3,256,256]{2,1,0:T(8,128)(2,1)S(1)}, bf16[3,768,256]{2,1,0:T(8,128)(2,1)S(1)}) custom-call(s32[1]{0:T(128)} %bitcast.index, s32[1]{0:T(128)S(6)} %convert_element_type.24.last, bf16[256,2,256]{2,1,0:T(2,128)(2,1)S(1)} %collective-permute-done.border, ...), custom_call_target="tpu_custom_call" | custom-call | flops 603979776 | bytes 2097152 | tf_op jit(solution)/shard_map/pallas_call | solution.py:279
  13.0 0.0 copy-start
  13.0 0.7 %copy-done = bf16[3,256,256]{2,1,0:T(8,128)(2,1)} copy-done((bf16[3,256,256]{2,1,0:T(8,128)(2,1)}, bf16[3,256,256]{2,1,0:T(8,128)(2,1)S(1)}, u32[]{:S(2)}) %copy-start) | copy-done | bytes 393240
  13.7 0.0 collective-permute-start.2
  13.7 9.1 %all-to-all-start = ((bf16[16,16,256]{2,1,0:T(8,128)(2,1)}), bf16[16,16,256]{2,1,0:T(8,128)(2,1)S(1)}, u32[]{:S(2)}, u32[]{:S(2)}) async-start(bf16[16,16,256]{2,1,0:T(8,128)(2,1)} %get-tuple-element.26), calls=%async_computation | async-start | bytes 262144 | tf_op jit(solution)/shard_map/all_to_all | solution.py:236
  22.8 0.0 copy-start.1
  22.8 1.0 %copy-done.1 = bf16[3,256,256]{2,1,0:T(8,128)(2,1)S(1)} copy-done((bf16[3,256,256]{2,1,0:T(8,128)(2,1)S(1)}, bf16[3,256,256]{2,1,0:T(8,128)(2,1)}, u32[]{:S(2)}) %copy-start.1) | copy-done | bytes 393240
  23.8 1.3 %shard_map.106 = (f32[256,128]{1,0:T(8,128)S(1)}, f32[256,128]{1,0:T(8,128)S(1)}) custom-call(s32[1]{0:T(128)} %bitcast.index, bf16[3,256,256]{2,1,0:T(8,128)(2,1)S(1)} %copy-done.1, bf16[2,512,256]{2,1,0:T(8,128)(2,1)S(1)} %get-tuple-element.31.f, bf16[2,256,512]{2,1,0:T(8,128)(2,1)S(1)} %get-tuple-element.32.i), custom_call_target="tpu_custom_call" | custom-call | flops 603979776 | bytes 1048576 | tf_op jit(solution)/shard_map/pallas_call | solution.py:288
  25.1 0.9 %collective-permute-start.1 = (f32[256,128]{1,0:T(8,128)S(1)}, f32[256,128]{1,0:T(8,128)S(1)}, u32[]{:S(2)}, u32[]{:S(2)}) collective-permute-start(f32[256,128]{1,0:T(8,128)S(1)} %get-tuple-element.36), channel_id=1, source_target_pairs={{0,16},{16,0},{32,48},{48,32},{64,80},{80,64},{96,112},{112,96},{1... | collective-permute-start | bytes 393224 | tf_op jit(solution)/shard_map/ppermute | solution.py:240
  26.0 0.0 collective-permute-done.2
  26.0 1.3 %collective-permute-start.3 = (bf16[256,128]{1,0:T(8,128)(2,1)S(1)}, bf16[256,128]{1,0:T(8,128)(2,1)S(1)}, u32[]{:S(2)}, u32[]{:S(2)}) collective-permute-start(bf16[256,128]{1,0:T(8,128)(2,1)S(1)} %add_convert_fusion.2), channel_id=1, source_target_pairs={{0,64},{16,80},{32,96},{48,112},{64,0},{80,16},{96,32},{112,48},{1... | collective-permute-start | bytes 196616 | tf_op jit(solution)/shard_map/ppermute | solution.py:240
  27.3 3.9 %all-to-all-done.gathered = bf16[16,16,256]{2,1,0:T(8,128)(2,1)S(1)} async-done(((bf16[16,16,256]{2,1,0:T(8,128)(2,1)}), bf16[16,16,256]{2,1,0:T(8,128)(2,1)S(1)}, u32[]{:S(2)}, u32[]{:S(2)}) %all-to-all-start) | async-done | bytes 131104 | tf_op jit(solution)/shard_map/all_to_all | solution.py:236
  31.3 0.0 collective-permute-done.1.came
  31.3 3.4 %shard_map.107 = (bf16[16,48,128]{2,1,0:T(8,128)(2,1)}, bf16[16,256]{1,0:T(8,128)(2,1)S(1)}) custom-call(bf16[16,16,256]{2,1,0:T(8,128)(2,1)S(1)} %all-to-all-done.gathered, f32[32,128]{1,0:T(8,128)S(1)} %get-tuple-element.27.gain, bf16[3,768,256]{2,1,0:T(8,128)(2,1)S(1)} %get-tuple-element.33.w_head, bf16[3,4096,256]{2,1,0:T(8,128)(2,1)} %bitcast.4, ...), custom_call_target="tpu_custom_call" | custom-call | flops 100663296 | bytes 6291456 | tf_op jit(solution)/shard_map/pallas_call | solution.py:300
  34.7 0.0 collective-permute-done.3
  34.7 3.6 %collective-permute-start.4 = (bf16[256,128]{1,0:T(8,128)(2,1)S(1)}, bf16[256,128]{1,0:T(8,128)(2,1)S(1)}, u32[]{:S(2)}, u32[]{:S(2)}) collective-permute-start(bf16[256,128]{1,0:T(8,128)(2,1)S(1)} %add_convert_fusion.1), channel_id=1, source_target_pairs={{0,32},{16,48},{32,0},{48,16},{64,96},{80,112},{96,64},{112,80},{1... | collective-permute-start | bytes 196616 | tf_op jit(solution)/shard_map/ppermute | solution.py:240
  38.3 6.7 %all-to-all-start.1 = ((bf16[16,48,128]{2,1,0:T(8,128)(2,1)}), bf16[16,48,128]{2,1,0:T(8,128)(2,1)S(1)}, u32[]{:S(2)}, u32[]{:S(2)}) async-start(bf16[16,48,128]{2,1,0:T(8,128)(2,1)} %get-tuple-element.40), calls=%async_computation.1 | async-start | bytes 393216 | tf_op jit(solution)/shard_map/all_to_all | solution.py:236
  45.0 0.0 collective-permute-done.4
  45.1 2.9 %collective-permute-start.5 = (bf16[256,128]{1,0:T(8,128)(2,1)S(1)}, bf16[256,128]{1,0:T(8,128)(2,1)S(1)}, u32[]{:S(2)}, u32[]{:S(2)}) collective-permute-start(bf16[256,128]{1,0:T(8,128)(2,1)S(1)} %add_convert_fusion.here), channel_id=1, source_target_pairs={{0,128},{16,144},{32,160},{48,176},{64,192},{80,208},{96,224},{112... | collective-permute-start | bytes 196616 | tf_op jit(solution)/shard_map/ppermute | solution.py:240
  48.0 1.3 %shard_map.108 = (f32[2,512,128]{2,1,0:T(8,128)S(1)}, bf16[256,2048]{1,0:T(8,128)(2,1)S(1)}) custom-call(s32[1]{0:T(128)} %bitcast.index, bf16[256,2,256]{2,1,0:T(2,128)(2,1)S(1)} %get-tuple-element.29.near, bf16[2,512,256]{2,1,0:T(8,128)(2,1)S(1)} %get-tuple-element.31.f, bf16[256,4096]{1,0:T(8,128)(2,1)} %w_hbm.3), custom_call_target="tpu_custom_call" | custom-call | flops 134217728 | bytes 2097152 | tf_op jit(solution)/shard_map/pallas_call | solution.py:322
  49.3 3.0 %collective-permute-done.5.there = bf16[256,128]{1,0:T(8,128)(2,1)S(1)} collective-permute-done((bf16[256,128]{1,0:T(8,128)(2,1)S(1)}, bf16[256,128]{1,0:T(8,128)(2,1)S(1)}, u32[]{:S(2)}, u32[]{:S(2)}) %collective-permute-start.5) | collective-permute-done | bytes 65568 | tf_op jit(solution)/shard_map/ppermute | solution.py:240
  52.3 1.3 %all-to-all-done.1.arrived = bf16[16,48,128]{2,1,0:T(8,128)(2,1)S(1)} async-done(((bf16[16,48,128]{2,1,0:T(8,128)(2,1)}), bf16[16,48,128]{2,1,0:T(8,128)(2,1)S(1)}, u32[]{:S(2)}, u32[]{:S(2)}) %all-to-all-start.1) | async-done | bytes 196640 | tf_op jit(solution)/shard_map/all_to_all | solution.py:236
  53.6 2.1 %shard_map.109 = (f32[2,16,128]{2,1,0:T(8,128)S(1)}, f32[2,16,128]{2,1,0:T(8,128)S(1)}, bf16[256,2048]{1,0:T(8,128)(2,1)S(1)}) custom-call(s32[1]{0:T(128)} %bitcast.index, bf16[16,48,128]{2,1,0:T(8,128)(2,1)S(1)} %all-to-all-done.1.arrived, bf16[256,128]{1,0:T(8,128)(2,1)S(1)} %add_convert_fusion.here, bf16[256,128]{1,0:T(8,128)(2,1)S(1)} %collective-permute-done.5.there, ...), custom_call_target="tpu_custom_call" | custom-call | flops 268435456 | bytes 4194304 | tf_op jit(solution)/shard_map/pallas_call | solution.py:332
  55.7 0.2 collective-permute-start.6
  55.9 1.1 %collective-permute-done.6.came = f32[2,16,128]{2,1,0:T(8,128)S(1)} collective-permute-done((f32[2,16,128]{2,1,0:T(8,128)S(1)}, f32[2,16,128]{2,1,0:T(8,128)S(1)}, u32[]{:S(2)}, u32[]{:S(2)}) %collective-permute-start.6) | collective-permute-done | bytes 16416 | tf_op jit(solution)/shard_map/ppermute | solution.py:240
  57.0 0.9 %shard_map.110 = (bf16[16,16,256]{2,1,0:T(8,128)(2,1)S(1)}, bf16[16,256]{1,0:T(8,128)(2,1)}) custom-call(s32[1]{0:T(128)} %bitcast.index, f32[2,16,128]{2,1,0:T(8,128)S(1)} %get-tuple-element.43.keep, f32[2,16,128]{2,1,0:T(8,128)S(1)} %collective-permute-done.6.came, bf16[16,256]{1,0:T(8,128)(2,1)S(1)} %get-tuple-element.45.gate_two, ...), custom_call_target="tpu_custom_call" | custom-call | flops 67108864 | bytes 1048576 | tf_op jit(solution)/shard_map/pallas_call | solution.py:345
  57.9 11.5 %all_to_all.15.arrived = bf16[16,16,256]{2,1,0:T(8,128)(2,1)S(1)} all-to-all(bf16[16,16,256]{2,1,0:T(8,128)(2,1)S(1)} %get-tuple-element.48), channel_id=1, replica_groups=mesh['ctx'=16,'chan'=16] {'chan'}, dimensions={0} | all-to-all | bytes 262144 | tf_op jit(solution)/shard_map/all_to_all | solution.py:236
  69.4 0.6 shard_map.111
  (3 shorter events, 0.1 us)
Async XLA Ops:
  0.6 10.5 %collective-permute-start = (bf16[256,2,256]{2,1,0:T(2,128)(2,1)}, bf16[256,2,256]{2,1,0:T(2,128)(2,1)S(1)}, u32[]{:S(2)}, u32[]{:S(2)}) collective-permute-start(bf16[256,2,256]{2,1,0:T(2,128)(2,1)} %refs_0_.1), channel_id=1, source_target_pairs={{16,0},{32,16},{48,32},{64,48},{80,64},{96,80},{112,96},{128,112},... | collective-permute-start | bytes 786440 | tf_op jit(solution)/shard_map/ppermute | solution.py:259
  13.0 0.7 %copy-start = (bf16[3,256,256]{2,1,0:T(8,128)(2,1)}, bf16[3,256,256]{2,1,0:T(8,128)(2,1)S(1)}, u32[]{:S(2)}) copy-start(bf16[3,256,256]{2,1,0:T(8,128)(2,1)S(1)} %get-tuple-element.34.rows) | copy-start | bytes 1179652
  13.7 12.3 %collective-permute-start.2 = (f32[256,128]{1,0:T(8,128)S(1)}, f32[256,128]{1,0:T(8,128)S(1)}, u32[]{:S(2)}, u32[]{:S(2)}) collective-permute-start(f32[256,128]{1,0:T(8,128)S(1)} %get-tuple-element.39), channel_id=1, source_target_pairs={{0,16},{16,0},{32,48},{48,32},{64,80},{80,64},{96,112},{112,96},{1... | collective-permute-start | bytes 393224 | tf_op jit(solution)/shard_map/ppermute | solution.py:240
  13.7 17.5 %all-to-all-start = ((bf16[16,16,256]{2,1,0:T(8,128)(2,1)}), bf16[16,16,256]{2,1,0:T(8,128)(2,1)S(1)}, u32[]{:S(2)}, u32[]{:S(2)}) async-start(bf16[16,16,256]{2,1,0:T(8,128)(2,1)} %get-tuple-element.26), calls=%async_computation | async-start | bytes 262144 | tf_op jit(solution)/shard_map/all_to_all | solution.py:236
  22.8 1.0 %copy-start.1 = (bf16[3,256,256]{2,1,0:T(8,128)(2,1)S(1)}, bf16[3,256,256]{2,1,0:T(8,128)(2,1)}, u32[]{:S(2)}) copy-start(bf16[3,256,256]{2,1,0:T(8,128)(2,1)} %copy-done) | copy-start | bytes 1179652
  25.1 6.1 %collective-permute-start.1 = (f32[256,128]{1,0:T(8,128)S(1)}, f32[256,128]{1,0:T(8,128)S(1)}, u32[]{:S(2)}, u32[]{:S(2)}) collective-permute-start(f32[256,128]{1,0:T(8,128)S(1)} %get-tuple-element.36), channel_id=1, source_target_pairs={{0,16},{16,0},{32,48},{48,32},{64,80},{80,64},{96,112},{112,96},{1... | collective-permute-start | bytes 393224 | tf_op jit(solution)/shard_map/ppermute | solution.py:240
  26.0 8.7 %collective-permute-start.3 = (bf16[256,128]{1,0:T(8,128)(2,1)S(1)}, bf16[256,128]{1,0:T(8,128)(2,1)S(1)}, u32[]{:S(2)}, u32[]{:S(2)}) collective-permute-start(bf16[256,128]{1,0:T(8,128)(2,1)S(1)} %add_convert_fusion.2), channel_id=1, source_target_pairs={{0,64},{16,80},{32,96},{48,112},{64,0},{80,16},{96,32},{112,48},{1... | collective-permute-start | bytes 196616 | tf_op jit(solution)/shard_map/ppermute | solution.py:240
  34.7 10.3 %collective-permute-start.4 = (bf16[256,128]{1,0:T(8,128)(2,1)S(1)}, bf16[256,128]{1,0:T(8,128)(2,1)S(1)}, u32[]{:S(2)}, u32[]{:S(2)}) collective-permute-start(bf16[256,128]{1,0:T(8,128)(2,1)S(1)} %add_convert_fusion.1), channel_id=1, source_target_pairs={{0,32},{16,48},{32,0},{48,16},{64,96},{80,112},{96,64},{112,80},{1... | collective-permute-start | bytes 196616 | tf_op jit(solution)/shard_map/ppermute | solution.py:240
  38.3 15.3 %all-to-all-start.1 = ((bf16[16,48,128]{2,1,0:T(8,128)(2,1)}), bf16[16,48,128]{2,1,0:T(8,128)(2,1)S(1)}, u32[]{:S(2)}, u32[]{:S(2)}) async-start(bf16[16,48,128]{2,1,0:T(8,128)(2,1)} %get-tuple-element.40), calls=%async_computation.1 | async-start | bytes 393216 | tf_op jit(solution)/shard_map/all_to_all | solution.py:236
  45.1 7.2 %collective-permute-start.5 = (bf16[256,128]{1,0:T(8,128)(2,1)S(1)}, bf16[256,128]{1,0:T(8,128)(2,1)S(1)}, u32[]{:S(2)}, u32[]{:S(2)}) collective-permute-start(bf16[256,128]{1,0:T(8,128)(2,1)S(1)} %add_convert_fusion.here), channel_id=1, source_target_pairs={{0,128},{16,144},{32,160},{48,176},{64,192},{80,208},{96,224},{112... | collective-permute-start | bytes 196616 | tf_op jit(solution)/shard_map/ppermute | solution.py:240
  55.7 1.3 %collective-permute-start.6 = (f32[2,16,128]{2,1,0:T(8,128)S(1)}, f32[2,16,128]{2,1,0:T(8,128)S(1)}, u32[]{:S(2)}, u32[]{:S(2)}) collective-permute-start(f32[2,16,128]{2,1,0:T(8,128)S(1)} %get-tuple-element.44), channel_id=1, source_target_pairs={{0,16},{16,0},{32,48},{48,32},{64,80},{80,64},{96,112},{112,96},{1... | collective-permute-start | bytes 49160 | tf_op jit(solution)/shard_map/ppermute | solution.py:240

commit v10 on v8

--- a/solution.py
+++ b/solution.py
@@ -44,6 +44,14 @@
     return dot(high, upper) + dot(high, lower) + dot(low, upper)
 
 
+def near_to_time(high, product):
+    upper = product.astype(BF16)
+    lower = (product - upper.astype(F32)).astype(BF16)
+    lanes = product.shape[1]
+    both = dot(high, jnp.concatenate([upper, lower], 1))
+    return both[:, :lanes] + both[:, lanes:]
+
+
 def times_conjugate(window, signal):
     half = window.shape[0] // 2
     wc, ws = window[:half], window[half:]
@@ -74,9 +82,10 @@
     return back_to_time(i[0], i[1], times_conjugate(window, spectrum(f, history)))
 
 
-def open_kernel(*refs):
-    (inputs, *loads), (copies, *kept), (held, sems) = refs[:7], refs[7:14], refs[14:]
-    moves = [pltpu.make_async_copy(a, b, sems.at[n]) for n, (a, b) in enumerate(zip([inputs, *loads], [held, *kept]))]
+def open_kernel(inputs, *refs):
+    loads, copies, kept, held, sems = refs[:4], refs[4], refs[5:9], refs[9], refs[10]
+    pairs = [(inputs, held), *zip(loads, kept)]
+    moves = [pltpu.make_async_copy(a, b, sems.at[n]) for n, (a, b) in enumerate(pairs)]
     for move in moves:
         move.start()
     moves[0].wait()
@@ -89,10 +98,16 @@
 
 
 def first_past_kernel(
-    index, last, border, own, near, history, f, i, w_hbm, keep, send, later, w_head, spread, sem
+    index, last, border, own, history, f, near_hbm, i_hbm, w_hbm,
+    keep, send, later, i, w_head, near, spread, sems,
 ):
-    load = pltpu.make_async_copy(w_hbm.at[:, pl.ds(0, w_head.shape[1]), :], w_head, sem)
-    load.start()
+    pairs = [(near_hbm, near), (i_hbm, i), (w_hbm.at[:, pl.ds(0, w_head.shape[1]), :], w_head)]
+    loads = [pltpu.make_async_copy(a, b, sems.at[n]) for n, (a, b) in enumerate(pairs)]
+    for load in loads:
+        load.start()
+    spread_out(own, spread.at[0])
+    spread_out(history, spread.at[2])
+    loads[0].wait()
 
     @pl.when(last[0] > 0)
     def _():
@@ -102,8 +117,7 @@
     def _():
         spread_out(border, spread.at[1])
 
-    spread_out(own, spread.at[0])
-    spread_out(history, spread.at[2])
+    loads[1].wait()
     part = past_part(*(parted(spread.at[n], 2, 0) for n in range(3)), f, i)
     lanes = keep.shape[1]
     low, high = part[:, :lanes], part[:, lanes:]
@@ -112,10 +126,14 @@
     send[...] = jnp.where(mine == 0, high, low)
     for n in range(3):
         later[n] = parted(spread.at[n], 2, 1)
-    load.wait()
-
-
-def second_past_kernel(index, rows, f, i, keep, send, parts):
+    loads[2].wait()
+
+
+def second_past_kernel(index, rows, f, i, w_hbm, keep, send, w_next, parts, sem):
+    size = w_next.shape[1]
+    start = w_hbm.shape[1] - size
+    load = pltpu.make_async_copy(w_hbm.at[:, pl.ds(start, size), :], w_next, sem)
+    load.start()
     mine = index[0] % 2
     parts[...] = past_part(rows[0], rows[1], rows[2], f, i).reshape(parts.shape)
     half, lanes = keep.shape[0] // 2, keep.shape[1]
@@ -124,13 +142,15 @@
         span = slice(h * lanes, (h + 1) * lanes)
         keep[there] = parts[:, mine, :, span].reshape(half, lanes)
         send[there] = parts[:, 1 - mine, :, span].reshape(half, lanes)
-
-
-def project_kernel(gathered, gain, w_head, w_hbm, keep, came, out, gate_two, w, sems):
+    load.wait()
+
+
+def project_kernel(gathered, gain, w_head, w_next, w_hbm, keep, came, out, gate_two, w, sems):
     pieces, rows, width = gathered.shape
     ready = w_head.shape[1] // width
     steps = sems.shape[0]
-    per = (pieces - ready) // steps
+    more = w_next.shape[1] // width
+    per = (pieces - ready - more) // steps
     copies = []
     for q in range(steps):
         there = pl.ds(q * per * width, per * width)
@@ -150,10 +170,15 @@
     mean_sq = jnp.sum(total, axis=1, keepdims=True) / (pieces * width)
     scale = lax.rsqrt(mean_sq + 1e-06)
     sums = [jnp.zeros((rows, width), F32) for _ in range(3)]
-    for s in range(pieces):
-        if s >= ready and (s - ready) % per == 0:
-            copies[(s - ready) // per].wait()
-        block, n = (w_head, s) if s < ready else (w, s - ready)
+    streamed = range(ready, pieces - more)
+    for s in [*range(ready), *range(pieces - more, pieces), *streamed]:
+        block, n = w_head, s
+        if s in streamed:
+            block, n = w, s - ready
+            if n % per == 0:
+                copies[n // per].wait()
+        elif s >= ready:
+            block, n = w_next, s - (pieces - more)
         g = jnp.concatenate([gain[2 * s : 2 * s + 1], gain[2 * s + 1 : 2 * s + 2]], 1)
         normed = (gathered[s].astype(F32) * scale * g).astype(BF16)
         for k in range(3):
@@ -164,9 +189,12 @@
         out[d, : 2 * rows] = shared[:, (d % 2) * lanes : (d % 2 + 1) * lanes]
 
 
-def near_kernel(index, near, f, w_hbm, spectra, w_out, spread, sem):
-    load = pltpu.make_async_copy(w_hbm.at[:, pl.ds(0, w_out.shape[1])], w_out, sem)
+def near_kernel(index, near_hbm, f, w_hbm, spectra, w_out, near, spread, sems):
+    first = pltpu.make_async_copy(near_hbm, near, sems.at[0])
+    first.start()
+    load = pltpu.make_async_copy(w_hbm.at[:, pl.ds(0, w_out.shape[1])], w_out, sems.at[1])
     load.start()
+    first.wait()
     lanes = spectra.shape[2]
     half = pl.ds(pl.multiple_of((index[0] % 2) * lanes, lanes), lanes)
     spread_out(near.at[:, :, half], spread)
@@ -185,12 +213,12 @@
     values = arrived[:, :rows].reshape(fresh, lanes)
     gate_one = arrived[:, rows : 2 * rows].reshape(fresh, lanes).astype(F32)
     past_one = here[...].astype(F32) + there[...].astype(F32)
-    first = back_to_time(i[0], i[1], times_conjugate(spectra[0], spectrum(f, values)))
+    first = near_to_time(i[0], times_conjugate(spectra[0], dot(f[0], values)))
     gated = (gate_one * (past_one + first)).astype(BF16)
     gated_all[...] = gated
     mine = index[0] % 2
     chip = pl.ds(pl.multiple_of((index[0] - mine) * rows, 2 * rows), 2 * rows)
-    second = back_to_time(i[0, chip, :], i[1, chip, :], times_conjugate(spectra[1], spectrum(f, gated)))
+    second = near_to_time(i[0, chip, :], times_conjugate(spectra[1], dot(f[0], gated)))
     past_two = [arrived[p, 2 * rows :].astype(F32) for p in range(2)]
     for s in range(2, count):
         past_two[s % 2] += arrived[s, 2 * rows :].astype(F32)
@@ -261,18 +289,18 @@
     unit = fresh * fresh * 4 * width
     w_three = w_in.transpose(1, 0, 2)
     border = lax.ppermute(filt_far, "ctx", [(i, i - 1) for i in range(1, ctx_count)])
-    loads = (filt_far, filt_near, history, forward, inverse, gain.reshape(-1, 128))
-    copies, own, near, past, f, i, scales = call(
+    loads = (filt_far, history, forward, gain.reshape(-1, 128))
+    copies, own, past, f, scales = call(
         open_kernel,
         (
             jax.ShapeDtypeStruct((chan_count, rows, width), BF16),
             *(jax.ShapeDtypeStruct(a.shape, a.dtype) for a in loads),
         ),
-        [HBM] * 7,
+        [HBM] * 5,
         1 << 10,
         1 << 21,
-        scratch=[pltpu.VMEM((rows, width), BF16), pltpu.SemaphoreType.DMA((7 + chan_count,))],
-        out_specs=(pl.BlockSpec(memory_space=pl.ANY), *[VMEM] * 6),
+        scratch=[pltpu.VMEM((rows, width), BF16), pltpu.SemaphoreType.DMA((5 + chan_count,))],
+        out_specs=(pl.BlockSpec(memory_space=pl.ANY), *[VMEM] * 4),
     )(*(in_hbm(a) for a in (inputs, *loads)))
     gathered = exchanged(copies, "chan")
 
@@ -280,23 +308,34 @@
     half = jax.ShapeDtypeStruct((fresh, lanes), F32)
     spread = (2 * fresh, lanes)
     head = jax.ShapeDtypeStruct((3, 3 * width, width), BF16)
-    keep_one, send_one, later, w_head = call(
+    keep_one, send_one, later, i, w_head = call(
         first_past_kernel,
-        (half, half, jax.ShapeDtypeStruct((3, fresh, width), BF16), head),
-        [SMEM, SMEM] + [VMEM] * 6 + [HBM],
+        (
+            half,
+            half,
+            jax.ShapeDtypeStruct((3, fresh, width), BF16),
+            jax.ShapeDtypeStruct(inverse.shape, inverse.dtype),
+            head,
+        ),
+        [SMEM, SMEM] + [VMEM] * 4 + [HBM] * 3,
         unit * 9,
         2 << 20,
-        scratch=[pltpu.VMEM((3, 2, *spread), F32), pltpu.SemaphoreType.DMA],
-    )(index, last, border, own, near, past, f, i, in_hbm(w_three))
+        scratch=[
+            pltpu.VMEM(filt_near.shape, BF16),
+            pltpu.VMEM((3, 2, *spread), F32),
+            pltpu.SemaphoreType.DMA((3,)),
+        ],
+    )(index, last, border, own, past, f, *(in_hbm(a) for a in (filt_near, inverse, w_three)))
     came_one = swapped(send_one, "ctx", 1)
-    keep_two, send_two = call(
+    next_rows = jax.ShapeDtypeStruct((3, width, width), BF16)
+    keep_two, send_two, w_next = call(
         second_past_kernel,
-        (half, half),
-        [SMEM] + [VMEM] * 3,
+        (half, half, next_rows),
+        [SMEM] + [VMEM] * 3 + [HBM],
         unit * 9,
         1 << 20,
-        scratch=[pltpu.VMEM((ctx_count // 2, 2, rows, width), F32)],
-    )(index, later, f, i)
+        scratch=[pltpu.VMEM((ctx_count // 2, 2, rows, width), F32), pltpu.SemaphoreType.DMA],
+    )(index, later, f, i, in_hbm(w_three))
     came_two = swapped(send_two, "ctx", 1)
     here = added(keep_one, came_one)
     there = swapped(here, "ctx", 2)
@@ -307,14 +346,14 @@
             jax.ShapeDtypeStruct((ctx_count, 3 * rows, lanes), BF16),
             jax.ShapeDtypeStruct((rows, width), BF16),
         ),
-        [VMEM, VMEM, VMEM, HBM, VMEM, VMEM],
+        [VMEM] * 4 + [HBM, VMEM, VMEM],
         2 * rows * w_in.size,
         2 * w_in.size,
         scratch=[
-            pltpu.VMEM((3, w_three.shape[1] - head.shape[1], width), BF16),
-            pltpu.SemaphoreType.DMA((chan_count - 3,)),
+            pltpu.VMEM((3, w_three.shape[1] - head.shape[1] - next_rows.shape[1], width), BF16),
+            pltpu.SemaphoreType.DMA((chan_count - 4,)),
         ],
-    )(gathered, scales, w_head, in_hbm(w_three), keep_two, came_two)
+    )(gathered, scales, w_head, w_next, in_hbm(w_three), keep_two, came_two)
 
     here = added(here, there)
     payload, here = lax.optimization_barrier((payload, here))
@@ -326,11 +365,11 @@
     spectra, w_head = call(
         near_kernel,
         (jax.ShapeDtypeStruct((2, 2 * fresh, lanes), F32), side),
-        [SMEM, VMEM, VMEM, HBM],
+        [SMEM, HBM, VMEM, HBM],
         unit * 2,
         2 << 20,
-        scratch=[pltpu.VMEM((1, *spread), F32), pltpu.SemaphoreType.DMA],
-    )(index, near, f, in_hbm(w_out))
+        scratch=[pltpu.VMEM(filt_near.shape, BF16), pltpu.VMEM((1, *spread), F32), pltpu.SemaphoreType.DMA((2,))],
+    )(index, in_hbm(filt_near), f, in_hbm(w_out))
 
     block = jax.ShapeDtypeStruct((2, rows, lanes), F32)
     keep, send, w_tail = call(

time: 70.9 us -> 71.3 us (level)
  local copies, waits for them, and re-layouts: 1.73 us -> 0 us
  Pallas kernels: 13.2 us -> 14.2 us
  other arithmetic: 0.06 us -> 0.96 us
    unnamed x4 -> x0, local copies, waits for them, and re-layouts: 1.73 us -> none
    pallas_call x1, Pallas kernels: 1.88 us -> 3.16 us  [layer(): call(first_past_kernel, (half, half, jax.ShapeDtypeStruct((3, fresh, widt...]
    convert_element_type x3, other arithmetic: 0.06 us -> 0.96 us  [added(): return (a.astype(F32) + b.astype(F32)).astype(BF16)]
  transfers between devices with their start and end apart: 9 -> 9, of which waited for: 5 -> 5; matrix products, arithmetic and copies ran while one was open for 0% -> 1% of each run, Pallas kernels for 11% -> 11%
where the time goes in v10:
time: 71.3 us; the launch traced here: 70.8 us
  starting transfers between devices  31.2 us (44%)
  Pallas kernels  14.2 us (20%)
  waiting for transfers between devices  12.2 us (17%)
  blocking collectives  11.5 us (16%)
  other arithmetic  0.96 us (1%)
  between operations  0.75 us (1%)
    all_to_all x2, starting transfers between devices, exchanged(): return lax.all_to_all(array, axis, split_axis=0, concat_axis=0, tiled=True)  17.1 us
    all_to_all x1, blocking collectives, exchanged(): return lax.all_to_all(array, axis, split_axis=0, concat_axis=0, tiled=True)  11.5 us
    ppermute x6, starting transfers between devices, swapped(): lax.ppermute(array, axis, [(i, i ^ step) for i in range(lax.axis_size(axi...  9.01 us
    ppermute x1, starting transfers between devices, layer(): lax.ppermute(filt_far, 'ctx', [(i, i - 1) for i in range(1, ctx_count)])  5.11 us
    all_to_all x2, waiting for transfers between devices, exchanged(): return lax.all_to_all(array, axis, split_axis=0, concat_axis=0, tiled=True)  4.55 us
    ppermute x6, waiting for transfers between devices, swapped(): lax.ppermute(array, axis, [(i, i ^ step) for i in range(lax.axis_size(axi...  3.86 us
    ppermute x1, waiting for transfers between devices, layer(): lax.ppermute(filt_far, 'ctx', [(i, i - 1) for i in range(1, ctx_count)])  3.78 us
    pallas_call x1, Pallas kernels, layer(): call(project_kernel, (jax.ShapeDtypeStruct((ctx_count, 3 * rows, lanes),...  3.4 us
  transfers between devices with their start and end apart: 9, of which 5 were waited for; matrix products, arithmetic and copies ran while one was open for 1% of the time, Pallas kernels for 11%

profile of v10, /device:TPU:1, one launch (start us, length us, event | category | flops | bytes accessed | tf_op | source)
XLA Modules:
  0.0 70.8 jit_solution(14625565142798466150)
XLA Ops:
  0.6 5.1 %collective-permute-start = (bf16[256,2,256]{2,1,0:T(2,128)(2,1)}, bf16[256,2,256]{2,1,0:T(2,128)(2,1)S(1)}, u32[]{:S(2)}, u32[]{:S(2)}) collective-permute-start(bf16[256,2,256]{2,1,0:T(2,128)(2,1)} %refs_0_.1), channel_id=1, source_target_pairs={{16,0},{32,16},{48,32},{64,48},{80,64},{96,80},{112,96},{128,112},... | collective-permute-start | bytes 786440 | tf_op jit(solution)/shard_map/ppermute | solution.py:291
  5.7 1.5 %shard_map.104 = (bf16[16,16,256]{2,1,0:T(8,128)(2,1)}, bf16[256,2,256]{2,1,0:T(2,128)(2,1)S(1)}, bf16[256,2,256]{2,1,0:T(2,128)(2,1)S(1)}, bf16[2,512,256]{2,1,0:T(8,128)(2,1)S(1)}, f32[32,128]{1,0:T(8,128)S(1)}) custom-call(bf16[16,256]{1,0:T(8,128)(2,1)} %inputs.1, bf16[256,2,256]{2,1,0:T(2,128)(2,1)} %refs_0_.1, bf16[256,2,256]{2,1,0:T(2,128)(2,1)} %refs_1_.1, ...), custom_call_target="tpu_custom_call" | custom-call | flops 1024 | bytes 2097152 | tf_op jit(solution)/shard_map/pallas_call | solution.py:293
  7.3 3.8 %collective-permute-done.border = bf16[256,2,256]{2,1,0:T(2,128)(2,1)S(1)} collective-permute-done((bf16[256,2,256]{2,1,0:T(2,128)(2,1)}, bf16[256,2,256]{2,1,0:T(2,128)(2,1)S(1)}, u32[]{:S(2)}, u32[]{:S(2)}) %collective-permute-start) | collective-permute-done | bytes 262176 | tf_op jit(solution)/shard_map/ppermute | solution.py:291
  11.1 3.2 %shard_map.105 = (f32[256,128]{1,0:T(8,128)S(1)}, f32[256,128]{1,0:T(8,128)}, bf16[3,256,256]{2,1,0:T(8,128)(2,1)S(1)}, bf16[2,256,512]{2,1,0:T(8,128)(2,1)S(1)}, bf16[3,768,256]{2,1,0:T(8,128)(2,1)S(1)}) custom-call(s32[1]{0:T(128)} %bitcast.index, s32[1]{0:T(128)S(6)} %convert_element_type.24.last, bf16[256,2,256]{2,1,0:T(2,128)(2,1)S(1)} %collective-permute-done.border, ...), custom_call_target="tpu_custom_call" | custom-call | flops 603979776 | bytes 2097152 | tf_op jit(solution)/shard_map/pallas_call | solution.py:311
  14.3 0.1 collective-permute-start.2
  14.4 9.1 %all-to-all-start = ((bf16[16,16,256]{2,1,0:T(8,128)(2,1)}), bf16[16,16,256]{2,1,0:T(8,128)(2,1)S(1)}, u32[]{:S(2)}, u32[]{:S(2)}) async-start(bf16[16,16,256]{2,1,0:T(8,128)(2,1)} %get-tuple-element.26), calls=%async_computation | async-start | bytes 262144 | tf_op jit(solution)/shard_map/all_to_all | solution.py:268
  23.4 1.4 %shard_map.106 = (f32[256,128]{1,0:T(8,128)S(1)}, f32[256,128]{1,0:T(8,128)S(1)}, bf16[3,256,256]{2,1,0:T(8,128)(2,1)S(1)}) custom-call(s32[1]{0:T(128)} %bitcast.index, bf16[3,256,256]{2,1,0:T(8,128)(2,1)S(1)} %get-tuple-element.32.rows, bf16[2,512,256]{2,1,0:T(8,128)(2,1)S(1)} %get-tuple-element.30.f, bf16[2,256,512]{2,1,0:T(8,128)(2,1)S(1)} %get-tuple-element.33.i, ...), custom_call_target="tpu_custom_call" | custom-call | flops 603979776 | bytes 1048576 | tf_op jit(solution)/shard_map/pallas_call | solution.py:331
  24.8 0.9 %collective-permute-start.1 = (f32[256,128]{1,0:T(8,128)S(1)}, f32[256,128]{1,0:T(8,128)S(1)}, u32[]{:S(2)}, u32[]{:S(2)}) collective-permute-start(f32[256,128]{1,0:T(8,128)S(1)} %get-tuple-element.36), channel_id=1, source_target_pairs={{0,16},{16,0},{32,48},{48,32},{64,80},{80,64},{96,112},{112,96},{1... | collective-permute-start | bytes 393224 | tf_op jit(solution)/shard_map/ppermute | solution.py:272
  25.7 0.0 collective-permute-done.2
  25.7 0.9 %add_convert_fusion.2 = bf16[256,128]{1,0:T(8,128)(2,1)S(1)} fusion(f32[256,128]{1,0:T(8,128)S(1)} %get-tuple-element.38, f32[256,128]{1,0:T(8,128)} %collective-permute-done.2), kind=kLoop, calls=%fused_computation.2 | loop fusion | flops 65536 | bytes 327680 | tf_op jit(solution)/shard_map/convert_element_type | solution.py:276
  26.6 3.6 %collective-permute-start.3 = (bf16[256,128]{1,0:T(8,128)(2,1)S(1)}, bf16[256,128]{1,0:T(8,128)(2,1)S(1)}, u32[]{:S(2)}, u32[]{:S(2)}) collective-permute-start(bf16[256,128]{1,0:T(8,128)(2,1)S(1)} %add_convert_fusion.2), channel_id=1, source_target_pairs={{0,32},{16,48},{32,0},{48,16},{64,96},{80,112},{96,64},{112,80},{1... | collective-permute-start | bytes 196616 | tf_op jit(solution)/shard_map/ppermute | solution.py:272
  30.2 1.7 %all-to-all-done.gathered = bf16[16,16,256]{2,1,0:T(8,128)(2,1)S(1)} async-done(((bf16[16,16,256]{2,1,0:T(8,128)(2,1)}), bf16[16,16,256]{2,1,0:T(8,128)(2,1)S(1)}, u32[]{:S(2)}, u32[]{:S(2)}) %all-to-all-start) | async-done | bytes 131104 | tf_op jit(solution)/shard_map/all_to_all | solution.py:268
  31.9 0.0 collective-permute-done.1.came
  31.9 3.4 %shard_map.107 = (bf16[16,48,128]{2,1,0:T(8,128)(2,1)}, bf16[16,256]{1,0:T(8,128)(2,1)S(1)}) custom-call(bf16[16,16,256]{2,1,0:T(8,128)(2,1)S(1)} %all-to-all-done.gathered, f32[32,128]{1,0:T(8,128)S(1)} %get-tuple-element.27.gain, bf16[3,768,256]{2,1,0:T(8,128)(2,1)S(1)} %get-tuple-element.31.w_head, bf16[3,256,256]{2,1,0:T(8,128)(2,1)S(1)} %get-tuple-element.34.w_next, ...), custom_call_target="tpu_custom_call" | custom-call | flops 100663296 | bytes 6291456 | tf_op jit(solution)/shard_map/pallas_call | solution.py:343
  35.3 0.0 collective-permute-done.3
  35.4 2.8 %collective-permute-start.4 = (bf16[256,128]{1,0:T(8,128)(2,1)S(1)}, bf16[256,128]{1,0:T(8,128)(2,1)S(1)}, u32[]{:S(2)}, u32[]{:S(2)}) collective-permute-start(bf16[256,128]{1,0:T(8,128)(2,1)S(1)} %add_convert_fusion.1), channel_id=1, source_target_pairs={{0,128},{16,144},{32,160},{48,176},{64,192},{80,208},{96,224},{112... | collective-permute-start | bytes 196616 | tf_op jit(solution)/shard_map/ppermute | solution.py:272
  38.2 8.0 %all-to-all-start.1 = ((bf16[16,48,128]{2,1,0:T(8,128)(2,1)}), bf16[16,48,128]{2,1,0:T(8,128)(2,1)S(1)}, u32[]{:S(2)}, u32[]{:S(2)}) async-start(bf16[16,48,128]{2,1,0:T(8,128)(2,1)} %get-tuple-element.40), calls=%async_computation.1 | async-start | bytes 393216 | tf_op jit(solution)/shard_map/all_to_all | solution.py:268
  46.2 0.0 collective-permute-done.4
  46.3 1.4 %collective-permute-start.5 = (bf16[256,128]{1,0:T(8,128)(2,1)S(1)}, bf16[256,128]{1,0:T(8,128)(2,1)S(1)}, u32[]{:S(2)}, u32[]{:S(2)}) collective-permute-start(bf16[256,128]{1,0:T(8,128)(2,1)S(1)} %add_convert_fusion.here), channel_id=1, source_target_pairs={{0,64},{16,80},{32,96},{48,112},{64,0},{80,16},{96,32},{112,48},{1... | collective-permute-start | bytes 196616 | tf_op jit(solution)/shard_map/ppermute | solution.py:272
  47.7 1.5 %shard_map.108 = (f32[2,512,128]{2,1,0:T(8,128)S(1)}, bf16[256,2048]{1,0:T(8,128)(2,1)S(1)}) custom-call(s32[1]{0:T(128)} %bitcast.index, bf16[256,2,256]{2,1,0:T(2,128)(2,1)} %near_hbm.3, bf16[2,512,256]{2,1,0:T(8,128)(2,1)S(1)} %get-tuple-element.30.f, bf16[256,4096]{1,0:T(8,128)(2,1)} %w_hbm.3), custom_call_target="tpu_custom_call" | custom-call | flops 134217728 | bytes 2097152 | tf_op jit(solution)/shard_map/pallas_call | solution.py:365
  49.2 2.8 %collective-permute-done.5.there = bf16[256,128]{1,0:T(8,128)(2,1)S(1)} collective-permute-done((bf16[256,128]{1,0:T(8,128)(2,1)S(1)}, bf16[256,128]{1,0:T(8,128)(2,1)S(1)}, u32[]{:S(2)}, u32[]{:S(2)}) %collective-permute-start.5) | collective-permute-done | bytes 65568 | tf_op jit(solution)/shard_map/ppermute | solution.py:272
  52.0 2.8 %all-to-all-done.1.arrived = bf16[16,48,128]{2,1,0:T(8,128)(2,1)S(1)} async-done(((bf16[16,48,128]{2,1,0:T(8,128)(2,1)}), bf16[16,48,128]{2,1,0:T(8,128)(2,1)S(1)}, u32[]{:S(2)}, u32[]{:S(2)}) %all-to-all-start.1) | async-done | bytes 196640 | tf_op jit(solution)/shard_map/all_to_all | solution.py:268
  54.8 1.8 %shard_map.109 = (f32[2,16,128]{2,1,0:T(8,128)S(1)}, f32[2,16,128]{2,1,0:T(8,128)S(1)}, bf16[256,2048]{1,0:T(8,128)(2,1)S(1)}) custom-call(s32[1]{0:T(128)} %bitcast.index, bf16[16,48,128]{2,1,0:T(8,128)(2,1)S(1)} %all-to-all-done.1.arrived, bf16[256,128]{1,0:T(8,128)(2,1)S(1)} %add_convert_fusion.here, bf16[256,128]{1,0:T(8,128)(2,1)S(1)} %collective-permute-done.5.there, ...), custom_call_target="tpu_custom_call" | custom-call | flops 268435456 | bytes 4194304 | tf_op jit(solution)/shard_map/pallas_call | solution.py:375
  56.6 0.2 collective-permute-start.6
  56.8 1.1 %collective-permute-done.6.came = f32[2,16,128]{2,1,0:T(8,128)S(1)} collective-permute-done((f32[2,16,128]{2,1,0:T(8,128)S(1)}, f32[2,16,128]{2,1,0:T(8,128)S(1)}, u32[]{:S(2)}, u32[]{:S(2)}) %collective-permute-start.6) | collective-permute-done | bytes 16416 | tf_op jit(solution)/shard_map/ppermute | solution.py:272
  57.9 0.9 %shard_map.110 = (bf16[16,16,256]{2,1,0:T(8,128)(2,1)S(1)}, bf16[16,256]{1,0:T(8,128)(2,1)}) custom-call(s32[1]{0:T(128)} %bitcast.index, f32[2,16,128]{2,1,0:T(8,128)S(1)} %get-tuple-element.43.keep, f32[2,16,128]{2,1,0:T(8,128)S(1)} %collective-permute-done.6.came, bf16[16,256]{1,0:T(8,128)(2,1)S(1)} %get-tuple-element.45.gate_two, ...), custom_call_target="tpu_custom_call" | custom-call | flops 67108864 | bytes 1048576 | tf_op jit(solution)/shard_map/pallas_call | solution.py:388
  58.7 11.5 %all_to_all.15.arrived = bf16[16,16,256]{2,1,0:T(8,128)(2,1)S(1)} all-to-all(bf16[16,16,256]{2,1,0:T(8,128)(2,1)S(1)} %get-tuple-element.48), channel_id=1, replica_groups=mesh['ctx'=16,'chan'=16] {'chan'}, dimensions={0} | all-to-all | bytes 262144 | tf_op jit(solution)/shard_map/all_to_all | solution.py:268
  70.2 0.6 shard_map.111
  (2 shorter events, 0.0 us)
Async XLA Ops:
  0.6 10.5 %collective-permute-start = (bf16[256,2,256]{2,1,0:T(2,128)(2,1)}, bf16[256,2,256]{2,1,0:T(2,128)(2,1)S(1)}, u32[]{:S(2)}, u32[]{:S(2)}) collective-permute-start(bf16[256,2,256]{2,1,0:T(2,128)(2,1)} %refs_0_.1), channel_id=1, source_target_pairs={{16,0},{32,16},{48,32},{64,48},{80,64},{96,80},{112,96},{128,112},... | collective-permute-start | bytes 786440 | tf_op jit(solution)/shard_map/ppermute | solution.py:291
  14.3 11.4 %collective-permute-start.2 = (f32[256,128]{1,0:T(8,128)}, f32[256,128]{1,0:T(8,128)}, u32[]{:S(2)}, u32[]{:S(2)}) collective-permute-start(f32[256,128]{1,0:T(8,128)} %get-tuple-element.39), channel_id=1, source_target_pairs={{0,16},{16,0},{32,48},{48,32},{64,80},{80,64},{96,112},{112,96},{1... | collective-permute-start | bytes 393224 | tf_op jit(solution)/shard_map/ppermute | solution.py:272
  14.4 17.6 %all-to-all-start = ((bf16[16,16,256]{2,1,0:T(8,128)(2,1)}), bf16[16,16,256]{2,1,0:T(8,128)(2,1)S(1)}, u32[]{:S(2)}, u32[]{:S(2)}) async-start(bf16[16,16,256]{2,1,0:T(8,128)(2,1)} %get-tuple-element.26), calls=%async_computation | async-start | bytes 262144 | tf_op jit(solution)/shard_map/all_to_all | solution.py:268
  24.8 7.1 %collective-permute-start.1 = (f32[256,128]{1,0:T(8,128)S(1)}, f32[256,128]{1,0:T(8,128)S(1)}, u32[]{:S(2)}, u32[]{:S(2)}) collective-permute-start(f32[256,128]{1,0:T(8,128)S(1)} %get-tuple-element.36), channel_id=1, source_target_pairs={{0,16},{16,0},{32,48},{48,32},{64,80},{80,64},{96,112},{112,96},{1... | collective-permute-start | bytes 393224 | tf_op jit(solution)/shard_map/ppermute | solution.py:272
  26.6 8.7 %collective-permute-start.3 = (bf16[256,128]{1,0:T(8,128)(2,1)S(1)}, bf16[256,128]{1,0:T(8,128)(2,1)S(1)}, u32[]{:S(2)}, u32[]{:S(2)}) collective-permute-start(bf16[256,128]{1,0:T(8,128)(2,1)S(1)} %add_convert_fusion.2), channel_id=1, source_target_pairs={{0,32},{16,48},{32,0},{48,16},{64,96},{80,112},{96,64},{112,80},{1... | collective-permute-start | bytes 196616 | tf_op jit(solution)/shard_map/ppermute | solution.py:272
  35.4 10.9 %collective-permute-start.4 = (bf16[256,128]{1,0:T(8,128)(2,1)S(1)}, bf16[256,128]{1,0:T(8,128)(2,1)S(1)}, u32[]{:S(2)}, u32[]{:S(2)}) collective-permute-start(bf16[256,128]{1,0:T(8,128)(2,1)S(1)} %add_convert_fusion.1), channel_id=1, source_target_pairs={{0,128},{16,144},{32,160},{48,176},{64,192},{80,208},{96,224},{112... | collective-permute-start | bytes 196616 | tf_op jit(solution)/shard_map/ppermute | solution.py:272
  38.2 16.6 %all-to-all-start.1 = ((bf16[16,48,128]{2,1,0:T(8,128)(2,1)}), bf16[16,48,128]{2,1,0:T(8,128)(2,1)S(1)}, u32[]{:S(2)}, u32[]{:S(2)}) async-start(bf16[16,48,128]{2,1,0:T(8,128)(2,1)} %get-tuple-element.40), calls=%async_computation.1 | async-start | bytes 393216 | tf_op jit(solution)/shard_map/all_to_all | solution.py:268
  46.3 5.7 %collective-permute-start.5 = (bf16[256,128]{1,0:T(8,128)(2,1)S(1)}, bf16[256,128]{1,0:T(8,128)(2,1)S(1)}, u32[]{:S(2)}, u32[]{:S(2)}) collective-permute-start(bf16[256,128]{1,0:T(8,128)(2,1)S(1)} %add_convert_fusion.here), channel_id=1, source_target_pairs={{0,64},{16,80},{32,96},{48,112},{64,0},{80,16},{96,32},{112,48},{1... | collective-permute-start | bytes 196616 | tf_op jit(solution)/shard_map/ppermute | solution.py:272
  56.6 1.3 %collective-permute-start.6 = (f32[2,16,128]{2,1,0:T(8,128)S(1)}, f32[2,16,128]{2,1,0:T(8,128)S(1)}, u32[]{:S(2)}, u32[]{:S(2)}) collective-permute-start(f32[2,16,128]{2,1,0:T(8,128)S(1)} %get-tuple-element.44), channel_id=1, source_target_pairs={{0,16},{16,0},{32,48},{48,32},{64,80},{80,64},{96,112},{112,96},{1... | collective-permute-start | bytes 49160 | tf_op jit(solution)/shard_map/ppermute | solution.py:272

commit v11 on v8

--- a/solution.py
+++ b/solution.py
@@ -42,6 +42,14 @@
     upper = product.astype(BF16)
     lower = (product - upper.astype(F32)).astype(BF16)
     return dot(high, upper) + dot(high, lower) + dot(low, upper)
+
+
+def near_to_time(high, product):
+    upper = product.astype(BF16)
+    lower = (product - upper.astype(F32)).astype(BF16)
+    lanes = product.shape[1]
+    both = dot(high, jnp.concatenate([upper, lower], 1))
+    return both[:, :lanes] + both[:, lanes:]
 
 
 def times_conjugate(window, signal):
@@ -91,7 +99,7 @@
 def first_past_kernel(
     index, last, border, own, near, history, f, i, w_hbm, keep, send, later, w_head, spread, sem
 ):
-    load = pltpu.make_async_copy(w_hbm.at[:, pl.ds(0, w_head.shape[1]), :], w_head, sem)
+    load = pltpu.make_async_copy(w_hbm.at[0, pl.ds(0, w_head.shape[0]), :], w_head, sem)
     load.start()
 
     @pl.when(last[0] > 0)
@@ -126,16 +134,19 @@
         send[there] = parts[:, 1 - mine, :, span].reshape(half, lanes)
 
 
-def project_kernel(gathered, gain, w_head, w_hbm, keep, came, out, gate_two, w, sems):
+def project_kernel(gathered, gain, w_head, w_hbm, keep, came, out_hbm, gate_two, out, normed, w, sems, done):
     pieces, rows, width = gathered.shape
-    ready = w_head.shape[1] // width
-    steps = sems.shape[0]
-    per = (pieces - ready) // steps
+    depth = pieces * width
+    ready = w_head.shape[0]
+    step = depth // 4
+    chunks = []
+    for k in range(3):
+        edges = [*range(ready, depth, step), depth] if k == 0 else range(0, depth + 1, step)
+        chunks += [(k, a, b) for a, b in zip(edges, edges[1:])]
     copies = []
-    for q in range(steps):
-        there = pl.ds(q * per * width, per * width)
-        here = pl.ds((ready + q * per) * width, per * width)
-        copies.append(pltpu.make_async_copy(w_hbm.at[:, here, :], w.at[:, there, :], sems.at[q]))
+    for n, (k, a, b) in enumerate(chunks):
+        span = pl.ds(a, b - a)
+        copies.append(pltpu.make_async_copy(w_hbm.at[k, span, :], w.at[k, span, :], sems.at[n]))
         copies[-1].start()
     lanes = out.shape[2]
     fresh = keep.shape[0]
@@ -147,21 +158,24 @@
     for s in range(pieces):
         x = gathered[s].astype(F32)
         total += x * x
-    mean_sq = jnp.sum(total, axis=1, keepdims=True) / (pieces * width)
+    mean_sq = jnp.sum(total, axis=1, keepdims=True) / depth
     scale = lax.rsqrt(mean_sq + 1e-06)
-    sums = [jnp.zeros((rows, width), F32) for _ in range(3)]
     for s in range(pieces):
-        if s >= ready and (s - ready) % per == 0:
-            copies[(s - ready) // per].wait()
-        block, n = (w_head, s) if s < ready else (w, s - ready)
         g = jnp.concatenate([gain[2 * s : 2 * s + 1], gain[2 * s + 1 : 2 * s + 2]], 1)
-        normed = (gathered[s].astype(F32) * scale * g).astype(BF16)
-        for k in range(3):
-            sums[k] += dot(normed, block[k, n * width : (n + 1) * width, :])
+        normed[:, s * width : (s + 1) * width] = (gathered[s].astype(F32) * scale * g).astype(BF16)
+    sums = [dot(normed[:, :ready], w_head[...]), jnp.zeros((rows, width), F32), jnp.zeros((rows, width), F32)]
+    sent = pltpu.make_async_copy(out, out_hbm, done)
+    for n, (k, a, b) in enumerate(chunks):
+        copies[n].wait()
+        sums[k] += dot(normed[:, a:b], w[k, a:b, :])
+        if k < 2 and b == depth:
+            part = sums[k].astype(BF16)
+            for d in range(out.shape[0]):
+                out[d, k * rows : (k + 1) * rows] = part[:, (d % 2) * lanes : (d % 2 + 1) * lanes]
+            if k == 1:
+                sent.start()
     gate_two[...] = sums[2].astype(BF16)
-    shared = jnp.concatenate([sums[0].astype(BF16), sums[1].astype(BF16)], 0)
-    for d in range(out.shape[0]):
-        out[d, : 2 * rows] = shared[:, (d % 2) * lanes : (d % 2 + 1) * lanes]
+    sent.wait()
 
 
 def near_kernel(index, near, f, w_hbm, spectra, w_out, spread, sem):
@@ -185,12 +199,12 @@
     values = arrived[:, :rows].reshape(fresh, lanes)
     gate_one = arrived[:, rows : 2 * rows].reshape(fresh, lanes).astype(F32)
     past_one = here[...].astype(F32) + there[...].astype(F32)
-    first = back_to_time(i[0], i[1], times_conjugate(spectra[0], spectrum(f, values)))
+    first = near_to_time(i[0], times_conjugate(spectra[0], dot(f[0], values)))
     gated = (gate_one * (past_one + first)).astype(BF16)
     gated_all[...] = gated
     mine = index[0] % 2
     chip = pl.ds(pl.multiple_of((index[0] - mine) * rows, 2 * rows), 2 * rows)
-    second = back_to_time(i[0, chip, :], i[1, chip, :], times_conjugate(spectra[1], spectrum(f, gated)))
+    second = near_to_time(i[0, chip, :], times_conjugate(spectra[1], dot(f[0], gated)))
     past_two = [arrived[p, 2 * rows :].astype(F32) for p in range(2)]
     for s in range(2, count):
         past_two[s % 2] += arrived[s, 2 * rows :].astype(F32)
@@ -279,7 +293,7 @@
     lanes = width // 2
     half = jax.ShapeDtypeStruct((fresh, lanes), F32)
     spread = (2 * fresh, lanes)
-    head = jax.ShapeDtypeStruct((3, 3 * width, width), BF16)
+    head = jax.ShapeDtypeStruct((9 * width, width), BF16)
     keep_one, send_one, later, w_head = call(
         first_past_kernel,
         (half, half, jax.ShapeDtypeStruct((3, fresh, width), BF16), head),
@@ -311,9 +325,13 @@
         2 * rows * w_in.size,
         2 * w_in.size,
         scratch=[
-            pltpu.VMEM((3, w_three.shape[1] - head.shape[1], width), BF16),
-            pltpu.SemaphoreType.DMA((chan_count - 3,)),
+            pltpu.VMEM((ctx_count, 3 * rows, lanes), BF16),
+            pltpu.VMEM((rows, w_in.shape[0]), BF16),
+            pltpu.VMEM(w_three.shape, BF16),
+            pltpu.SemaphoreType.DMA((10,)),
+            pltpu.SemaphoreType.DMA,
         ],
+        out_specs=(pl.BlockSpec(memory_space=pl.ANY), VMEM),
     )(gathered, scales, w_head, in_hbm(w_three), keep_two, came_two)
 
     here = added(here, there)

time: 70.9 us -> 70.3 us (level)
  no operation moved by 1% of the time
where the time goes in v11:
time: 70.3 us; the launch traced here: 69.9 us
  starting transfers between devices  31.1 us (44%)
  Pallas kernels  12.6 us (18%)
  waiting for transfers between devices  12.2 us (17%)
  blocking collectives  11.4 us (16%)
  local copies, waits for them, and re-layouts  1.73 us (2%)
  between operations  0.75 us (1%)
    all_to_all x2, starting transfers between devices, exchanged(): return lax.all_to_all(array, axis, split_axis=0, concat_axis=0, tiled=True)  17.1 us
    all_to_all x1, blocking collectives, exchanged(): return lax.all_to_all(array, axis, split_axis=0, concat_axis=0, tiled=True)  11.4 us
    ppermute x6, starting transfers between devices, swapped(): lax.ppermute(array, axis, [(i, i ^ step) for i in range(lax.axis_size(axi...  8.94 us
    ppermute x1, starting transfers between devices, layer(): lax.ppermute(filt_far, 'ctx', [(i, i - 1) for i in range(1, ctx_count)])  5.11 us
    all_to_all x2, waiting for transfers between devices, exchanged(): return lax.all_to_all(array, axis, split_axis=0, concat_axis=0, tiled=True)  4.46 us
    ppermute x6, waiting for transfers between devices, swapped(): lax.ppermute(array, axis, [(i, i ^ step) for i in range(lax.axis_size(axi...  4.1 us
    ppermute x1, waiting for transfers between devices, layer(): lax.ppermute(filt_far, 'ctx', [(i, i - 1) for i in range(1, ctx_count)])  3.64 us
    pallas_call x1, Pallas kernels, layer(): call(project_kernel, (jax.ShapeDtypeStruct((ctx_count, 3 * rows, lanes),...  3.14 us
  transfers between devices with their start and end apart: 9, of which 5 were waited for; matrix products, arithmetic and copies ran while one was open for 0% of the time, Pallas kernels for 11%

profile of v11, /device:TPU:1, one launch (start us, length us, event | category | flops | bytes accessed | tf_op | source)
XLA Modules:
  0.0 69.9 jit_solution(8575441715669782789)
XLA Ops:
  0.6 5.1 %collective-permute-start = (bf16[256,2,256]{2,1,0:T(2,128)(2,1)}, bf16[256,2,256]{2,1,0:T(2,128)(2,1)S(1)}, u32[]{:S(2)}, u32[]{:S(2)}) collective-permute-start(bf16[256,2,256]{2,1,0:T(2,128)(2,1)} %refs_1_.1), channel_id=1, source_target_pairs={{16,0},{32,16},{48,32},{64,48},{80,64},{96,80},{112,96},{128,112},... | collective-permute-start | bytes 786440 | tf_op jit(solution)/shard_map/ppermute | solution.py:277
  5.7 1.7 %shard_map.104 = (bf16[16,16,256]{2,1,0:T(8,128)(2,1)}, bf16[256,2,256]{2,1,0:T(2,128)(2,1)S(1)}, bf16[256,2,256]{2,1,0:T(2,128)(2,1)S(1)}, bf16[256,2,256]{2,1,...) custom-call(bf16[16,256]{1,0:T(8,128)(2,1)} %refs_0_.1, ...), custom_call_target="tpu_custom_call" | custom-call | flops 1024 | bytes 2097152 | tf_op jit(solution)/shard_map/pallas_call | solution.py:279
  7.4 3.6 %collective-permute-done.border = bf16[256,2,256]{2,1,0:T(2,128)(2,1)S(1)} collective-permute-done((bf16[256,2,256]{2,1,0:T(2,128)(2,1)}, bf16[256,2,256]{2,1,0:T(2,128)(2,1)S(1)}, u32[]{:S(2)}, u32[]{:S(2)}) %collective-permute-start) | collective-permute-done | bytes 262176 | tf_op jit(solution)/shard_map/ppermute | solution.py:277
  11.1 1.9 %shard_map.105 = (f32[256,128]{1,0:T(8,128)S(1)}, f32[256,128]{1,0:T(8,128)S(1)}, bf16[3,256,256]{2,1,0:T(8,128)(2,1)S(1)}, bf16[2304,256]{1,0:T(8,128)(2,1)S(1)}) custom-call(s32[1]{0:T(128)} %bitcast.index, s32[1]{0:T(128)S(6)} %convert_element_type.24.last, bf16[256,2,256]{2,1,0:T(2,128)(2,1)S(1)} %collective-permute-done.border, ...), custom_call_target="tpu_custom_call" | custom-call | flops 603979776 | bytes 2097152 | tf_op jit(solution)/shard_map/pallas_call | solution.py:297
  13.0 0.0 copy-start
  13.0 0.7 %copy-done = bf16[3,256,256]{2,1,0:T(8,128)(2,1)} copy-done((bf16[3,256,256]{2,1,0:T(8,128)(2,1)}, bf16[3,256,256]{2,1,0:T(8,128)(2,1)S(1)}, u32[]{:S(2)}) %copy-start) | copy-done | bytes 393240
  13.7 0.0 collective-permute-start.2
  13.7 9.1 %all-to-all-start = ((bf16[16,16,256]{2,1,0:T(8,128)(2,1)}), bf16[16,16,256]{2,1,0:T(8,128)(2,1)S(1)}, u32[]{:S(2)}, u32[]{:S(2)}) async-start(bf16[16,16,256]{2,1,0:T(8,128)(2,1)} %get-tuple-element.26), calls=%async_computation | async-start | bytes 262144 | tf_op jit(solution)/shard_map/all_to_all | solution.py:254
  22.8 0.0 copy-start.1
  22.8 1.0 %copy-done.1 = bf16[3,256,256]{2,1,0:T(8,128)(2,1)S(1)} copy-done((bf16[3,256,256]{2,1,0:T(8,128)(2,1)S(1)}, bf16[3,256,256]{2,1,0:T(8,128)(2,1)}, u32[]{:S(2)}) %copy-start.1) | copy-done | bytes 393240
  23.8 1.3 %shard_map.106 = (f32[256,128]{1,0:T(8,128)S(1)}, f32[256,128]{1,0:T(8,128)S(1)}) custom-call(s32[1]{0:T(128)} %bitcast.index, bf16[3,256,256]{2,1,0:T(8,128)(2,1)S(1)} %copy-done.1, bf16[2,512,256]{2,1,0:T(8,128)(2,1)S(1)} %get-tuple-element.31.f, bf16[2,256,512]{2,1,0:T(8,128)(2,1)S(1)} %get-tuple-element.32.i), custom_call_target="tpu_custom_call" | custom-call | flops 603979776 | bytes 1048576 | tf_op jit(solution)/shard_map/pallas_call | solution.py:306
  25.1 0.9 %collective-permute-start.1 = (f32[256,128]{1,0:T(8,128)S(1)}, f32[256,128]{1,0:T(8,128)S(1)}, u32[]{:S(2)}, u32[]{:S(2)}) collective-permute-start(f32[256,128]{1,0:T(8,128)S(1)} %get-tuple-element.36), channel_id=1, source_target_pairs={{0,16},{16,0},{32,48},{48,32},{64,80},{80,64},{96,112},{112,96},{1... | collective-permute-start | bytes 393224 | tf_op jit(solution)/shard_map/ppermute | solution.py:258
  26.0 0.0 collective-permute-done.2
  26.0 3.6 %collective-permute-start.3 = (bf16[256,128]{1,0:T(8,128)(2,1)S(1)}, bf16[256,128]{1,0:T(8,128)(2,1)S(1)}, u32[]{:S(2)}, u32[]{:S(2)}) collective-permute-start(bf16[256,128]{1,0:T(8,128)(2,1)S(1)} %add_convert_fusion.2), channel_id=1, source_target_pairs={{0,32},{16,48},{32,0},{48,16},{64,96},{80,112},{96,64},{112,80},{1... | collective-permute-start | bytes 196616 | tf_op jit(solution)/shard_map/ppermute | solution.py:258
  29.6 1.6 %all-to-all-done.gathered = bf16[16,16,256]{2,1,0:T(8,128)(2,1)S(1)} async-done(((bf16[16,16,256]{2,1,0:T(8,128)(2,1)}), bf16[16,16,256]{2,1,0:T(8,128)(2,1)S(1)}, u32[]{:S(2)}, u32[]{:S(2)}) %all-to-all-start) | async-done | bytes 131104 | tf_op jit(solution)/shard_map/all_to_all | solution.py:254
  31.3 0.0 collective-permute-done.1.came
  31.3 3.1 %shard_map.107 = (bf16[16,48,128]{2,1,0:T(8,128)(2,1)}, bf16[16,256]{1,0:T(8,128)(2,1)S(1)}) custom-call(bf16[16,16,256]{2,1,0:T(8,128)(2,1)S(1)} %all-to-all-done.gathered, f32[32,128]{1,0:T(8,128)S(1)} %get-tuple-element.27.gain, bf16[2304,256]{1,0:T(8,128)(2,1)S(1)} %get-tuple-element.33.w_head, bf16[3,4096,256]{2,1,0:T(8,128)(2,1)} %bitcast.4, ...), custom_call_target="tpu_custom_call" | custom-call | flops 100663296 | bytes 6291456 | tf_op jit(solution)/shard_map/pallas_call | solution.py:318
  34.4 0.0 collective-permute-done.3
  34.5 2.8 %collective-permute-start.4 = (bf16[256,128]{1,0:T(8,128)(2,1)S(1)}, bf16[256,128]{1,0:T(8,128)(2,1)S(1)}, u32[]{:S(2)}, u32[]{:S(2)}) collective-permute-start(bf16[256,128]{1,0:T(8,128)(2,1)S(1)} %add_convert_fusion.1), channel_id=1, source_target_pairs={{0,128},{16,144},{32,160},{48,176},{64,192},{80,208},{96,224},{112... | collective-permute-start | bytes 196616 | tf_op jit(solution)/shard_map/ppermute | solution.py:258
  37.3 8.0 %all-to-all-start.1 = ((bf16[16,48,128]{2,1,0:T(8,128)(2,1)}), bf16[16,48,128]{2,1,0:T(8,128)(2,1)S(1)}, u32[]{:S(2)}, u32[]{:S(2)}) async-start(bf16[16,48,128]{2,1,0:T(8,128)(2,1)} %get-tuple-element.40), calls=%async_computation.1 | async-start | bytes 393216 | tf_op jit(solution)/shard_map/all_to_all | solution.py:254
  45.3 0.0 collective-permute-done.4
  45.4 1.4 %collective-permute-start.5 = (bf16[256,128]{1,0:T(8,128)(2,1)S(1)}, bf16[256,128]{1,0:T(8,128)(2,1)S(1)}, u32[]{:S(2)}, u32[]{:S(2)}) collective-permute-start(bf16[256,128]{1,0:T(8,128)(2,1)S(1)} %add_convert_fusion.here), channel_id=1, source_target_pairs={{0,64},{16,80},{32,96},{48,112},{64,0},{80,16},{96,32},{112,48},{1... | collective-permute-start | bytes 196616 | tf_op jit(solution)/shard_map/ppermute | solution.py:258
  46.8 1.3 %shard_map.108 = (f32[2,512,128]{2,1,0:T(8,128)S(1)}, bf16[256,2048]{1,0:T(8,128)(2,1)S(1)}) custom-call(s32[1]{0:T(128)} %bitcast.index, bf16[256,2,256]{2,1,0:T(2,128)(2,1)S(1)} %get-tuple-element.29.near, bf16[2,512,256]{2,1,0:T(8,128)(2,1)S(1)} %get-tuple-element.31.f, bf16[256,4096]{1,0:T(8,128)(2,1)} %w_hbm.3), custom_call_target="tpu_custom_call" | custom-call | flops 134217728 | bytes 2097152 | tf_op jit(solution)/shard_map/pallas_call | solution.py:344
  48.1 3.0 %collective-permute-done.5.there = bf16[256,128]{1,0:T(8,128)(2,1)S(1)} collective-permute-done((bf16[256,128]{1,0:T(8,128)(2,1)S(1)}, bf16[256,128]{1,0:T(8,128)(2,1)S(1)}, u32[]{:S(2)}, u32[]{:S(2)}) %collective-permute-start.5) | collective-permute-done | bytes 65568 | tf_op jit(solution)/shard_map/ppermute | solution.py:258
  51.1 2.8 %all-to-all-done.1.arrived = bf16[16,48,128]{2,1,0:T(8,128)(2,1)S(1)} async-done(((bf16[16,48,128]{2,1,0:T(8,128)(2,1)}), bf16[16,48,128]{2,1,0:T(8,128)(2,1)S(1)}, u32[]{:S(2)}, u32[]{:S(2)}) %all-to-all-start.1) | async-done | bytes 196640 | tf_op jit(solution)/shard_map/all_to_all | solution.py:254
  53.9 1.8 %shard_map.109 = (f32[2,16,128]{2,1,0:T(8,128)S(1)}, f32[2,16,128]{2,1,0:T(8,128)S(1)}, bf16[256,2048]{1,0:T(8,128)(2,1)S(1)}) custom-call(s32[1]{0:T(128)} %bitcast.index, bf16[16,48,128]{2,1,0:T(8,128)(2,1)S(1)} %all-to-all-done.1.arrived, bf16[256,128]{1,0:T(8,128)(2,1)S(1)} %add_convert_fusion.here, bf16[256,128]{1,0:T(8,128)(2,1)S(1)} %collective-permute-done.5.there, ...), custom_call_target="tpu_custom_call" | custom-call | flops 268435456 | bytes 4194304 | tf_op jit(solution)/shard_map/pallas_call | solution.py:354
  55.7 0.2 collective-permute-start.6
  55.9 1.1 %collective-permute-done.6.came = f32[2,16,128]{2,1,0:T(8,128)S(1)} collective-permute-done((f32[2,16,128]{2,1,0:T(8,128)S(1)}, f32[2,16,128]{2,1,0:T(8,128)S(1)}, u32[]{:S(2)}, u32[]{:S(2)}) %collective-permute-start.6) | collective-permute-done | bytes 16416 | tf_op jit(solution)/shard_map/ppermute | solution.py:258
  57.0 0.9 %shard_map.110 = (bf16[16,16,256]{2,1,0:T(8,128)(2,1)S(1)}, bf16[16,256]{1,0:T(8,128)(2,1)}) custom-call(s32[1]{0:T(128)} %bitcast.index, f32[2,16,128]{2,1,0:T(8,128)S(1)} %get-tuple-element.43.keep, f32[2,16,128]{2,1,0:T(8,128)S(1)} %collective-permute-done.6.came, bf16[16,256]{1,0:T(8,128)(2,1)S(1)} %get-tuple-element.45.gate_two, ...), custom_call_target="tpu_custom_call" | custom-call | flops 67108864 | bytes 1048576 | tf_op jit(solution)/shard_map/pallas_call | solution.py:367
  57.8 11.4 %all_to_all.15.arrived = bf16[16,16,256]{2,1,0:T(8,128)(2,1)S(1)} all-to-all(bf16[16,16,256]{2,1,0:T(8,128)(2,1)S(1)} %get-tuple-element.48), channel_id=1, replica_groups=mesh['ctx'=16,'chan'=16] {'chan'}, dimensions={0} | all-to-all | bytes 262144 | tf_op jit(solution)/shard_map/all_to_all | solution.py:254
  69.2 0.6 shard_map.111
  (3 shorter events, 0.1 us)
Async XLA Ops:
  0.6 10.5 %collective-permute-start = (bf16[256,2,256]{2,1,0:T(2,128)(2,1)}, bf16[256,2,256]{2,1,0:T(2,128)(2,1)S(1)}, u32[]{:S(2)}, u32[]{:S(2)}) collective-permute-start(bf16[256,2,256]{2,1,0:T(2,128)(2,1)} %refs_1_.1), channel_id=1, source_target_pairs={{16,0},{32,16},{48,32},{64,48},{80,64},{96,80},{112,96},{128,112},... | collective-permute-start | bytes 786440 | tf_op jit(solution)/shard_map/ppermute | solution.py:277
  13.0 0.7 %copy-start = (bf16[3,256,256]{2,1,0:T(8,128)(2,1)}, bf16[3,256,256]{2,1,0:T(8,128)(2,1)S(1)}, u32[]{:S(2)}) copy-start(bf16[3,256,256]{2,1,0:T(8,128)(2,1)S(1)} %get-tuple-element.34.rows) | copy-start | bytes 1179652
  13.7 12.3 %collective-permute-start.2 = (f32[256,128]{1,0:T(8,128)S(1)}, f32[256,128]{1,0:T(8,128)S(1)}, u32[]{:S(2)}, u32[]{:S(2)}) collective-permute-start(f32[256,128]{1,0:T(8,128)S(1)} %get-tuple-element.39), channel_id=1, source_target_pairs={{0,16},{16,0},{32,48},{48,32},{64,80},{80,64},{96,112},{112,96},{1... | collective-permute-start | bytes 393224 | tf_op jit(solution)/shard_map/ppermute | solution.py:258
  13.7 17.5 %all-to-all-start = ((bf16[16,16,256]{2,1,0:T(8,128)(2,1)}), bf16[16,16,256]{2,1,0:T(8,128)(2,1)S(1)}, u32[]{:S(2)}, u32[]{:S(2)}) async-start(bf16[16,16,256]{2,1,0:T(8,128)(2,1)} %get-tuple-element.26), calls=%async_computation | async-start | bytes 262144 | tf_op jit(solution)/shard_map/all_to_all | solution.py:254
  22.8 1.0 %copy-start.1 = (bf16[3,256,256]{2,1,0:T(8,128)(2,1)S(1)}, bf16[3,256,256]{2,1,0:T(8,128)(2,1)}, u32[]{:S(2)}) copy-start(bf16[3,256,256]{2,1,0:T(8,128)(2,1)} %copy-done) | copy-start | bytes 1179652
  25.1 6.1 %collective-permute-start.1 = (f32[256,128]{1,0:T(8,128)S(1)}, f32[256,128]{1,0:T(8,128)S(1)}, u32[]{:S(2)}, u32[]{:S(2)}) collective-permute-start(f32[256,128]{1,0:T(8,128)S(1)} %get-tuple-element.36), channel_id=1, source_target_pairs={{0,16},{16,0},{32,48},{48,32},{64,80},{80,64},{96,112},{112,96},{1... | collective-permute-start | bytes 393224 | tf_op jit(solution)/shard_map/ppermute | solution.py:258
  26.0 8.4 %collective-permute-start.3 = (bf16[256,128]{1,0:T(8,128)(2,1)S(1)}, bf16[256,128]{1,0:T(8,128)(2,1)S(1)}, u32[]{:S(2)}, u32[]{:S(2)}) collective-permute-start(bf16[256,128]{1,0:T(8,128)(2,1)S(1)} %add_convert_fusion.2), channel_id=1, source_target_pairs={{0,32},{16,48},{32,0},{48,16},{64,96},{80,112},{96,64},{112,80},{1... | collective-permute-start | bytes 196616 | tf_op jit(solution)/shard_map/ppermute | solution.py:258
  34.5 10.9 %collective-permute-start.4 = (bf16[256,128]{1,0:T(8,128)(2,1)S(1)}, bf16[256,128]{1,0:T(8,128)(2,1)S(1)}, u32[]{:S(2)}, u32[]{:S(2)}) collective-permute-start(bf16[256,128]{1,0:T(8,128)(2,1)S(1)} %add_convert_fusion.1), channel_id=1, source_target_pairs={{0,128},{16,144},{32,160},{48,176},{64,192},{80,208},{96,224},{112... | collective-permute-start | bytes 196616 | tf_op jit(solution)/shard_map/ppermute | solution.py:258
  37.3 16.6 %all-to-all-start.1 = ((bf16[16,48,128]{2,1,0:T(8,128)(2,1)}), bf16[16,48,128]{2,1,0:T(8,128)(2,1)S(1)}, u32[]{:S(2)}, u32[]{:S(2)}) async-start(bf16[16,48,128]{2,1,0:T(8,128)(2,1)} %get-tuple-element.40), calls=%async_computation.1 | async-start | bytes 393216 | tf_op jit(solution)/shard_map/all_to_all | solution.py:254
  45.4 5.7 %collective-permute-start.5 = (bf16[256,128]{1,0:T(8,128)(2,1)S(1)}, bf16[256,128]{1,0:T(8,128)(2,1)S(1)}, u32[]{:S(2)}, u32[]{:S(2)}) collective-permute-start(bf16[256,128]{1,0:T(8,128)(2,1)S(1)} %add_convert_fusion.here), channel_id=1, source_target_pairs={{0,64},{16,80},{32,96},{48,112},{64,0},{80,16},{96,32},{112,48},{1... | collective-permute-start | bytes 196616 | tf_op jit(solution)/shard_map/ppermute | solution.py:258
  55.7 1.3 %collective-permute-start.6 = (f32[2,16,128]{2,1,0:T(8,128)S(1)}, f32[2,16,128]{2,1,0:T(8,128)S(1)}, u32[]{:S(2)}, u32[]{:S(2)}) collective-permute-start(f32[2,16,128]{2,1,0:T(8,128)S(1)} %get-tuple-element.44), channel_id=1, source_target_pairs={{0,16},{16,0},{32,48},{48,32},{64,80},{80,64},{96,112},{112,96},{1... | collective-permute-start | bytes 49160 | tf_op jit(solution)/shard_map/ppermute | solution.py:258

commit v12 on v11

--- a/solution.py
+++ b/solution.py
@@ -189,7 +189,7 @@
     load.wait()
 
 
-def mix_kernel(index, arrived, here, there, spectra, f, i, w_hbm, keep, send, w_tail, gated_all, sums, sem):
+def mix_kernel(index, arrived, here, one, two, three, spectra, f, i, w_hbm, keep, send, w_tail, gated_all, sums, sem):
     start = w_hbm.shape[1] - w_tail.shape[1]
     load = pltpu.make_async_copy(w_hbm.at[:, pl.ds(start, w_tail.shape[1])], w_tail, sem)
     load.start()
@@ -198,7 +198,7 @@
     fresh = count * rows
     values = arrived[:, :rows].reshape(fresh, lanes)
     gate_one = arrived[:, rows : 2 * rows].reshape(fresh, lanes).astype(F32)
-    past_one = here[...].astype(F32) + there[...].astype(F32)
+    past_one = here[...].astype(F32) + one[...].astype(F32) + two[...].astype(F32) + three[...].astype(F32)
     first = near_to_time(i[0], times_conjugate(spectra[0], dot(f[0], values)))
     gated = (gate_one * (past_one + first)).astype(BF16)
     gated_all[...] = gated
@@ -336,10 +336,8 @@
 
     here = added(here, there)
     payload, here = lax.optimization_barrier((payload, here))
-    there = swapped(here, "ctx", 8)
+    others = [swapped(here, "ctx", step) for step in (8, 12, 4)]
     arrived = exchanged(payload, "ctx")
-    here = added(here, there)
-    there = swapped(here, "ctx", 4)
     side = jax.ShapeDtypeStruct((width, w_out.shape[1] // 2), BF16)
     spectra, w_head = call(
         near_kernel,
@@ -354,7 +352,7 @@
     keep, send, w_tail = call(
         mix_kernel,
         (block, block, side),
-        [SMEM] + [VMEM] * 6 + [HBM],
+        [SMEM] + [VMEM] * 8 + [HBM],
         unit * 4,
         4 << 20,
         scratch=[
@@ -362,7 +360,7 @@
             pltpu.VMEM((2, 2, rows, lanes), F32),
             pltpu.SemaphoreType.DMA,
         ],
-    )(index, arrived, here, there, spectra, f, i, in_hbm(w_out))
+    )(index, arrived, here, *others, spectra, f, i, in_hbm(w_out))
     came = swapped(send, "ctx", 1)
     partial, gated = call(
         finish_kernel,

time: 70.3 us -> 70.7 us (level); the launches traced: 69.9 us -> 69.4 us
  waiting for transfers between devices: 12.2 us -> 9.67 us
  starting transfers between devices: 31.1 us -> 33.4 us
    all_to_all x2, waiting for transfers between devices: 4.46 us -> 1.7 us  [exchanged(): return lax.all_to_all(array, axis, split_axis=0, concat_axis=0, tiled=True)]
    all_to_all x2, starting transfers between devices: 17.1 us -> 18.7 us  [exchanged(): return lax.all_to_all(array, axis, split_axis=0, concat_axis=0, tiled=True)]
    ppermute x6 -> x7, starting transfers between devices: 8.94 us -> 9.62 us  [swapped(): lax.ppermute(array, axis, [(i, i ^ step) for i in range(lax.axis_size(axi...]
    ppermute x6 -> x7, waiting for transfers between devices: 4.1 us -> 4.32 us  [swapped(): lax.ppermute(array, axis, [(i, i ^ step) for i in range(lax.axis_size(axi...]
  transfers between devices with their start and end apart: 9 -> 10, of which waited for: 5 -> 7; matrix products, arithmetic and copies ran while one was open for 0% -> 0% of each run, Pallas kernels for 11% -> 11%
where the time goes in v12:
time: 70.7 us; the launch traced here: 69.4 us
  starting transfers between devices  33.4 us (47%)
  Pallas kernels  12.6 us (18%)
  blocking collectives  11.2 us (16%)
  waiting for transfers between devices  9.67 us (14%)
  local copies, waits for them, and re-layouts  1.73 us (2%)
  between operations  0.75 us (1%)
    all_to_all x2, starting transfers between devices, exchanged(): return lax.all_to_all(array, axis, split_axis=0, concat_axis=0, tiled=True)  18.7 us
    all_to_all x1, blocking collectives, exchanged(): return lax.all_to_all(array, axis, split_axis=0, concat_axis=0, tiled=True)  11.2 us
    ppermute x7, starting transfers between devices, swapped(): lax.ppermute(array, axis, [(i, i ^ step) for i in range(lax.axis_size(axi...  9.62 us
    ppermute x1, starting transfers between devices, layer(): lax.ppermute(filt_far, 'ctx', [(i, i - 1) for i in range(1, ctx_count)])  5.11 us
    ppermute x7, waiting for transfers between devices, swapped(): lax.ppermute(array, axis, [(i, i ^ step) for i in range(lax.axis_size(axi...  4.32 us
    ppermute x1, waiting for transfers between devices, layer(): lax.ppermute(filt_far, 'ctx', [(i, i - 1) for i in range(1, ctx_count)])  3.64 us
    pallas_call x1, Pallas kernels, layer(): call(project_kernel, (jax.ShapeDtypeStruct((ctx_count, 3 * rows, lanes),...  3.14 us
    pallas_call x1, Pallas kernels, layer(): call(first_past_kernel, (half, half, jax.ShapeDtypeStruct((3, fresh, widt...  1.88 us
  transfers between devices with their start and end apart: 10, of which 7 were waited for; matrix products, arithmetic and copies ran while one was open for 0% of the time, Pallas kernels for 11%

profile of v12, /device:TPU:1, one launch (start us, length us, event | category | flops | bytes accessed | tf_op | source)
XLA Modules:
  0.0 69.4 jit_solution(7085438793487633610)
XLA Ops:
  0.6 5.1 %collective-permute-start = (bf16[256,2,256]{2,1,0:T(2,128)(2,1)}, bf16[256,2,256]{2,1,0:T(2,128)(2,1)S(1)}, u32[]{:S(2)}, u32[]{:S(2)}) collective-permute-start(bf16[256,2,256]{2,1,0:T(2,128)(2,1)} %refs_1_.1), channel_id=1, source_target_pairs={{16,0},{32,16},{48,32},{64,48},{80,64},{96,80},{112,96},{128,112},... | collective-permute-start | bytes 786440 | tf_op jit(solution)/shard_map/ppermute | solution.py:277
  5.7 1.7 %shard_map.104 = (bf16[16,16,256]{2,1,0:T(8,128)(2,1)}, bf16[256,2,256]{2,1,0:T(2,128)(2,1)S(1)}, bf16[256,2,256]{2,1,0:T(2,128)(2,1)S(1)}, bf16[256,2,256]{2,1,...) custom-call(bf16[16,256]{1,0:T(8,128)(2,1)} %refs_0_.1, ...), custom_call_target="tpu_custom_call" | custom-call | flops 1024 | bytes 2097152 | tf_op jit(solution)/shard_map/pallas_call | solution.py:279
  7.4 3.6 %collective-permute-done.border = bf16[256,2,256]{2,1,0:T(2,128)(2,1)S(1)} collective-permute-done((bf16[256,2,256]{2,1,0:T(2,128)(2,1)}, bf16[256,2,256]{2,1,0:T(2,128)(2,1)S(1)}, u32[]{:S(2)}, u32[]{:S(2)}) %collective-permute-start) | collective-permute-done | bytes 262176 | tf_op jit(solution)/shard_map/ppermute | solution.py:277
  11.1 1.9 %shard_map.105 = (f32[256,128]{1,0:T(8,128)S(1)}, f32[256,128]{1,0:T(8,128)S(1)}, bf16[3,256,256]{2,1,0:T(8,128)(2,1)S(1)}, bf16[2304,256]{1,0:T(8,128)(2,1)S(1)}) custom-call(s32[1]{0:T(128)} %bitcast.index, s32[1]{0:T(128)S(6)} %convert_element_type.15.last, bf16[256,2,256]{2,1,0:T(2,128)(2,1)S(1)} %collective-permute-done.border, ...), custom_call_target="tpu_custom_call" | custom-call | flops 603979776 | bytes 2097152 | tf_op jit(solution)/shard_map/pallas_call | solution.py:297
  13.0 0.0 copy-start
  13.0 0.7 %copy-done = bf16[3,256,256]{2,1,0:T(8,128)(2,1)} copy-done((bf16[3,256,256]{2,1,0:T(8,128)(2,1)}, bf16[3,256,256]{2,1,0:T(8,128)(2,1)S(1)}, u32[]{:S(2)}) %copy-start) | copy-done | bytes 393240
  13.7 0.0 collective-permute-start.2
  13.7 9.1 %all-to-all-start = ((bf16[16,16,256]{2,1,0:T(8,128)(2,1)}), bf16[16,16,256]{2,1,0:T(8,128)(2,1)S(1)}, u32[]{:S(2)}, u32[]{:S(2)}) async-start(bf16[16,16,256]{2,1,0:T(8,128)(2,1)} %get-tuple-element.26), calls=%async_computation | async-start | bytes 262144 | tf_op jit(solution)/shard_map/all_to_all | solution.py:254
  22.8 0.0 copy-start.1
  22.8 1.0 %copy-done.1 = bf16[3,256,256]{2,1,0:T(8,128)(2,1)S(1)} copy-done((bf16[3,256,256]{2,1,0:T(8,128)(2,1)S(1)}, bf16[3,256,256]{2,1,0:T(8,128)(2,1)}, u32[]{:S(2)}) %copy-start.1) | copy-done | bytes 393240
  23.8 1.3 %shard_map.106 = (f32[256,128]{1,0:T(8,128)S(1)}, f32[256,128]{1,0:T(8,128)S(1)}) custom-call(s32[1]{0:T(128)} %bitcast.index, bf16[3,256,256]{2,1,0:T(8,128)(2,1)S(1)} %copy-done.1, bf16[2,512,256]{2,1,0:T(8,128)(2,1)S(1)} %get-tuple-element.31.f, bf16[2,256,512]{2,1,0:T(8,128)(2,1)S(1)} %get-tuple-element.32.i), custom_call_target="tpu_custom_call" | custom-call | flops 603979776 | bytes 1048576 | tf_op jit(solution)/shard_map/pallas_call | solution.py:306
  25.1 0.9 %collective-permute-start.1 = (f32[256,128]{1,0:T(8,128)S(1)}, f32[256,128]{1,0:T(8,128)S(1)}, u32[]{:S(2)}, u32[]{:S(2)}) collective-permute-start(f32[256,128]{1,0:T(8,128)S(1)} %get-tuple-element.36), channel_id=1, source_target_pairs={{0,16},{16,0},{32,48},{48,32},{64,80},{80,64},{96,112},{112,96},{1... | collective-permute-start | bytes 393224 | tf_op jit(solution)/shard_map/ppermute | solution.py:258
  26.0 0.0 collective-permute-done.2
  26.0 3.6 %collective-permute-start.3 = (bf16[256,128]{1,0:T(8,128)(2,1)S(1)}, bf16[256,128]{1,0:T(8,128)(2,1)S(1)}, u32[]{:S(2)}, u32[]{:S(2)}) collective-permute-start(bf16[256,128]{1,0:T(8,128)(2,1)S(1)} %add_convert_fusion.1), channel_id=1, source_target_pairs={{0,32},{16,48},{32,0},{48,16},{64,96},{80,112},{96,64},{112,80},{1... | collective-permute-start | bytes 196616 | tf_op jit(solution)/shard_map/ppermute | solution.py:258
  29.7 1.6 %all-to-all-done.gathered = bf16[16,16,256]{2,1,0:T(8,128)(2,1)S(1)} async-done(((bf16[16,16,256]{2,1,0:T(8,128)(2,1)}), bf16[16,16,256]{2,1,0:T(8,128)(2,1)S(1)}, u32[]{:S(2)}, u32[]{:S(2)}) %all-to-all-start) | async-done | bytes 131104 | tf_op jit(solution)/shard_map/all_to_all | solution.py:254
  31.3 0.0 collective-permute-done.1.came
  31.3 3.1 %shard_map.107 = (bf16[16,48,128]{2,1,0:T(8,128)(2,1)}, bf16[16,256]{1,0:T(8,128)(2,1)S(1)}) custom-call(bf16[16,16,256]{2,1,0:T(8,128)(2,1)S(1)} %all-to-all-done.gathered, f32[32,128]{1,0:T(8,128)S(1)} %get-tuple-element.27.gain, bf16[2304,256]{1,0:T(8,128)(2,1)S(1)} %get-tuple-element.33.w_head, bf16[3,4096,256]{2,1,0:T(8,128)(2,1)} %bitcast.4, ...), custom_call_target="tpu_custom_call" | custom-call | flops 100663296 | bytes 6291456 | tf_op jit(solution)/shard_map/pallas_call | solution.py:318
  34.4 0.0 collective-permute-done.3
  34.5 9.7 %all-to-all-start.1 = ((bf16[16,48,128]{2,1,0:T(8,128)(2,1)}), bf16[16,48,128]{2,1,0:T(8,128)(2,1)S(1)}, u32[]{:S(2)}, u32[]{:S(2)}) async-start(bf16[16,48,128]{2,1,0:T(8,128)(2,1)} %get-tuple-element.40), calls=%async_computation.1 | async-start | bytes 393216 | tf_op jit(solution)/shard_map/all_to_all | solution.py:254
  44.1 1.4 %collective-permute-start.6 = (bf16[256,128]{1,0:T(8,128)(2,1)S(1)}, bf16[256,128]{1,0:T(8,128)(2,1)S(1)}, u32[]{:S(2)}, u32[]{:S(2)}) collective-permute-start(bf16[256,128]{1,0:T(8,128)(2,1)S(1)} %add_convert_fusion.here), channel_id=1, source_target_pairs={{0,64},{16,80},{32,96},{48,112},{64,0},{80,16},{96,32},{112,48},{1... | collective-permute-start | bytes 196616 | tf_op jit(solution)/shard_map/ppermute | solution.py:258
  45.5 1.8 %collective-permute-start.5 = (bf16[256,128]{1,0:T(8,128)(2,1)S(1)}, bf16[256,128]{1,0:T(8,128)(2,1)S(1)}, u32[]{:S(2)}, u32[]{:S(2)}) collective-permute-start(bf16[256,128]{1,0:T(8,128)(2,1)S(1)} %add_convert_fusion.here), channel_id=1, source_target_pairs={{0,192},{16,208},{32,224},{48,240},{64,128},{80,144},{96,160},{112... | collective-permute-start | bytes 196616 | tf_op jit(solution)/shard_map/ppermute | solution.py:258
  47.3 0.6 collective-permute-start.4
  47.9 1.3 %shard_map.108 = (f32[2,512,128]{2,1,0:T(8,128)S(1)}, bf16[256,2048]{1,0:T(8,128)(2,1)S(1)}) custom-call(s32[1]{0:T(128)} %bitcast.index, bf16[256,2,256]{2,1,0:T(2,128)(2,1)S(1)} %get-tuple-element.29.near, bf16[2,512,256]{2,1,0:T(8,128)(2,1)S(1)} %get-tuple-element.31.f, bf16[256,4096]{1,0:T(8,128)(2,1)} %w_hbm.3), custom_call_target="tpu_custom_call" | custom-call | flops 134217728 | bytes 2097152 | tf_op jit(solution)/shard_map/pallas_call | solution.py:342
  49.1 0.7 %collective-permute-done.6.three = bf16[256,128]{1,0:T(8,128)(2,1)S(1)} collective-permute-done((bf16[256,128]{1,0:T(8,128)(2,1)S(1)}, bf16[256,128]{1,0:T(8,128)(2,1)S(1)}, u32[]{:S(2)}, u32[]{:S(2)}) %collective-permute-start.6) | collective-permute-done | bytes 65568 | tf_op jit(solution)/shard_map/ppermute | solution.py:258
  49.9 1.3 %collective-permute-done.5.two = bf16[256,128]{1,0:T(8,128)(2,1)S(1)} collective-permute-done((bf16[256,128]{1,0:T(8,128)(2,1)S(1)}, bf16[256,128]{1,0:T(8,128)(2,1)S(1)}, u32[]{:S(2)}, u32[]{:S(2)}) %collective-permute-start.5) | collective-permute-done | bytes 65568 | tf_op jit(solution)/shard_map/ppermute | solution.py:258
  51.2 1.5 %collective-permute-done.4.one = bf16[256,128]{1,0:T(8,128)(2,1)S(1)} collective-permute-done((bf16[256,128]{1,0:T(8,128)(2,1)S(1)}, bf16[256,128]{1,0:T(8,128)(2,1)S(1)}, u32[]{:S(2)}, u32[]{:S(2)}) %collective-permute-start.4) | collective-permute-done | bytes 65568 | tf_op jit(solution)/shard_map/ppermute | solution.py:258
  52.6 0.1 all-to-all-done.1.arrived
  52.7 1.8 %shard_map.109 = (f32[2,16,128]{2,1,0:T(8,128)S(1)}, f32[2,16,128]{2,1,0:T(8,128)S(1)}, bf16[256,2048]{1,0:T(8,128)(2,1)S(1)}) custom-call(s32[1]{0:T(128)} %bitcast.index, bf16[16,48,128]{2,1,0:T(8,128)(2,1)S(1)} %all-to-all-done.1.arrived, bf16[256,128]{1,0:T(8,128)(2,1)S(1)} %add_convert_fusion.here, bf16[256,128]{1,0:T(8,128)(2,1)S(1)} %collective-permute-done.4.one, ...), custom_call_target="tpu_custom_call" | custom-call | flops 268435456 | bytes 4194304 | tf_op jit(solution)/shard_map/pallas_call | solution.py:352
  54.5 1.4 %collective-permute-start.7 = (f32[2,16,128]{2,1,0:T(8,128)S(1)}, f32[2,16,128]{2,1,0:T(8,128)S(1)}, u32[]{:S(2)}, u32[]{:S(2)}) collective-permute-start(f32[2,16,128]{2,1,0:T(8,128)S(1)} %get-tuple-element.44), channel_id=1, source_target_pairs={{0,16},{16,0},{32,48},{48,32},{64,80},{80,64},{96,112},{112,96},{1... | collective-permute-start | bytes 49160 | tf_op jit(solution)/shard_map/ppermute | solution.py:258
  55.9 0.8 %collective-permute-done.7.came = f32[2,16,128]{2,1,0:T(8,128)S(1)} collective-permute-done((f32[2,16,128]{2,1,0:T(8,128)S(1)}, f32[2,16,128]{2,1,0:T(8,128)S(1)}, u32[]{:S(2)}, u32[]{:S(2)}) %collective-permute-start.7) | collective-permute-done | bytes 16416 | tf_op jit(solution)/shard_map/ppermute | solution.py:258
  56.7 0.9 %shard_map.110 = (bf16[16,16,256]{2,1,0:T(8,128)(2,1)S(1)}, bf16[16,256]{1,0:T(8,128)(2,1)}) custom-call(s32[1]{0:T(128)} %bitcast.index, f32[2,16,128]{2,1,0:T(8,128)S(1)} %get-tuple-element.43.keep, f32[2,16,128]{2,1,0:T(8,128)S(1)} %collective-permute-done.7.came, bf16[16,256]{1,0:T(8,128)(2,1)S(1)} %get-tuple-element.45.gate_two, ...), custom_call_target="tpu_custom_call" | custom-call | flops 67108864 | bytes 1048576 | tf_op jit(solution)/shard_map/pallas_call | solution.py:365
  57.6 11.2 %all_to_all.15.arrived = bf16[16,16,256]{2,1,0:T(8,128)(2,1)S(1)} all-to-all(bf16[16,16,256]{2,1,0:T(8,128)(2,1)S(1)} %get-tuple-element.48), channel_id=1, replica_groups=mesh['ctx'=16,'chan'=16] {'chan'}, dimensions={0} | all-to-all | bytes 262144 | tf_op jit(solution)/shard_map/all_to_all | solution.py:254
  68.8 0.6 shard_map.111
  (2 shorter events, 0.0 us)
Async XLA Ops:
  0.6 10.5 %collective-permute-start = (bf16[256,2,256]{2,1,0:T(2,128)(2,1)}, bf16[256,2,256]{2,1,0:T(2,128)(2,1)S(1)}, u32[]{:S(2)}, u32[]{:S(2)}) collective-permute-start(bf16[256,2,256]{2,1,0:T(2,128)(2,1)} %refs_1_.1), channel_id=1, source_target_pairs={{16,0},{32,16},{48,32},{64,48},{80,64},{96,80},{112,96},{128,112},... | collective-permute-start | bytes 786440 | tf_op jit(solution)/shard_map/ppermute | solution.py:277
  13.0 0.8 %copy-start = (bf16[3,256,256]{2,1,0:T(8,128)(2,1)}, bf16[3,256,256]{2,1,0:T(8,128)(2,1)S(1)}, u32[]{:S(2)}) copy-start(bf16[3,256,256]{2,1,0:T(8,128)(2,1)S(1)} %get-tuple-element.34.rows) | copy-start | bytes 1179652
  13.7 12.3 %collective-permute-start.2 = (f32[256,128]{1,0:T(8,128)S(1)}, f32[256,128]{1,0:T(8,128)S(1)}, u32[]{:S(2)}, u32[]{:S(2)}) collective-permute-start(f32[256,128]{1,0:T(8,128)S(1)} %get-tuple-element.39), channel_id=1, source_target_pairs={{0,16},{16,0},{32,48},{48,32},{64,80},{80,64},{96,112},{112,96},{1... | collective-permute-start | bytes 393224 | tf_op jit(solution)/shard_map/ppermute | solution.py:258
  13.7 17.5 %all-to-all-start = ((bf16[16,16,256]{2,1,0:T(8,128)(2,1)}), bf16[16,16,256]{2,1,0:T(8,128)(2,1)S(1)}, u32[]{:S(2)}, u32[]{:S(2)}) async-start(bf16[16,16,256]{2,1,0:T(8,128)(2,1)} %get-tuple-element.26), calls=%async_computation | async-start | bytes 262144 | tf_op jit(solution)/shard_map/all_to_all | solution.py:254
  22.8 1.0 %copy-start.1 = (bf16[3,256,256]{2,1,0:T(8,128)(2,1)S(1)}, bf16[3,256,256]{2,1,0:T(8,128)(2,1)}, u32[]{:S(2)}) copy-start(bf16[3,256,256]{2,1,0:T(8,128)(2,1)} %copy-done) | copy-start | bytes 1179652
  25.1 6.1 %collective-permute-start.1 = (f32[256,128]{1,0:T(8,128)S(1)}, f32[256,128]{1,0:T(8,128)S(1)}, u32[]{:S(2)}, u32[]{:S(2)}) collective-permute-start(f32[256,128]{1,0:T(8,128)S(1)} %get-tuple-element.36), channel_id=1, source_target_pairs={{0,16},{16,0},{32,48},{48,32},{64,80},{80,64},{96,112},{112,96},{1... | collective-permute-start | bytes 393224 | tf_op jit(solution)/shard_map/ppermute | solution.py:258
  26.0 8.4 %collective-permute-start.3 = (bf16[256,128]{1,0:T(8,128)(2,1)S(1)}, bf16[256,128]{1,0:T(8,128)(2,1)S(1)}, u32[]{:S(2)}, u32[]{:S(2)}) collective-permute-start(bf16[256,128]{1,0:T(8,128)(2,1)S(1)} %add_convert_fusion.1), channel_id=1, source_target_pairs={{0,32},{16,48},{32,0},{48,16},{64,96},{80,112},{96,64},{112,80},{1... | collective-permute-start | bytes 196616 | tf_op jit(solution)/shard_map/ppermute | solution.py:258
  34.5 18.2 %all-to-all-start.1 = ((bf16[16,48,128]{2,1,0:T(8,128)(2,1)}), bf16[16,48,128]{2,1,0:T(8,128)(2,1)S(1)}, u32[]{:S(2)}, u32[]{:S(2)}) async-start(bf16[16,48,128]{2,1,0:T(8,128)(2,1)} %get-tuple-element.40), calls=%async_computation.1 | async-start | bytes 393216 | tf_op jit(solution)/shard_map/all_to_all | solution.py:254
  44.1 5.7 %collective-permute-start.6 = (bf16[256,128]{1,0:T(8,128)(2,1)S(1)}, bf16[256,128]{1,0:T(8,128)(2,1)S(1)}, u32[]{:S(2)}, u32[]{:S(2)}) collective-permute-start(bf16[256,128]{1,0:T(8,128)(2,1)S(1)} %add_convert_fusion.here), channel_id=1, source_target_pairs={{0,64},{16,80},{32,96},{48,112},{64,0},{80,16},{96,32},{112,48},{1... | collective-permute-start | bytes 196616 | tf_op jit(solution)/shard_map/ppermute | solution.py:258
  45.5 5.7 %collective-permute-start.5 = (bf16[256,128]{1,0:T(8,128)(2,1)S(1)}, bf16[256,128]{1,0:T(8,128)(2,1)S(1)}, u32[]{:S(2)}, u32[]{:S(2)}) collective-permute-start(bf16[256,128]{1,0:T(8,128)(2,1)S(1)} %add_convert_fusion.here), channel_id=1, source_target_pairs={{0,192},{16,208},{32,224},{48,240},{64,128},{80,144},{96,160},{112... | collective-permute-start | bytes 196616 | tf_op jit(solution)/shard_map/ppermute | solution.py:258
  47.3 5.3 %collective-permute-start.4 = (bf16[256,128]{1,0:T(8,128)(2,1)S(1)}, bf16[256,128]{1,0:T(8,128)(2,1)S(1)}, u32[]{:S(2)}, u32[]{:S(2)}) collective-permute-start(bf16[256,128]{1,0:T(8,128)(2,1)S(1)} %add_convert_fusion.here), channel_id=1, source_target_pairs={{0,128},{16,144},{32,160},{48,176},{64,192},{80,208},{96,224},{112... | collective-permute-start | bytes 196616 | tf_op jit(solution)/shard_map/ppermute | solution.py:258
  54.5 2.2 %collective-permute-start.7 = (f32[2,16,128]{2,1,0:T(8,128)S(1)}, f32[2,16,128]{2,1,0:T(8,128)S(1)}, u32[]{:S(2)}, u32[]{:S(2)}) collective-permute-start(f32[2,16,128]{2,1,0:T(8,128)S(1)} %get-tuple-element.44), channel_id=1, source_target_pairs={{0,16},{16,0},{32,48},{48,32},{64,80},{80,64},{96,112},{112,96},{1... | collective-permute-start | bytes 49160 | tf_op jit(solution)/shard_map/ppermute | solution.py:258

commit v13 on v11

--- a/solution.py
+++ b/solution.py
@@ -35,13 +35,26 @@
 
 
 def spectrum(forward, rows):
-    return dot(forward[0], rows) + dot(forward[1], rows)
-
-
-def back_to_time(high, low, product):
+    half = forward.shape[1] // 2
+    return [dot(forward[0, r], rows) + dot(forward[1, r], rows) for r in (slice(half), slice(half, None))]
+
+
+def back_to_time(inverse, product):
     upper = product.astype(BF16)
     lower = (product - upper.astype(F32)).astype(BF16)
-    return dot(high, upper) + dot(high, lower) + dot(low, upper)
+    half = inverse.shape[1] // 2
+    return jnp.concatenate(
+        [
+            dot(inverse[0, r], upper) + dot(inverse[0, r], lower) + dot(inverse[1, r], upper)
+            for r in (slice(half), slice(half, None))
+        ],
+        0,
+    )
+
+
+def halves(rows):
+    half = rows.shape[0] // 2
+    return rows[:half], rows[half:]
 
 
 def near_to_time(high, product):
@@ -53,9 +66,7 @@
 
 
 def times_conjugate(window, signal):
-    half = window.shape[0] // 2
-    wc, ws = window[:half], window[half:]
-    sc, ss = signal[:half], signal[half:]
+    (wc, ws), (sc, ss) = window, signal
     return jnp.concatenate([wc * sc + ws * ss, wc * ss - ws * sc], 0)
 
 
@@ -74,12 +85,14 @@
 
 
 def past_part(own, after, history, f, i):
-    half = f.shape[1] // 2
-    quarter = half // 2
-    first, second = spectrum(f, own), spectrum(f, after)
-    bc, bs = second[:half], second[half:]
-    window = first + jnp.concatenate([-bs[:quarter], bs[quarter:], bc[:quarter], -bc[quarter:]], 0)
-    return back_to_time(i[0], i[1], times_conjugate(window, spectrum(f, history)))
+    quarter = f.shape[1] // 4
+    first_cos, first_sin = spectrum(f, own)
+    bc, bs = spectrum(f, after)
+    window = (
+        first_cos + jnp.concatenate([-bs[:quarter], bs[quarter:]], 0),
+        first_sin + jnp.concatenate([bc[:quarter], -bc[quarter:]], 0),
+    )
+    return back_to_time(i, times_conjugate(window, spectrum(f, history)))
 
 
 def open_kernel(*refs):
@@ -185,7 +198,8 @@
     half = pl.ds(pl.multiple_of((index[0] % 2) * lanes, lanes), lanes)
     spread_out(near.at[:, :, half], spread)
     for which in range(2):
-        spectra[which] = spectrum(f, parted(spread, 2, which))
+        half = spectra.shape[1] // 2
+        spectra[which, :half], spectra[which, half:] = spectrum(f, parted(spread, 2, which))
     load.wait()
 
 
@@ -199,12 +213,12 @@
     values = arrived[:, :rows].reshape(fresh, lanes)
     gate_one = arrived[:, rows : 2 * rows].reshape(fresh, lanes).astype(F32)
     past_one = here[...].astype(F32) + there[...].astype(F32)
-    first = near_to_time(i[0], times_conjugate(spectra[0], dot(f[0], values)))
+    first = near_to_time(i[0], times_conjugate(halves(spectra[0]), halves(dot(f[0], values))))
     gated = (gate_one * (past_one + first)).astype(BF16)
     gated_all[...] = gated
     mine = index[0] % 2
     chip = pl.ds(pl.multiple_of((index[0] - mine) * rows, 2 * rows), 2 * rows)
-    second = near_to_time(i[0, chip, :], times_conjugate(spectra[1], dot(f[0], gated)))
+    second = near_to_time(i[0, chip, :], times_conjugate(halves(spectra[1]), halves(dot(f[0], gated))))
     past_two = [arrived[p, 2 * rows :].astype(F32) for p in range(2)]
     for s in range(2, count):
         past_two[s % 2] += arrived[s, 2 * rows :].astype(F32)

time: 70.3 us -> 70 us (level)
  Pallas kernels: 12.6 us -> 11.8 us
  transfers between devices with their start and end apart: 9 -> 9, of which waited for: 5 -> 5; matrix products, arithmetic and copies ran while one was open for 0% -> 0% of each run, Pallas kernels for 11% -> 10%
where the time goes in v13:
time: 70 us; the launch traced here: 69.6 us
  starting transfers between devices  31.1 us (44%)
  waiting for transfers between devices  12.6 us (18%)
  Pallas kernels  11.8 us (17%)
  blocking collectives  11.5 us (16%)
  local copies, waits for them, and re-layouts  1.73 us (2%)
  between operations  0.76 us (1%)
    all_to_all x2, starting transfers between devices, exchanged(): return lax.all_to_all(array, axis, split_axis=0, concat_axis=0, tiled=True)  17.1 us
    all_to_all x1, blocking collectives, exchanged(): return lax.all_to_all(array, axis, split_axis=0, concat_axis=0, tiled=True)  11.5 us
    ppermute x6, starting transfers between devices, swapped(): lax.ppermute(array, axis, [(i, i ^ step) for i in range(lax.axis_size(axi...  8.94 us
    ppermute x1, starting transfers between devices, layer(): lax.ppermute(filt_far, 'ctx', [(i, i - 1) for i in range(1, ctx_count)])  5.11 us
    all_to_all x2, waiting for transfers between devices, exchanged(): return lax.all_to_all(array, axis, split_axis=0, concat_axis=0, tiled=True)  4.81 us
    ppermute x6, waiting for transfers between devices, swapped(): lax.ppermute(array, axis, [(i, i ^ step) for i in range(lax.axis_size(axi...  4.11 us
    ppermute x1, waiting for transfers between devices, layer(): lax.ppermute(filt_far, 'ctx', [(i, i - 1) for i in range(1, ctx_count)])  3.64 us
    pallas_call x1, Pallas kernels, layer(): call(project_kernel, (jax.ShapeDtypeStruct((ctx_count, 3 * rows, lanes),...  3.14 us
  transfers between devices with their start and end apart: 9, of which 5 were waited for; matrix products, arithmetic and copies ran while one was open for 0% of the time, Pallas kernels for 10%

profile of v13, /device:TPU:1, one launch (start us, length us, event | category | flops | bytes accessed | tf_op | source)
XLA Modules:
  0.0 69.6 jit_solution(1756118451956769030)
XLA Ops:
  0.6 5.1 %collective-permute-start = (bf16[256,2,256]{2,1,0:T(2,128)(2,1)}, bf16[256,2,256]{2,1,0:T(2,128)(2,1)S(1)}, u32[]{:S(2)}, u32[]{:S(2)}) collective-permute-start(bf16[256,2,256]{2,1,0:T(2,128)(2,1)} %refs_1_.1), channel_id=1, source_target_pairs={{16,0},{32,16},{48,32},{64,48},{80,64},{96,80},{112,96},{128,112},... | collective-permute-start | bytes 786440 | tf_op jit(solution)/shard_map/ppermute | solution.py:291
  5.7 1.7 %shard_map.104 = (bf16[16,16,256]{2,1,0:T(8,128)(2,1)}, bf16[256,2,256]{2,1,0:T(2,128)(2,1)S(1)}, bf16[256,2,256]{2,1,0:T(2,128)(2,1)S(1)}, bf16[256,2,256]{2,1,...) custom-call(bf16[16,256]{1,0:T(8,128)(2,1)} %refs_0_.1, ...), custom_call_target="tpu_custom_call" | custom-call | flops 1024 | bytes 2097152 | tf_op jit(solution)/shard_map/pallas_call | solution.py:293
  7.4 3.6 %collective-permute-done.border = bf16[256,2,256]{2,1,0:T(2,128)(2,1)S(1)} collective-permute-done((bf16[256,2,256]{2,1,0:T(2,128)(2,1)}, bf16[256,2,256]{2,1,0:T(2,128)(2,1)S(1)}, u32[]{:S(2)}, u32[]{:S(2)}) %collective-permute-start) | collective-permute-done | bytes 262176 | tf_op jit(solution)/shard_map/ppermute | solution.py:291
  11.1 1.5 %shard_map.105 = (f32[256,128]{1,0:T(8,128)S(1)}, f32[256,128]{1,0:T(8,128)S(1)}, bf16[3,256,256]{2,1,0:T(8,128)(2,1)S(1)}, bf16[2304,256]{1,0:T(8,128)(2,1)S(1)}) custom-call(s32[1]{0:T(128)} %bitcast.index, s32[1]{0:T(128)S(6)} %convert_element_type.24.last, bf16[256,2,256]{2,1,0:T(2,128)(2,1)S(1)} %collective-permute-done.border, ...), custom_call_target="tpu_custom_call" | custom-call | flops 603979776 | bytes 2097152 | tf_op jit(solution)/shard_map/pallas_call | solution.py:311
  12.6 0.0 copy-start
  12.6 0.7 %copy-done = bf16[3,256,256]{2,1,0:T(8,128)(2,1)} copy-done((bf16[3,256,256]{2,1,0:T(8,128)(2,1)}, bf16[3,256,256]{2,1,0:T(8,128)(2,1)S(1)}, u32[]{:S(2)}) %copy-start) | copy-done | bytes 393240
  13.4 0.0 collective-permute-start.2
  13.4 9.1 %all-to-all-start = ((bf16[16,16,256]{2,1,0:T(8,128)(2,1)}), bf16[16,16,256]{2,1,0:T(8,128)(2,1)S(1)}, u32[]{:S(2)}, u32[]{:S(2)}) async-start(bf16[16,16,256]{2,1,0:T(8,128)(2,1)} %get-tuple-element.26), calls=%async_computation | async-start | bytes 262144 | tf_op jit(solution)/shard_map/all_to_all | solution.py:268
  22.4 0.0 copy-start.1
  22.4 1.0 %copy-done.1 = bf16[3,256,256]{2,1,0:T(8,128)(2,1)S(1)} copy-done((bf16[3,256,256]{2,1,0:T(8,128)(2,1)S(1)}, bf16[3,256,256]{2,1,0:T(8,128)(2,1)}, u32[]{:S(2)}) %copy-start.1) | copy-done | bytes 393240
  23.4 1.0 %shard_map.106 = (f32[256,128]{1,0:T(8,128)S(1)}, f32[256,128]{1,0:T(8,128)S(1)}) custom-call(s32[1]{0:T(128)} %bitcast.index, bf16[3,256,256]{2,1,0:T(8,128)(2,1)S(1)} %copy-done.1, bf16[2,512,256]{2,1,0:T(8,128)(2,1)S(1)} %get-tuple-element.31.f, bf16[2,256,512]{2,1,0:T(8,128)(2,1)S(1)} %get-tuple-element.32.i), custom_call_target="tpu_custom_call" | custom-call | flops 603979776 | bytes 1048576 | tf_op jit(solution)/shard_map/pallas_call | solution.py:320
  24.4 0.9 %collective-permute-start.1 = (f32[256,128]{1,0:T(8,128)S(1)}, f32[256,128]{1,0:T(8,128)S(1)}, u32[]{:S(2)}, u32[]{:S(2)}) collective-permute-start(f32[256,128]{1,0:T(8,128)S(1)} %get-tuple-element.36), channel_id=1, source_target_pairs={{0,16},{16,0},{32,48},{48,32},{64,80},{80,64},{96,112},{112,96},{1... | collective-permute-start | bytes 393224 | tf_op jit(solution)/shard_map/ppermute | solution.py:272
  25.3 0.0 collective-permute-done.2
  25.3 3.6 %collective-permute-start.3 = (bf16[256,128]{1,0:T(8,128)(2,1)S(1)}, bf16[256,128]{1,0:T(8,128)(2,1)S(1)}, u32[]{:S(2)}, u32[]{:S(2)}) collective-permute-start(bf16[256,128]{1,0:T(8,128)(2,1)S(1)} %add_convert_fusion.2), channel_id=1, source_target_pairs={{0,32},{16,48},{32,0},{48,16},{64,96},{80,112},{96,64},{112,80},{1... | collective-permute-start | bytes 196616 | tf_op jit(solution)/shard_map/ppermute | solution.py:272
  28.9 2.0 %all-to-all-done.gathered = bf16[16,16,256]{2,1,0:T(8,128)(2,1)S(1)} async-done(((bf16[16,16,256]{2,1,0:T(8,128)(2,1)}), bf16[16,16,256]{2,1,0:T(8,128)(2,1)S(1)}, u32[]{:S(2)}, u32[]{:S(2)}) %all-to-all-start) | async-done | bytes 131104 | tf_op jit(solution)/shard_map/all_to_all | solution.py:268
  30.9 0.0 collective-permute-done.1.came
  30.9 3.1 %shard_map.107 = (bf16[16,48,128]{2,1,0:T(8,128)(2,1)}, bf16[16,256]{1,0:T(8,128)(2,1)S(1)}) custom-call(bf16[16,16,256]{2,1,0:T(8,128)(2,1)S(1)} %all-to-all-done.gathered, f32[32,128]{1,0:T(8,128)S(1)} %get-tuple-element.27.gain, bf16[2304,256]{1,0:T(8,128)(2,1)S(1)} %get-tuple-element.33.w_head, bf16[3,4096,256]{2,1,0:T(8,128)(2,1)} %bitcast.4, ...), custom_call_target="tpu_custom_call" | custom-call | flops 100663296 | bytes 6291456 | tf_op jit(solution)/shard_map/pallas_call | solution.py:332
  34.1 0.0 collective-permute-done.3
  34.1 2.8 %collective-permute-start.4 = (bf16[256,128]{1,0:T(8,128)(2,1)S(1)}, bf16[256,128]{1,0:T(8,128)(2,1)S(1)}, u32[]{:S(2)}, u32[]{:S(2)}) collective-permute-start(bf16[256,128]{1,0:T(8,128)(2,1)S(1)} %add_convert_fusion.1), channel_id=1, source_target_pairs={{0,128},{16,144},{32,160},{48,176},{64,192},{80,208},{96,224},{112... | collective-permute-start | bytes 196616 | tf_op jit(solution)/shard_map/ppermute | solution.py:272
  36.9 8.0 %all-to-all-start.1 = ((bf16[16,48,128]{2,1,0:T(8,128)(2,1)}), bf16[16,48,128]{2,1,0:T(8,128)(2,1)S(1)}, u32[]{:S(2)}, u32[]{:S(2)}) async-start(bf16[16,48,128]{2,1,0:T(8,128)(2,1)} %get-tuple-element.40), calls=%async_computation.1 | async-start | bytes 393216 | tf_op jit(solution)/shard_map/all_to_all | solution.py:268
  45.0 0.0 collective-permute-done.4
  45.0 1.4 %collective-permute-start.5 = (bf16[256,128]{1,0:T(8,128)(2,1)S(1)}, bf16[256,128]{1,0:T(8,128)(2,1)S(1)}, u32[]{:S(2)}, u32[]{:S(2)}) collective-permute-start(bf16[256,128]{1,0:T(8,128)(2,1)S(1)} %add_convert_fusion.here), channel_id=1, source_target_pairs={{0,64},{16,80},{32,96},{48,112},{64,0},{80,16},{96,32},{112,48},{1... | collective-permute-start | bytes 196616 | tf_op jit(solution)/shard_map/ppermute | solution.py:272
  46.4 1.2 %shard_map.108 = (f32[2,512,128]{2,1,0:T(8,128)S(1)}, bf16[256,2048]{1,0:T(8,128)(2,1)S(1)}) custom-call(s32[1]{0:T(128)} %bitcast.index, bf16[256,2,256]{2,1,0:T(2,128)(2,1)S(1)} %get-tuple-element.29.near, bf16[2,512,256]{2,1,0:T(8,128)(2,1)S(1)} %get-tuple-element.31.f, bf16[256,4096]{1,0:T(8,128)(2,1)} %w_hbm.3), custom_call_target="tpu_custom_call" | custom-call | flops 134217728 | bytes 2097152 | tf_op jit(solution)/shard_map/pallas_call | solution.py:358
  47.7 3.0 %collective-permute-done.5.there = bf16[256,128]{1,0:T(8,128)(2,1)S(1)} collective-permute-done((bf16[256,128]{1,0:T(8,128)(2,1)S(1)}, bf16[256,128]{1,0:T(8,128)(2,1)S(1)}, u32[]{:S(2)}, u32[]{:S(2)}) %collective-permute-start.5) | collective-permute-done | bytes 65568 | tf_op jit(solution)/shard_map/ppermute | solution.py:272
  50.7 2.8 %all-to-all-done.1.arrived = bf16[16,48,128]{2,1,0:T(8,128)(2,1)S(1)} async-done(((bf16[16,48,128]{2,1,0:T(8,128)(2,1)}), bf16[16,48,128]{2,1,0:T(8,128)(2,1)S(1)}, u32[]{:S(2)}, u32[]{:S(2)}) %all-to-all-start.1) | async-done | bytes 196640 | tf_op jit(solution)/shard_map/all_to_all | solution.py:268
  53.5 1.8 %shard_map.109 = (f32[2,16,128]{2,1,0:T(8,128)S(1)}, f32[2,16,128]{2,1,0:T(8,128)S(1)}, bf16[256,2048]{1,0:T(8,128)(2,1)S(1)}) custom-call(s32[1]{0:T(128)} %bitcast.index, bf16[16,48,128]{2,1,0:T(8,128)(2,1)S(1)} %all-to-all-done.1.arrived, bf16[256,128]{1,0:T(8,128)(2,1)S(1)} %add_convert_fusion.here, bf16[256,128]{1,0:T(8,128)(2,1)S(1)} %collective-permute-done.5.there, ...), custom_call_target="tpu_custom_call" | custom-call | flops 268435456 | bytes 4194304 | tf_op jit(solution)/shard_map/pallas_call | solution.py:368
  55.3 0.2 collective-permute-start.6
  55.5 1.1 %collective-permute-done.6.came = f32[2,16,128]{2,1,0:T(8,128)S(1)} collective-permute-done((f32[2,16,128]{2,1,0:T(8,128)S(1)}, f32[2,16,128]{2,1,0:T(8,128)S(1)}, u32[]{:S(2)}, u32[]{:S(2)}) %collective-permute-start.6) | collective-permute-done | bytes 16416 | tf_op jit(solution)/shard_map/ppermute | solution.py:272
  56.6 0.9 %shard_map.110 = (bf16[16,16,256]{2,1,0:T(8,128)(2,1)S(1)}, bf16[16,256]{1,0:T(8,128)(2,1)}) custom-call(s32[1]{0:T(128)} %bitcast.index, f32[2,16,128]{2,1,0:T(8,128)S(1)} %get-tuple-element.43.keep, f32[2,16,128]{2,1,0:T(8,128)S(1)} %collective-permute-done.6.came, bf16[16,256]{1,0:T(8,128)(2,1)S(1)} %get-tuple-element.45.gate_two, ...), custom_call_target="tpu_custom_call" | custom-call | flops 67108864 | bytes 1048576 | tf_op jit(solution)/shard_map/pallas_call | solution.py:381
  57.5 11.5 %all_to_all.15.arrived = bf16[16,16,256]{2,1,0:T(8,128)(2,1)S(1)} all-to-all(bf16[16,16,256]{2,1,0:T(8,128)(2,1)S(1)} %get-tuple-element.48), channel_id=1, replica_groups=mesh['ctx'=16,'chan'=16] {'chan'}, dimensions={0} | all-to-all | bytes 262144 | tf_op jit(solution)/shard_map/all_to_all | solution.py:268
  68.9 0.6 shard_map.111
  (3 shorter events, 0.1 us)
Async XLA Ops:
  0.6 10.5 %collective-permute-start = (bf16[256,2,256]{2,1,0:T(2,128)(2,1)}, bf16[256,2,256]{2,1,0:T(2,128)(2,1)S(1)}, u32[]{:S(2)}, u32[]{:S(2)}) collective-permute-start(bf16[256,2,256]{2,1,0:T(2,128)(2,1)} %refs_1_.1), channel_id=1, source_target_pairs={{16,0},{32,16},{48,32},{64,48},{80,64},{96,80},{112,96},{128,112},... | collective-permute-start | bytes 786440 | tf_op jit(solution)/shard_map/ppermute | solution.py:291
  12.6 0.7 %copy-start = (bf16[3,256,256]{2,1,0:T(8,128)(2,1)}, bf16[3,256,256]{2,1,0:T(8,128)(2,1)S(1)}, u32[]{:S(2)}) copy-start(bf16[3,256,256]{2,1,0:T(8,128)(2,1)S(1)} %get-tuple-element.34.rows) | copy-start | bytes 1179652
  13.4 11.9 %collective-permute-start.2 = (f32[256,128]{1,0:T(8,128)S(1)}, f32[256,128]{1,0:T(8,128)S(1)}, u32[]{:S(2)}, u32[]{:S(2)}) collective-permute-start(f32[256,128]{1,0:T(8,128)S(1)} %get-tuple-element.39), channel_id=1, source_target_pairs={{0,16},{16,0},{32,48},{48,32},{64,80},{80,64},{96,112},{112,96},{1... | collective-permute-start | bytes 393224 | tf_op jit(solution)/shard_map/ppermute | solution.py:272
  13.4 17.5 %all-to-all-start = ((bf16[16,16,256]{2,1,0:T(8,128)(2,1)}), bf16[16,16,256]{2,1,0:T(8,128)(2,1)S(1)}, u32[]{:S(2)}, u32[]{:S(2)}) async-start(bf16[16,16,256]{2,1,0:T(8,128)(2,1)} %get-tuple-element.26), calls=%async_computation | async-start | bytes 262144 | tf_op jit(solution)/shard_map/all_to_all | solution.py:268
  22.4 1.0 %copy-start.1 = (bf16[3,256,256]{2,1,0:T(8,128)(2,1)S(1)}, bf16[3,256,256]{2,1,0:T(8,128)(2,1)}, u32[]{:S(2)}) copy-start(bf16[3,256,256]{2,1,0:T(8,128)(2,1)} %copy-done) | copy-start | bytes 1179652
  24.4 6.5 %collective-permute-start.1 = (f32[256,128]{1,0:T(8,128)S(1)}, f32[256,128]{1,0:T(8,128)S(1)}, u32[]{:S(2)}, u32[]{:S(2)}) collective-permute-start(f32[256,128]{1,0:T(8,128)S(1)} %get-tuple-element.36), channel_id=1, source_target_pairs={{0,16},{16,0},{32,48},{48,32},{64,80},{80,64},{96,112},{112,96},{1... | collective-permute-start | bytes 393224 | tf_op jit(solution)/shard_map/ppermute | solution.py:272
  25.3 8.7 %collective-permute-start.3 = (bf16[256,128]{1,0:T(8,128)(2,1)S(1)}, bf16[256,128]{1,0:T(8,128)(2,1)S(1)}, u32[]{:S(2)}, u32[]{:S(2)}) collective-permute-start(bf16[256,128]{1,0:T(8,128)(2,1)S(1)} %add_convert_fusion.2), channel_id=1, source_target_pairs={{0,32},{16,48},{32,0},{48,16},{64,96},{80,112},{96,64},{112,80},{1... | collective-permute-start | bytes 196616 | tf_op jit(solution)/shard_map/ppermute | solution.py:272
  34.1 10.9 %collective-permute-start.4 = (bf16[256,128]{1,0:T(8,128)(2,1)S(1)}, bf16[256,128]{1,0:T(8,128)(2,1)S(1)}, u32[]{:S(2)}, u32[]{:S(2)}) collective-permute-start(bf16[256,128]{1,0:T(8,128)(2,1)S(1)} %add_convert_fusion.1), channel_id=1, source_target_pairs={{0,128},{16,144},{32,160},{48,176},{64,192},{80,208},{96,224},{112... | collective-permute-start | bytes 196616 | tf_op jit(solution)/shard_map/ppermute | solution.py:272
  36.9 16.6 %all-to-all-start.1 = ((bf16[16,48,128]{2,1,0:T(8,128)(2,1)}), bf16[16,48,128]{2,1,0:T(8,128)(2,1)S(1)}, u32[]{:S(2)}, u32[]{:S(2)}) async-start(bf16[16,48,128]{2,1,0:T(8,128)(2,1)} %get-tuple-element.40), calls=%async_computation.1 | async-start | bytes 393216 | tf_op jit(solution)/shard_map/all_to_all | solution.py:268
  45.0 5.7 %collective-permute-start.5 = (bf16[256,128]{1,0:T(8,128)(2,1)S(1)}, bf16[256,128]{1,0:T(8,128)(2,1)S(1)}, u32[]{:S(2)}, u32[]{:S(2)}) collective-permute-start(bf16[256,128]{1,0:T(8,128)(2,1)S(1)} %add_convert_fusion.here), channel_id=1, source_target_pairs={{0,64},{16,80},{32,96},{48,112},{64,0},{80,16},{96,32},{112,48},{1... | collective-permute-start | bytes 196616 | tf_op jit(solution)/shard_map/ppermute | solution.py:272
  55.3 1.3 %collective-permute-start.6 = (f32[2,16,128]{2,1,0:T(8,128)S(1)}, f32[2,16,128]{2,1,0:T(8,128)S(1)}, u32[]{:S(2)}, u32[]{:S(2)}) collective-permute-start(f32[2,16,128]{2,1,0:T(8,128)S(1)} %get-tuple-element.44), channel_id=1, source_target_pairs={{0,16},{16,0},{32,48},{48,32},{64,80},{80,64},{96,112},{112,96},{1... | collective-permute-start | bytes 49160 | tf_op jit(solution)/shard_map/ppermute | solution.py:272
